TPU v7x, 32 devices: a whole 2x2x4 slice. The times are simulated.
32 devices in a mesh: dp: 2 (over y), expert: 16 (over z, x, core).
Axes of the slice: x: 2, y: 2, z: 4, core: 2. Of those that a mesh axis runs over, the one named last changes fastest.
Arguments:
- tokens: bfloat16 [2, 2, 1024, 2048], P(None, 'dp', 'expert'), may hold values from -6 to 6
- grad_out: bfloat16 [2, 2, 1024, 2048], P(None, 'dp', 'expert'), may hold values from -6 to 6
- segments: int32 [2, 2, 1024], P(None, 'dp'), may hold values from 0 to 3, never falling along the last dimension, each value on 1 to 512 neighbouring positions
- routes: int32 [2, 2, 1024, 6], P(None, 'dp', 'expert'), may hold values from 0 to 15, all different within a row; in each aligned block of 64 rows (0 to 63, 64 to 127, ..., all dimensions but the last counted through in order) at most 32 rows name the same one
- gates: float32 [2, 2, 1024, 6], P(None, 'dp', 'expert'), may hold values from 0.05 to 0.45
- attn_gain: bfloat16 [2048], P('dp'), may hold values from 0.5 to 1.5
- w_query: bfloat16 [2048, 3072], P('dp'), may hold values from -0.125 to 0.125
- w_kv_down: bfloat16 [2048, 576], P('dp'), may hold values from -0.125 to 0.125
- kv_gain: bfloat16 [512], P('dp'), may hold values from 0.5 to 1.5
- w_kv_up: bfloat16 [512, 4096], P('dp'), may hold values from -0.25 to 0.25
- w_out: bfloat16 [2048, 2048], P('dp'), may hold values from -0.375 to 0.375
- ffn_gain: bfloat16 [2048], P('dp'), may hold values from 0.5 to 1.5
- w_shared_in: bfloat16 [2048, 5632], P('dp'), may hold values from -0.125 to 0.125
- w_shared_out: bfloat16 [2816, 2048], P('dp'), may hold values from -0.109375 to 0.109375
- w_expert_in: bfloat16 [16, 2048, 2816], P('expert', 'dp'), may hold values from -0.125 to 0.125
- w_expert_out: bfloat16 [16, 1408, 2048], P('expert', 'dp'), may hold values from -0.15625 to 0.15625
Outputs:
- mixed: bfloat16 [2, 2, 1024, 2048], P(None, 'dp', 'expert')
- input_grad: float32 [2, 2, 1024, 2048], P(None, 'dp', 'expert')
- attn_gain_grad: float32 [2048], P('dp')
- w_query_grad: float32 [2048, 3072], P('dp')
- w_kv_down_grad: float32 [2048, 576], P('dp')
- kv_gain_grad: float32 [512], P('dp')
- w_kv_up_grad: float32 [512, 4096], P('dp')
- w_out_grad: float32 [2048, 2048], P('dp')
- ffn_gain_grad: float32 [2048], P('dp')
- w_shared_in_grad: float32 [2048, 5632], P('dp')
- w_shared_out_grad: float32 [2816, 2048], P('dp')
- w_expert_in_grad: float32 [16, 2048, 2816], P('expert', 'dp')
- w_expert_out_grad: float32 [16, 1408, 2048], P('expert', 'dp')
Inputs may be any that keep to these rules, and one draw needn't show every extreme that they name: `routes`: within the tokens of one device in one micro-batch (aligned blocks of 64 rows in the order micro-batch, sequence, position) no expert is named more than 32 times, a bound that some block reaches. A token names 6 different experts. `segments`: document numbers never fall along a sequence; a document may cross the positions of several devices.
All inputs are finite; a program needn't handle non-finite values.
Results may differ from a plain program's by a relative error of at most 0.018.
Values may be sent and summed in bfloat16 or wider, within the bound.
No kernel may reach another device: no remote copies, remote signals or barrier semaphores. Data moves between devices by JAX's collectives and lax.ppermute only.
A program may use at most 576 MiB of HBM per device.

v0:
```python
import functools

import jax
import jax.numpy as jnp
from jax import lax
from jax.experimental import pallas as pl
from jax.experimental.layout import Layout, with_layout_constraint
from jax.experimental.pallas import tpu as pltpu
from jax.sharding import PartitionSpec as P

HEADS = 16
NOPE = 128
ROPE = 64
VDIM = 128
LATENT = 512
DOC_MAX = 512


theta_base = 50000.0
eps_norm = 1e-06
bf16 = jnp.bfloat16
f32 = jnp.float32


def rope_tables(length, width):
    half = width // 2
    freq = theta_base ** (-2.0 * jnp.arange(half, dtype=f32) / width)
    angle = jnp.arange(length, dtype=f32)[:, None] * freq[None, :]
    cosine = jnp.concatenate([jnp.cos(angle), jnp.cos(angle)], -1)
    sine = jnp.concatenate([jnp.sin(angle), jnp.sin(angle)], -1)
    return (cosine, sine)


def rotate_back(value, cosine, sine):
    half = value.shape[-1] // 2
    scaled = value * sine
    turned = jnp.concatenate([scaled[..., half:], -scaled[..., :half]], -1)
    return value * cosine + turned


def normed(value, gain):
    return (
        value
        * lax.rsqrt(jnp.mean(value * value, -1, keepdims=True) + eps_norm)
        * gain.astype(f32)
    )


def normed_back(value, gain, grad):
    inv = lax.rsqrt(jnp.mean(value * value, -1, keepdims=True) + eps_norm)
    hat = value * inv
    scaled = grad * gain.astype(f32)
    inner = jnp.mean(scaled * hat, -1, keepdims=True)
    return inv * (scaled - hat * inner), jnp.sum(grad * hat, 0)


def swiglu_parts(packed):
    half = packed.shape[-1] // 2
    return packed[..., :half], packed[..., half:]


def swiglu(packed):
    gate, up = swiglu_parts(packed)
    return gate * jax.nn.sigmoid(gate) * up


def swiglu_back(packed, grad):
    gate, up = swiglu_parts(packed)
    sig = jax.nn.sigmoid(gate)
    d_gate = grad * up * sig * (1.0 + gate * (1.0 - sig))
    d_up = grad * gate * sig
    return jnp.concatenate([d_gate, d_up], -1)


def dot(left, right):
    return jnp.dot(left, right, preferred_element_type=f32)


def dot_tn(left, right):
    return lax.dot_general(left, right, (((0,), (0,)), ((), ())), preferred_element_type=f32)


def dot_nt(left, right):
    return lax.dot_general(left, right, (((1,), (1,)), ((), ())), preferred_element_type=f32)


def row_major(x):
    return with_layout_constraint(x, Layout(major_to_minor=tuple(range(x.ndim))))


def after(value, *first):
    return lax.optimization_barrier((value,) + first)[0]


def block_of_keys(refs, start, stop, low):
    qn_ref, rope_ref, kv_ref, seg_col, seg_row = refs
    rows = qn_ref.shape[2]

    def take(ref, first, last):
        return ref[first // rows : last // rows, 0].reshape(last - first, ref.shape[3])

    query = jnp.concatenate([take(qn_ref, start, stop), take(rope_ref, start, stop)[:, :ROPE]], 1)
    kv = take(kv_ref, low, stop)
    key = jnp.concatenate([kv[:, :NOPE], take(rope_ref, low, stop)[:, ROPE:]], 1)
    value = kv[:, NOPE:]
    score = dot_nt(query, key) * ((NOPE + ROPE) ** (-0.5))
    size = (stop - start, stop - low)
    q_at = lax.broadcasted_iota(jnp.int32, size, 0) + (start - low)
    k_at = lax.broadcasted_iota(jnp.int32, size, 1)
    allowed = (seg_col[0, start:stop] == seg_row[0, :, low:stop]) & (k_at <= q_at)
    return query, key, value, jnp.where(allowed, score, -1e30)


def query_blocks(seq, rows, size=256):
    for start in range(0, seq, size):
        low = max(0, start - DOC_MAX + 1) // rows * rows
        yield start, start + size, low


def attend_kernel(qn_ref, rope_ref, kv_ref, seg_col, seg_row, out_ref, lse_ref):
    owners, _, rows, _ = qn_ref.shape
    refs = (qn_ref, rope_ref, kv_ref, seg_col, seg_row)
    for start, stop, low in query_blocks(owners * rows, rows):
        _, _, value, score = block_of_keys(refs, start, stop, low)
        top = jnp.max(score, -1, keepdims=True)
        expo = jnp.exp(score - top)
        total = jnp.sum(expo, -1, keepdims=True)
        out = dot((expo / total).astype(bf16), value).astype(bf16)
        at = slice(start // rows, stop // rows)
        out_ref[at, 0] = out.reshape((stop - start) // rows, rows, VDIM)
        lse_ref[0, start:stop] = top + jnp.log(total)


def attend_back_kernel(
    qn_ref, rope_ref, kv_ref, seg_col, seg_row, lse_ref, dout_ref, cos_ref, sin_ref, back_ref, acc
):
    owners, _, rows, _ = qn_ref.shape
    seq = owners * rows
    refs = (qn_ref, rope_ref, kv_ref, seg_col, seg_row)
    acc[...] = jnp.zeros_like(acc)
    for start, stop, low in query_blocks(seq, rows):
        at = slice(start // rows, stop // rows)
        query, key, value, score = block_of_keys(refs, start, stop, low)
        prob = jnp.exp(score - lse_ref[0, start:stop])
        dout = dout_ref[at, 0].reshape(stop - start, VDIM)
        dprob = dot_nt(dout, value)
        delta = jnp.sum(prob * dprob, -1, keepdims=True)
        dscore = (prob * (dprob - delta) * ((NOPE + ROPE) ** (-0.5))).astype(bf16)
        dquery = dot(dscore, key)
        acc[low:stop, : NOPE + ROPE] += dot_tn(dscore, query)
        acc[low:stop, 256:] += dot_tn(prob.astype(bf16), dout)
        rope = rotate_back(dquery[:, NOPE:], cos_ref[start:stop], sin_ref[start:stop])
        whole = jnp.concatenate([dquery[:, :NOPE], rope, rope, dquery, rope], 1)
        back_ref[at, 0] = whole.astype(bf16).reshape((stop - start) // rows, rows, 512)
    dkey = acc[...]
    tail = jnp.concatenate([dkey[:, NOPE : NOPE + ROPE], dkey[:, :NOPE], dkey[:, 256:]], 1)
    back_ref[:, 0, :, NOPE + ROPE :] = tail.astype(bf16).reshape(owners, rows, 320)


def attend(q_nope, roped, kvup, segs):
    owners, micro, rows, _ = q_nope.shape
    seq = owners * rows
    spec = lambda c: pl.BlockSpec((owners, 1, rows, c), lambda m: (0, m, 0, 0))
    return pl.pallas_call(
        attend_kernel,
        out_shape=(
            jax.ShapeDtypeStruct((owners, micro, rows, VDIM), bf16),
            jax.ShapeDtypeStruct((micro, seq, 1), f32),
        ),
        grid=(micro,),
        in_specs=[
            spec(NOPE),
            spec(2 * ROPE),
            spec(2 * NOPE),
            pl.BlockSpec((1, seq, 1), lambda m: (m, 0, 0)),
            pl.BlockSpec((1, 1, seq), lambda m: (m, 0, 0)),
        ],
        out_specs=(spec(VDIM), pl.BlockSpec((1, seq, 1), lambda m: (m, 0, 0))),
        cost_estimate=pl.CostEstimate(
            flops=2 * micro * seq * 640 * 320,
            transcendentals=micro * seq * 640,
            bytes_accessed=micro * seq * 1400,
        ),
    )(q_nope, roped, kvup, segs[:, :, None], segs[:, None, :])


def attend_back(q_nope, roped, kvup, segs, lse, dout, cosine, sine):
    owners, micro, rows, _ = q_nope.shape
    seq = owners * rows
    spec = lambda c: pl.BlockSpec((owners, 1, rows, c), lambda m: (0, m, 0, 0))
    flat = pl.BlockSpec((seq, ROPE), lambda m: (0, 0))
    return pl.pallas_call(
        attend_back_kernel,
        out_shape=jax.ShapeDtypeStruct((owners, micro, rows, 512), bf16),
        grid=(micro,),
        in_specs=[
            spec(NOPE),
            spec(2 * ROPE),
            spec(2 * NOPE),
            pl.BlockSpec((1, seq, 1), lambda m: (m, 0, 0)),
            pl.BlockSpec((1, 1, seq), lambda m: (m, 0, 0)),
            pl.BlockSpec((1, seq, 1), lambda m: (m, 0, 0)),
            spec(VDIM),
            flat,
            flat,
        ],
        out_specs=spec(512),
        scratch_shapes=[pltpu.VMEM((seq, 384), f32)],
        cost_estimate=pl.CostEstimate(
            flops=2 * micro * seq * 640 * 832,
            transcendentals=micro * seq * 640,
            bytes_accessed=micro * seq * 2600,
        ),
    )(q_nope, roped, kvup, segs[:, :, None], segs[:, None, :], lse, dout, cosine, sine)


def put_back_kernel(place_ref, rows_ref, units_ref, weight_ref, out_ref):
    left = jnp.concatenate([place_ref[0], units_ref[...]], 1)
    right = jnp.concatenate([rows_ref[...], weight_ref[...]], 0)
    out_ref[...] = dot(left, right).astype(bf16)


def put_back(place, rows, units, weight):
    many, size, height = place.shape
    total, count = units.shape
    width = rows.shape[1]
    return pl.pallas_call(
        put_back_kernel,
        out_shape=jax.ShapeDtypeStruct((total, width), bf16),
        grid=(many,),
        in_specs=[
            pl.BlockSpec((1, size, height), lambda i: (i, 0, 0)),
            pl.BlockSpec((height, width), lambda i: (i, 0)),
            pl.BlockSpec((size, count), lambda i: (i, 0)),
            pl.BlockSpec(weight.shape, lambda i: (0, 0)),
        ],
        out_specs=pl.BlockSpec((size, width), lambda i: (i, 0)),
        cost_estimate=pl.CostEstimate(
            flops=2 * total * width * (height + count),
            transcendentals=0,
            bytes_accessed=2 * (total * width + rows.size + units.size + weight.size),
        ),
    )(place, rows, units, weight)


def shared_in_kernel(x_ref, out_ref, *, runs, piece):
    groups = x_ref.shape[0]
    turned = [x_ref[e].astype(f32).T for e in range(groups)]
    length = groups * piece
    parts = []
    for c in range(runs):
        parts += [t[:, c * piece : (c + 1) * piece] for t in turned]
        if length % 128 == 0:
            out_ref[:, c * length : (c + 1) * length] = jnp.concatenate(parts, 1)
            parts = []
    if parts:
        out_ref[...] = jnp.concatenate(parts, 1)


def shared_out_kernel(x_ref, out_ref, *, piece):
    rows = x_ref[0].astype(f32)
    count = rows.shape[0] // piece
    out_ref[0] = jnp.concatenate([rows[c * piece : (c + 1) * piece] for c in range(count)], 1)


def shared_rows(stacked, runs, piece):
    groups, count, size = stacked.shape
    first = runs * piece
    rest = count - first
    step = 128
    in_grad = pl.pallas_call(
        functools.partial(shared_in_kernel, runs=runs, piece=piece),
        out_shape=jax.ShapeDtypeStruct((size, groups * first), f32),
        grid=(size // step,),
        in_specs=[pl.BlockSpec((groups, first, step), lambda i: (0, 0, i))],
        out_specs=pl.BlockSpec((step, groups * first), lambda i: (i, 0)),
        cost_estimate=pl.CostEstimate(
            flops=0, transcendentals=0, bytes_accessed=6 * groups * first * size
        ),
    )(stacked)
    out_grad = pl.pallas_call(
        functools.partial(shared_out_kernel, piece=piece),
        out_shape=jax.ShapeDtypeStruct((groups, piece, rest // piece * size), f32),
        grid=(groups,),
        in_specs=[pl.BlockSpec((1, rest, size), lambda e: (e, first // rest, 0))],
        out_specs=pl.BlockSpec((1, piece, rest // piece * size), lambda e: (e, 0, 0)),
        cost_estimate=pl.CostEstimate(
            flops=0, transcendentals=0, bytes_accessed=6 * groups * rest * size
        ),
    )(stacked)
    return in_grad, out_grad.reshape(groups * piece, -1)


def attn_rows_kernel(x_ref, extra_ref, out_ref, query_ref, kvup_ref, down_ref, *, a, b, height):
    groups, _, count = x_ref.shape
    rest = count - a - b
    runs = x_ref.shape[1] // kvup_ref.shape[0]
    step = kvup_ref.shape[0]
    for e in range(0, groups, 2):
        one, two = x_ref[e].astype(f32), x_ref[e + 1].astype(f32)
        out_ref[:, e * a : (e + 2) * a] = jnp.concatenate([one[:, :a], two[:, :a]], 1)
        query_ref[:, e * b : (e + 2) * b] = jnp.concatenate(
            [one[:, a : a + b], two[:, a : a + b]], 1
        )
        pieces = [
            x[c * step : (c + 1) * step, a + b :] for x in (one, two) for c in range(runs)
        ]
        kvup_ref[:, e * runs * rest : (e + 2) * runs * rest] = jnp.concatenate(pieces, 1)
    for e in range(extra_ref.shape[0]):
        x = extra_ref[e].astype(f32)
        tail = x[height : height + height // 2]
        half = count // 2
        tail = jnp.concatenate([tail[:, :half], tail[:, half:]], 0)
        down_ref[e * height : (e + 1) * height] = jnp.concatenate([x[:height], tail], 1)


def attn_rows(stacked, rows, a, b, kvup_height, down_height):
    groups, _, count = stacked.shape
    size = 128
    steps = rows // size
    kvup_width = (count - a - b) * rows // kvup_height
    return pl.pallas_call(
        functools.partial(attn_rows_kernel, a=a, b=b, height=down_height),
        out_shape=(
            jax.ShapeDtypeStruct((rows, groups * a), f32),
            jax.ShapeDtypeStruct((rows, groups * b), f32),
            jax.ShapeDtypeStruct((kvup_height, groups * kvup_width), f32),
            jax.ShapeDtypeStruct((groups * down_height, count * 3 // 2), f32),
        ),
        grid=(steps,),
        in_specs=[
            pl.BlockSpec((groups, size, count), lambda i: (0, i, 0)),
            pl.BlockSpec((groups // steps, size, count), lambda i: (i, steps, 0)),
        ],
        out_specs=(
            pl.BlockSpec((size, groups * a), lambda i: (i, 0)),
            pl.BlockSpec((size, groups * b), lambda i: (i, 0)),
            pl.BlockSpec((kvup_height // steps, groups * kvup_width), lambda i: (i, 0)),
            pl.BlockSpec((groups // steps * down_height, count * 3 // 2), lambda i: (i, 0)),
        ),
        cost_estimate=pl.CostEstimate(
            flops=0, transcendentals=0, bytes_accessed=6 * stacked.size
        ),
    )(stacked, stacked)


def per_device(
    tokens,
    grad_out,
    segments,
    routes,
    gates,
    attn_gain,
    w_query,
    w_kv_down,
    kv_gain,
    w_kv_up,
    w_out,
    ffn_gain,
    w_shared_in,
    w_shared_out,
    w_expert_in,
    w_expert_out,
):
    micro, _, rows, width = tokens.shape
    groups = lax.axis_size("expert")
    parts = lax.axis_size("dp")
    me = lax.axis_index("expert")
    part = lax.axis_index("dp")
    own = micro * rows
    total = groups * own
    seq = rows * groups
    top = routes.shape[3]
    capacity = max(2, rows * top * 4 // (3 * groups))
    qk = NOPE + ROPE
    assert HEADS == groups

    def shift(x, step):
        return lax.ppermute(x, "dp", [((i + step) % parts, i) for i in range(parts)])

    def send(x, step):
        return lax.ppermute(x, "dp", [(i, (i + step) % parts) for i in range(parts)])

    def others(x):
        return [shift(x, r) for r in range(1, parts)]

    def turn(x, axis, amount):
        size = x.shape[axis]
        return lax.dynamic_slice_in_dim(
            jnp.concatenate([x, x], axis), amount * (size // parts), size, axis
        )

    def own_first(x, axis):
        return turn(x, axis, part)

    def natural(x, axis):
        return turn(x, axis, (parts - part) % parts)

    def lay_out(x, rest):
        size = x.shape[0]
        whole = jnp.zeros((parts * size,) + x.shape[1:], x.dtype)
        for r, piece in enumerate([x] + rest):
            at = ((part + r) % parts) * size
            whole = lax.dynamic_update_slice_in_dim(whole, piece, at, 0)
        return whole

    def block_of(full, index):
        size = full.shape[0] // parts
        return lax.dynamic_slice_in_dim(full, (index % parts) * size, size, 0)

    def exchanged(own_block, block_for):
        result = own_block.astype(f32)
        for r in range(1, parts):
            result = result + send(block_for(r), r).astype(f32)
        return result

    pairs = [(i, i ^ 1) for i in range(groups)]
    odd = me % 2

    def pieces(x, *first):
        size = x.shape[0]
        found = [(x, part * size)]
        if parts == 2:
            half = size // 2
            asked = lax.dynamic_slice_in_dim(x, odd * half, half, 0)
            if first:
                asked = after(asked, *first)
            got = shift(asked, 1)
            swapped = lax.ppermute(got, "expert", pairs)
            base = (1 - part) * size
            found += [(got, base + odd * half), (swapped, base + (1 - odd) * half)]
        else:
            asked = after(x, *first) if first else x
            found += [(y, ((part + r) % parts) * size) for r, y in enumerate(others(asked), 1)]
        return found

    def dot_pieces(x, blocks):
        return sum(
            dot(lax.dynamic_slice_in_dim(x, at, w.shape[0], 1), w) for w, at in blocks
        )

    def dot_pieces_t(x, blocks):
        whole = jnp.zeros((x.shape[0], sum(w.shape[0] for w, _ in blocks)), f32)
        for w, at in blocks:
            whole = lax.dynamic_update_slice_in_dim(whole, dot_nt(x, w), at, 1)
        return whole

    def spread(x):
        return lax.all_gather(x, "expert", axis=0, tiled=True)

    def stack(x):
        return lax.all_gather(x, "expert", axis=0, tiled=False)

    def swap(x):
        return lax.all_to_all(x, "expert", split_axis=0, concat_axis=0, tiled=True)

    def collect(x):
        return lax.psum_scatter(x, "expert", scatter_dimension=0, tiled=True)

    gain_sizes = (width // parts, LATENT // parts, width // parts)
    cuts = (gain_sizes[0], gain_sizes[0] + gain_sizes[1])
    own_gains = jnp.concatenate([attn_gain, kv_gain, ffn_gain])
    gain_rows = jnp.split(lay_out(own_gains[None], [y[None] for y in others(own_gains)]), cuts, 1)
    gain_attn, gain_kv, gain_ffn = (rows_of.reshape(-1) for rows_of in gain_rows)

    wq_own = lax.dynamic_slice_in_dim(w_query, me * qk, qk, 1)
    wq_me = jnp.concatenate([wq_own] + others(wq_own), 0)
    down_pieces = pieces(w_kv_down)
    w_down = jnp.zeros((width, LATENT + ROPE), bf16)
    for w, start in down_pieces:
        start = (start - part * (width // parts)) % width
        w_down = lax.dynamic_update_slice_in_dim(w_down, w, start, 0)
    wkvup_own = lax.dynamic_slice_in_dim(w_kv_up, me * 2 * NOPE, 2 * NOPE, 1)
    wkvup_me = lay_out(wkvup_own, others(wkvup_own))
    wout = pieces(w_out)

    def turned(w):
        return jnp.concatenate([-w[:, ROPE // 2 :], w[:, : ROPE // 2]], 1)

    rope_q, rope_k = wq_me[:, NOPE:], w_down[:, LATENT:]
    w_first = jnp.concatenate(
        [
            wq_me[:, :NOPE],
            w_down[:, :LATENT],
            rope_q,
            rope_k,
            turned(rope_q),
            turned(rope_k),
        ],
        1,
    )

    x_own = tokens[:, 0].reshape(own, width)
    dy_own = grad_out[:, 0].reshape(own, width)
    act_own = normed(x_own.astype(f32), gain_attn).astype(bf16)
    act = spread(own_first(act_own, 1))
    dy_all = spread(after(dy_own, act))

    expert_ids = jnp.arange(groups, dtype=jnp.int32)
    routes_own = routes[:, 0].reshape(own, top)
    gates_own = gates[:, 0].reshape(own, top)
    table = jnp.sum(
        jnp.where(routes_own[None] == expert_ids[:, None, None], gates_own[None], 0.0), -1
    )
    gate_rows = swap(table).reshape(groups * micro, rows)
    hit = gate_rows > 0.0
    slot = jnp.cumsum(hit.astype(jnp.int32), 1) - 1
    pick = (slot[:, None, :] == jnp.arange(capacity, dtype=jnp.int32)[None, :, None]) & hit[
        :, None, :
    ]
    gate_slots = jnp.sum(jnp.where(pick, gate_rows[:, None, :], 0.0), -1).reshape(-1, 1)
    pick = pick.astype(bf16)
    together = 4
    place = pick.swapaxes(1, 2).reshape(-1, together, rows, 1, capacity)
    place = place * jnp.eye(together, dtype=bf16)[None, :, None, :, None]
    place = place.reshape(-1, together * rows, together * capacity)

    def dispatch(x):
        picked = jnp.einsum(
            "bst,btd->bsd",
            pick,
            x.reshape(groups * micro, rows, width),
            preferred_element_type=f32,
        )
        return picked.reshape(groups * micro * capacity, width)

    ff = w_shared_in.shape[1] // 2
    run = ff // (parts * groups)
    wsi_own = jnp.concatenate(
        [
            lax.dynamic_slice_in_dim(w_shared_in, c * (ff // parts) + me * run, run, 1).T
            for c in range(2 * parts)
        ],
        0,
    )
    wso_own = lax.dynamic_slice_in_dim(w_shared_out, me * run, run, 0)
    wsi_me = jnp.concatenate([wsi_own] + others(wsi_own), 1)
    wso_me = lay_out(wso_own, others(wso_own))
    wei_others = others(w_expert_in[0])
    weo_others = others(w_expert_out[0])
    wq = pieces(w_query, wei_others[0], weo_others[0])
    wkvup = pieces(w_kv_up, wei_others[0], weo_others[0])
    wso = pieces(w_shared_out, wei_others[0], weo_others[0])

    cosine, sine = rope_tables(seq, ROPE)

    def table_of(values):
        both = jnp.concatenate([values, values], 1).reshape(groups, 1, rows, 2 * ROPE)
        return jnp.broadcast_to(both, (groups, micro, rows, 2 * ROPE)).reshape(total, 2 * ROPE)

    first = dot(after(act, gate_rows), w_first)
    q_nope = first[:, :NOPE].astype(bf16)
    latent_raw = first[:, NOPE : NOPE + LATENT]
    latent = normed(latent_raw, gain_kv).astype(bf16)
    at = NOPE + LATENT
    roped = (
        first[:, at : at + 2 * ROPE] * table_of(cosine) + first[:, at + 2 * ROPE :] * table_of(sine)
    ).astype(bf16)
    kvup = dot(latent, wkvup_me).astype(bf16)

    def owners(x):
        return x.reshape(groups, micro, rows, x.shape[-1])

    segs = segments[:, 0]
    head = (owners(q_nope), owners(roped), owners(kvup), segs)
    attn, lse = attend(*head)
    attn_own = swap(attn.reshape(groups, own, VDIM))
    attn_own = attn_own.swapaxes(0, 1).reshape(own, groups * VDIM)
    x1 = x_own.astype(f32) + dot_pieces(attn_own, wout)
    hid_own = normed(x1, gain_ffn).astype(bf16)
    hid_all = spread(own_first(hid_own, 1))
    attn_all = spread(after(attn_own, hid_all))

    size = width // parts
    arrived = dispatch(hid_all).astype(bf16)
    dyexp = (gate_slots * dispatch(dy_all)).astype(bf16)
    wei = jnp.concatenate([w_expert_in[0]] + wei_others, 0)
    weo = lay_out(w_expert_out[0], weo_others)
    epre = dot(arrived, wei)
    eact = swiglu(epre).astype(bf16)
    deact = dot_nt(dyexp, weo)
    depre = swiglu_back(epre, deact).astype(bf16)
    dhid_rows = dot_nt(depre, wei).astype(bf16)

    spre = dot_nt(hid_all, wsi_me)
    sact = swiglu(spre).astype(bf16)
    dsact = dot_nt(dy_all, wso_me)
    dspre = swiglu_back(spre, dsact).astype(bf16)
    dhid_part = put_back(place, dhid_rows, dspre, wsi_me)
    dhid_sum = collect(dhid_part)

    arrived, depre, eact, dyexp, dspre, sact = lax.optimization_barrier(
        (arrived, depre, eact, dyexp, dspre, sact, dhid_part)
    )[:6]
    g_si = dot_tn(dspre, hid_all)
    g_so = dot_tn(sact, dy_all)

    def shared_grads(r):
        rows_of = block_of(g_so, part + r)
        return jnp.concatenate(
            [g_si[:, r * size : (r + 1) * size]] + jnp.split(rows_of, parts, 1), 0
        )

    g_shared = exchanged(shared_grads(0), lambda r: shared_grads(r).astype(bf16))
    g_shared = stack(after(g_shared.astype(bf16), dhid_sum))

    def expert_in_grad(r):
        return dot_tn(arrived[:, r * size : (r + 1) * size], depre)

    def expert_out_grad(r):
        short = eact.shape[1] // parts
        some = lax.dynamic_slice_in_dim(eact, ((part + r) % parts) * short, short, 1)
        return dot_tn(some, dyexp)

    sent_in = [expert_in_grad(r).astype(bf16) for r in range(1, parts)]
    sent_out = [expert_out_grad(r).astype(bf16) for r in range(1, parts)]
    gated = (gate_slots * dot(eact, weo)).astype(bf16)
    dhid_sum = after(dhid_sum, gated, *sent_in, *sent_out)
    got_in = [send(x, r).astype(f32) for r, x in enumerate(sent_in, 1)]
    got_out = [send(x, r).astype(f32) for r, x in enumerate(sent_out, 1)]
    dhid = natural(dhid_sum, 1).astype(f32)

    dy = dy_own.astype(f32)
    dx1_norm, g_ffn_gain = normed_back(x1, gain_ffn, dhid)
    dx1 = dy + dx1_norm
    dx1_low = dx1.astype(bf16)
    dattn_own = dot_pieces_t(dx1_low, wout).astype(bf16)
    dattn = swap(dattn_own.reshape(own, groups, VDIM).swapaxes(0, 1))
    dao = after(dx1_low, dattn).reshape(own, groups, width // groups).swapaxes(0, 1)
    dao = swap(dao)
    dattn = dattn.reshape(groups, micro, rows, VDIM)
    back = attend_back(*head, lse, dattn, cosine, sine)
    moved = swap(back.reshape(groups, own, 512))

    def back_of(x, first_column, last_column):
        piece = x[..., first_column:last_column]
        return piece.swapaxes(0, 1).reshape(own, groups * (last_column - first_column))

    flat = back.reshape(total, 512)
    g_query = dot_tn(act, flat[:, :qk])
    g_kvup = dot_tn(latent, flat[:, 256:])
    g_out = dot_tn(attn_all, dao.reshape(total, width // groups))

    def fold(x):
        steps = size // 128
        runs = size // x.shape[0]
        x = x.reshape(steps, x.shape[0] // steps, runs, x.shape[1] // runs)
        return x.swapaxes(1, 2).reshape(size, -1)

    def attn_grads(r):
        return jnp.concatenate(
            [
                block_of(g_out, part + r),
                g_query[r * size : (r + 1) * size],
                fold(block_of(g_kvup, part + r)),
            ],
            1,
        )

    g_attn = exchanged(attn_grads(0), lambda r: attn_grads(r).astype(bf16))

    gated, sact = lax.optimization_barrier((gated, sact, moved))[:2]
    returned = swap(gated.reshape(groups, micro * capacity, width))
    hidden = swap(after(sact, returned).reshape(groups, own, -1))
    hidden = hidden.reshape(groups, own, parts, run).transpose(1, 2, 0, 3).reshape(own, ff)
    hit_own = routes_own.reshape(micro, rows, 1, top) == expert_ids[:, None]
    hit_own = jnp.any(hit_own, -1)
    slot_own = jnp.cumsum(hit_own.astype(jnp.int32), 1) - 1
    slots = jnp.arange(capacity, dtype=jnp.int32)
    find = ((slot_own[..., None] == slots) & hit_own[..., None]).astype(bf16)
    routed = jnp.einsum(
        "mtk,mkd->mtd",
        find.reshape(micro, rows, groups * capacity),
        returned.reshape(groups, micro, capacity, width)
        .swapaxes(0, 1)
        .reshape(micro, groups * capacity, width),
        preferred_element_type=f32,
    ).reshape(own, width)
    out_sum = routed + dot_pieces(hidden, wso)

    dq_own = back_of(moved, 0, qk)
    dkvup_own = back_of(moved, 256, 512)
    dkrope_own = jnp.sum(moved[..., qk:256].astype(f32), 0)
    dlatent = dot_pieces_t(dkvup_own, wkvup)
    latent_own = lax.dynamic_slice_in_dim(latent_raw, me * own, own, 0)
    cos_own = jnp.tile(lax.dynamic_slice_in_dim(cosine, me * rows, rows, 0), (micro, 1))
    sin_own = jnp.tile(lax.dynamic_slice_in_dim(sine, me * rows, rows, 0), (micro, 1))
    dlatent_raw, g_kv_gain = normed_back(latent_own, gain_kv, dlatent)
    dkvfull = jnp.concatenate([dlatent_raw, rotate_back(dkrope_own, cos_own, sin_own)], -1)
    dkvfull = dkvfull.astype(bf16)
    down = LATENT + ROPE
    early = jnp.concatenate([g_kv_gain, g_ffn_gain])
    short = early.shape[0]
    early = jnp.pad(early, (0, 16 * down - short)).reshape(16, down)
    dkv_all = spread(jnp.concatenate([dkvfull, early.astype(bf16)], 0))
    dkv_all = dkv_all.reshape(groups, own + 16, down)
    early = jnp.sum(dkv_all[:, own:].astype(f32), 0).reshape(-1)[:short]
    dkv_all = dkv_all[:, :own].reshape(total, down)
    dact = dot_pieces_t(dq_own, wq) + natural(dot_nt(dkvfull, w_down), 1)
    dx_norm, g_attn_gain = normed_back(x_own.astype(f32), gain_attn, dact)
    input_grad = dx1 + dx_norm

    height = size // groups
    act_rows = jnp.concatenate(
        [
            lax.dynamic_slice_in_dim(act, c * size + me * height, height, 1)
            for c in range(parts)
        ],
        1,
    )
    g_down = dot_tn(act_rows, dkv_all)
    g_down = exchanged(
        g_down[:height], lambda r: g_down[r * height : (r + 1) * height].astype(bf16)
    ).astype(bf16)
    early_kv, early_ffn = early[:LATENT], early[LATENT:]

    def early_gains(r):
        return jnp.concatenate([block_of(early_kv, part + r), block_of(early_ffn, part + r)])

    early = exchanged(early_gains(0), early_gains)
    late = exchanged(block_of(g_attn_gain, part), lambda r: block_of(g_attn_gain, part + r))
    count = g_attn.shape[1]
    tail = g_down[:, count:]
    tail = jnp.concatenate([tail[: height // 2], tail[height // 2 :]], 1)
    extra = jnp.concatenate([g_down[:, :count], tail], 0)
    at_late = size + extra.shape[0]
    late_rows = -(-size // count)
    late = jnp.pad(late, (0, late_rows * count - size)).reshape(late_rows, count)
    extra = jnp.concatenate([extra, late.astype(bf16)], 0)
    extra = jnp.pad(extra, ((0, 128 - extra.shape[0]), (0, 0)))
    g_attn = jnp.concatenate([g_attn.astype(bf16), extra], 0)
    g_attn = stack(row_major(g_attn))
    late = jnp.sum(g_attn[:, at_late : at_late + late_rows].astype(f32), 0).reshape(-1)[:size]
    gains = (late, early[: LATENT // parts], early[LATENT // parts :])

    mixed = (x1 + out_sum).astype(bf16)
    g_ein = sum(got_in, expert_in_grad(0))
    g_eout = sum(got_out, expert_out_grad(0))
    out_grad, query_grad, kvup_grad, g_down = attn_rows(
        g_attn, size, width // groups, qk, LATENT // parts, height
    )
    shared_in_grad, shared_out_grad = shared_rows(g_shared, 2 * parts, run)
    return (
        mixed.reshape(micro, 1, rows, width),
        input_grad.reshape(micro, 1, rows, width),
        gains[0],
        query_grad,
        g_down,
        gains[1],
        kvup_grad,
        out_grad,
        gains[2],
        shared_in_grad,
        shared_out_grad,
        g_ein[None],
        g_eout[None],
    )


def solution(mesh):
    tok = P(None, "dp", "expert", None)
    row = P("dp", None)
    exp = P("expert", "dp", None)
    in_specs = (
        tok, tok, P(None, "dp", None), tok, tok,
        P("dp"), row, row, P("dp"), row, row, P("dp"), row, row, exp, exp,
    )
    out_specs = (
        tok, tok, P("dp"), row, row, P("dp"), row, row, P("dp"), row, row, exp, exp,
    )

    return jax.shard_map(
        per_device, mesh=mesh, in_specs=in_specs, out_specs=out_specs, check_vma=False
    )
```

profile of v0, /device:TPU:1, one launch (start us, length us, event | category | flops | bytes accessed | tf_op | source)
XLA Modules:
  0.0 1356.3 jit_solution(7590011888771099310)
XLA Ops:
  17.0 77.0 %all-gather.10.cloned.1.call-done = bf16[2048,2048]{1,0:T(8,128)(2,1)} async-done(((bf16[128,2048]{1,0:T(8,128)(2,1)}), bf16[2048,2048]{1,0:T(8,128)(2,1)}) %all-gather.10.cloned.1.call-update) | async-done | bytes 8388624 | tf_op jit(solution)/shard_map/all_gather | solution.py:449
  94.8 3.5 all-to-all-start
  103.8 3.2 constant_dynamic-slice_fusion.13
  109.3 13.8 %collective-permute-done.2 = bf16[512,576]{0,1:T(8,128)(2,1)} collective-permute-done((bf16[512,576]{0,1:T(8,128)(2,1)S(1)}, bf16[512,576]{0,1:T(8,128)(2,1)}, u32[]{:S(2)}, u32[]{:S(2)}) %collective-permute-start.2) | collective-permute-done | bytes 589856 | tf_op jit(solution)/shard_map/ppermute | solution.py:379
  135.4 7.2 dynamic_update_slice.63
  142.6 7.6 dynamic_update_slice.64
  155.9 15.0 %collective-permute-done.5 = bf16[512,2048]{1,0:T(8,128)(2,1)} collective-permute-done((bf16[512,2048]{1,0:T(8,128)(2,1)}, bf16[512,2048]{1,0:T(8,128)(2,1)}, u32[]{:S(2)}, u32[]{:S(2)}) %collective-permute-start.5) | collective-permute-done | bytes 2097184 | tf_op jit(solution)/shard_map/ppermute | solution.py:379
  172.0 12.4 fusion.116
  191.0 7.9 shard_map.255
  200.9 5.7 all-to-all-start.1
  206.7 13.9 %all-to-all-done.1 = bf16[16,128,128]{1,2,0:T(8,128)(2,1)S(1)} async-done(((bf16[16,128,128]{1,2,0:T(8,128)(2,1)}), bf16[16,128,128]{1,2,0:T(8,128)(2,1)S(1)}, u32[]{:S(2)}, u32[]{:S(2)}) %all-to-all-start.1) | async-done | bytes 524320 | tf_op jit(solution)/shard_map/all_to_all | solution.py:455
  220.7 3.1 fusion.58
  240.1 3.3 broadcast_in_dim.106
  248.4 191.2 %collective-permute-done.9 = bf16[88,2048]{1,0:T(8,128)(2,1)} collective-permute-done((bf16[88,2048]{1,0:T(8,128)(2,1)}, bf16[88,2048]{1,0:T(8,128)(2,1)}, u32[]{:S(2)}, u32[]{:S(2)}) %collective-permute-start.9) | collective-permute-done | bytes 360480 | tf_op jit(solution)/shard_map/ppermute | solution.py:379
  443.8 3.8 constant_dynamic-update-slice_fusion.3
  447.5 4.6 fusion.46
  454.7 8.3 fusion.107
  463.0 8.1 multiply_convert_fusion.7
  476.1 18.7 %fusion.2 = f32[1024,2816]{1,0:T(8,128)} fusion(bf16[1024,2048]{1,0:T(8,128)(2,1)S(1)} %bitcast.215, bf16[1024,2816]{1,0:T(8,128)(2,1)} %collective-permute-done.8, bf16[1024,2816]{1,0:T(8,128)(2,1)} %bitcast.275), kind=kOutput, calls=%fused_computation.6 | convolution fusion | flops 11834228736 | bytes 27262976 | tf_op jit(solution)/shard_map/dot_general | solution.py:76
  494.8 14.9 %multiply_convert_fusion.3 = (bf16[1024,1408]{1,0:T(8,128)(2,1)S(1)}, bf16[1024,1408]{1,0:T(8,128)(2,1)}, bf16[1024,1408]{1,0:T(8,128)(2,1)}) fusion(f32[1024,2816]{1,0:T(8,128)} %fusion.2, bf16[1024,2048]{1,0:T(8,128)(2,1)S(1)} %copy-done.7, bf16[1408,2048]{1,0:T(8,128)(2,1)} %constant_dynamic-update-slice_fusion.3), kind=kOutput, calls=%fused_computation.11 | convolution fusion | flops 5928648704 | bytes 30146560 | tf_op jit(solution)/shard_map/dot_general | solution.py:84
  509.7 17.4 %fusion.3.rows_ref = bf16[1024,2048]{1,0:T(8,128)(2,1)} fusion(bf16[1024,2816]{1,0:T(8,128)(2,1)} %collective-permute-done.8, bf16[1024,2816]{1,0:T(8,128)(2,1)} %bitcast.276, bf16[1024,1408]{1,0:T(8,128)(2,1)} %get-tuple-element.152, bf16[1024,1408]{1,0:T(8,128)(2,1)S(1)} %get-tuple-element.151), kind=kOutput, calls=%fused_computation.16 | convolution fusion | flops 11847860224 | bytes 21495808 | tf_op jit(solution)/shard_map/dot_general | solution.py:84
  527.1 10.9 shard_map.256
  541.7 8.3 convolution_convert_fusion.2
  550.0 8.3 convolution_convert_fusion
  558.4 11.6 multiply_convert_fusion
  570.0 71.6 %reduce-scatter.2.cloned.1.call-done = bf16[128,2048]{1,0:T(8,128)(2,1)} async-done(((bf16[2048,2048]{1,0:T(8,128)(2,1)}), bf16[128,2048]{1,0:T(8,128)(2,1)}) %reduce-scatter.2.cloned.1.call-update) | async-done | bytes 524304 | tf_op jit(solution)/shard_map/reduce_scatter | solution.py:458
  657.9 5.8 all-to-all-start.2
  667.0 17.0 %all-to-all-done.2 = bf16[16,128,128]{2,1,0:T(8,128)(2,1)S(1)} async-done(((bf16[16,128,128]{2,1,0:T(8,128)(2,1)}), bf16[16,128,128]{2,1,0:T(8,128)(2,1)S(1)}, u32[]{:S(2)}, u32[]{:S(2)}) %all-to-all-start.2) | async-done | bytes 524320 | tf_op jit(solution)/shard_map/all_to_all | solution.py:455
  684.8 9.8 shard_map.257
  694.7 3.9 copy.248
  698.6 5.9 all-to-all-start.3
  708.1 23.6 %collective-permute-done.15 = bf16[128,4096]{1,0:T(8,128)(2,1)} collective-permute-done((bf16[128,4096]{1,0:T(8,128)(2,1)}, bf16[128,4096]{1,0:T(8,128)(2,1)}, u32[]{:S(2)}, u32[]{:S(2)}) %collective-permute-start.15) | collective-permute-done | bytes 1048608 | tf_op jit(solution)/shard_map/ppermute | solution.py:379
  735.1 28.6 %all-to-all-done.3 = bf16[16,128,512]{1,2,0:T(8,128)(2,1)} async-done(((bf16[16,128,512]{1,2,0:T(8,128)(2,1)}), bf16[16,128,512]{1,2,0:T(8,128)(2,1)}, u32[]{:S(2)}, u32[]{:S(2)}) %all-to-all-start.3) | async-done | bytes 2097184 | tf_op jit(solution)/shard_map/all_to_all | solution.py:455
  779.4 5.6 fusion.123
  785.2 6.0 fusion.124
  795.8 23.0 %collective-permute-done.21 = bf16[528,1024]{1,0:T(8,128)(2,1)} collective-permute-done((bf16[528,1024]{1,0:T(8,128)(2,1)}, bf16[528,1024]{1,0:T(8,128)(2,1)}, u32[]{:S(2)}, u32[]{:S(2)}) %collective-permute-start.21) | collective-permute-done | bytes 1081376 | tf_op jit(solution)/shard_map/ppermute | solution.py:382
  821.5 3.8 constant_dynamic-slice_fusion.5
  826.4 67.5 %collective-permute-done.13 = bf16[512,3072]{1,0:T(8,128)(2,1)} collective-permute-done((bf16[512,3072]{1,0:T(8,128)(2,1)}, bf16[512,3072]{1,0:T(8,128)(2,1)}, u32[]{:S(2)}, u32[]{:S(2)}) %collective-permute-start.13) | collective-permute-done | bytes 3145760 | tf_op jit(solution)/shard_map/ppermute | solution.py:379
  897.0 10.5 all-to-all-start.6
  907.7 4.0 fusion.28
  914.4 5.2 fusion.30
  921.0 8.9 all-to-all-done.6
  929.9 5.8 fusion.122
  944.5 10.9 collective-permute-done.17
  959.0 4.1 fusion.120
  964.2 5.8 convolution_dynamic-update-slice_fusion.1
  972.1 4.0 fusion.121
  987.5 2.9 collective-permute-done.18
  991.9 7.7 all-to-all-start.4
  999.5 4.0 constant_dynamic-slice_fusion.6
  1005.6 170.9 %collective-permute-done.11 = bf16[704,2048]{1,0:T(8,128)(2,1)} collective-permute-done((bf16[704,2048]{1,0:T(8,128)(2,1)}, bf16[704,2048]{1,0:T(8,128)(2,1)}, u32[]{:S(2)}, u32[]{:S(2)}) %collective-permute-start.11) | collective-permute-done | bytes 2883616 | tf_op jit(solution)/shard_map/ppermute | solution.py:379
  1176.5 7.5 collective-permute-start.12
  1184.1 54.3 %collective-permute-done.23 = bf16[704,2048]{1,0:T(8,128)(2,1)} collective-permute-done((bf16[704,2048]{1,0:T(8,128)(2,1)}, bf16[704,2048]{1,0:T(8,128)(2,1)}, u32[]{:S(2)}, u32[]{:S(2)}) %collective-permute-start.23) | collective-permute-done | bytes 2883616 | tf_op jit(solution)/shard_map/ppermute | solution.py:382
  1238.3 9.6 add_bitcast_fusion.1
  1247.9 12.6 add_bitcast_fusion
  1263.1 8.4 all-to-all-start.5
  1271.7 2.9 multiply_add_fusion
  1279.2 9.8 all-to-all-done.5
  1290.1 3.7 fusion.52
  1296.2 3.3 fusion.7
  1299.5 17.3 %shard_map.259 = f32[1024,5632]{1,0:T(8,128)} custom-call(bf16[16,528,1024]{2,1,0:T(8,128)(2,1)} %bitcast.197), custom_call_target="tpu_custom_call" | custom-call | bytes 34603008 | tf_op jit(solution)/shard_map/pallas_call | solution.py:271
  1316.8 11.7 shard_map.260
  1329.5 15.8 %shard_map.258 = (f32[1024,2048]{1,0:T(8,128)}, f32[1024,3072]{1,0:T(8,128)}, f32[256,4096]{1,0:T(8,128)}, f32[1024,576]{1,0:T(8,128)}) custom-call(bf16[16,1152,384]{2,1,0:T(8,128)(2,1)} %bitcast.200, bf16[16,1152,384]{2,1,0:T(8,128)(2,1)} %bitcast.201), custom_call_target="tpu_custom_call" | custom-call | bytes 42467328 | tf_op jit(solution)/shard_map/pallas_call | solution.py:322
  1345.9 3.1 copy.268
  (407 shorter events, 183.6 us)
Async XLA Ops:
  7.2 86.8 %copy-start.63 = (f32[2,1,64,6]{2,1,3,0:T(1,128)S(1)}, f32[2,1,64,6]{2,1,3,0:T(1,128)}, u32[]{:S(2)}) copy-start(f32[2,1,64,6]{2,1,3,0:T(1,128)} %param.20) | copy-start | bytes 9220
  7.2 86.9 %copy-start.64 = (s32[2,1,64,6]{2,1,3,0:T(1,128)S(1)}, s32[2,1,64,6]{2,1,3,0:T(1,128)}, u32[]{:S(2)}) copy-start(s32[2,1,64,6]{2,1,3,0:T(1,128)} %param.19) | copy-start | bytes 9220
  7.2 93.9 %copy-start.28 = (bf16[1024,576]{0,1:T(8,128)(2,1)S(1)}, bf16[1024,576]{0,1:T(8,128)(2,1)}, u32[]{:S(2)}) copy-start(bf16[1024,576]{0,1:T(8,128)(2,1)} %param.23) | copy-start | bytes 3538948
  7.2 86.7 %all-gather.10.cloned.1.call-start = ((), (), s32[]{:S(2)}) async-start(), calls=%async_computation.8 | async-start | bytes 8912896 | tf_op jit(solution)/shard_map/all_gather | solution.py:449
  9.7 3.5 collective-permute-start
  13.2 85.1 %copy-start.65 = (f32[128]{0:T(128)}, f32[128]{0:T(128)S(1)}, u32[]{:S(2)}) copy-start(f32[128]{0:T(128)S(1)} %rsqrt.38) | copy-start | bytes 1540
  13.3 80.6 %copy-start.53 = (bf16[2,2304]{1,0:T(2,128)(2,1)}, bf16[2,2304]{1,0:T(2,128)(2,1)S(1)}, u32[]{:S(2)}) copy-start(bf16[2,2304]{1,0:T(2,128)(2,1)S(1)} %dynamic_update_slice.61) | copy-start | bytes 27652
  16.9 430.6 %all-gather.14.cloned.1.call-start = ((), (), s32[]{:S(2)}) async-start(), calls=%async_computation.10 | async-start | bytes 8912896 | tf_op jit(solution)/shard_map/all_gather | solution.py:449
  94.8 35.7 %all-to-all-start = ((f32[16,1,128]{2,1,0:T(1,128)}), f32[16,1,128]{2,1,0:T(1,128)S(1)}, u32[]{:S(2)}, u32[]{:S(2)}) async-start(f32[16,1,128]{2,1,0:T(1,128)} %bitcast.2), calls=%async_computation | async-start | bytes 16384 | tf_op jit(solution)/shard_map/all_to_all | solution.py:455
  99.9 34.6 %collective-permute-start.1 = (bf16[1024,192]{0,1:T(8,128)(2,1)S(1)}, bf16[1024,192]{0,1:T(8,128)(2,1)S(1)}, u32[]{:S(2)}, u32[]{:S(2)}) collective-permute-start(bf16[1024,192]{0,1:T(8,128)(2,1)S(1)} %copy.275), channel_id=1, source_target_pairs={{16,0},{0,16},{17,1},{1,17},{18,2},{2,18},{19,3},{3,19},{20,4},{4,... | collective-permute-start | bytes 1179656 | tf_op jit(solution)/shard_map/ppermute | solution.py:379
  101.2 21.9 %collective-permute-start.2 = (bf16[512,576]{0,1:T(8,128)(2,1)S(1)}, bf16[512,576]{0,1:T(8,128)(2,1)}, u32[]{:S(2)}, u32[]{:S(2)}) collective-permute-start(bf16[512,576]{0,1:T(8,128)(2,1)S(1)} %constant_dynamic-slice_fusion.15), channel_id=1, source_target_pairs={{16,0},{0,16},{17,1},{1,17},{18,2},{2,18},{19,3},{3,19},{20,4},{4,... | collective-permute-start | bytes 1769480 | tf_op jit(solution)/shard_map/ppermute | solution.py:379
  102.5 24.3 %copy-start.29 = (bf16[1024,576]{0,1:T(8,128)(2,1)S(1)}, bf16[1024,576]{0,1:T(8,128)(2,1)}, u32[]{:S(2)}) copy-start(bf16[1024,576]{0,1:T(8,128)(2,1)} %param.23) | copy-start | bytes 3538948
  102.5 31.1 %collective-permute-start.4 = (bf16[256,256]{1,0:T(8,128)(2,1)S(1)}, bf16[256,256]{1,0:T(8,128)(2,1)}, u32[]{:S(2)}, u32[]{:S(2)}) collective-permute-start(bf16[256,256]{1,0:T(8,128)(2,1)S(1)} %get-tuple-element.150), channel_id=1, source_target_pairs={{16,0},{0,16},{17,1},{1,17},{18,2},{2,18},{19,3},{3,19},{20,4},{4,... | collective-permute-start | bytes 393224 | tf_op jit(solution)/shard_map/ppermute | solution.py:379
  106.9 20.2 %copy-start.56 = (s32[2,1,1024]{2,1,0:T(1,128)S(1)}, s32[2,1,1024]{2,1,0:T(1,128)}, u32[]{:S(2)}) copy-start(s32[2,1,1024]{2,1,0:T(1,128)} %seg_row.3) | copy-start | bytes 24580
  106.9 64.0 %collective-permute-start.5 = (bf16[512,2048]{1,0:T(8,128)(2,1)}, bf16[512,2048]{1,0:T(8,128)(2,1)}, u32[]{:S(2)}, u32[]{:S(2)}) collective-permute-start(bf16[512,2048]{1,0:T(8,128)(2,1)} %constant_dynamic-slice_fusion.13), channel_id=1, source_target_pairs={{16,0},{0,16},{17,1},{1,17},{18,2},{2,18},{19,3},{3,19},{20,4},{4,... | collective-permute-start | bytes 6291464 | tf_op jit(solution)/shard_map/ppermute | solution.py:379
  107.4 17.5 %copy-start.69 = (f32[32]{0:T(128)}, f32[32]{0:T(128)S(1)}, u32[]{:S(2)}) copy-start(f32[32]{0:T(128)S(1)} %multiply_power_fusion) | copy-start | bytes 388
  123.1 19.5 %collective-permute-start.3 = (bf16[512,576]{0,1:T(8,128)(2,1)}, bf16[512,576]{0,1:T(8,128)(2,1)}, u32[]{:S(2)}, u32[]{:S(2)}) collective-permute-start(bf16[512,576]{0,1:T(8,128)(2,1)} %collective-permute-done.2), channel_id=1, source_target_pairs={{0,1},{1,0},{2,3},{3,2},{4,5},{5,4},{6,7},{7,6},{8,9},{9,8},{10,11... | collective-permute-start | bytes 1769480 | tf_op jit(solution)/shard_map/ppermute | solution.py:429
  130.4 58.8 %copy-start.54 = (f32[1,2,2,128]{3,1,2,0:T(2,128)}, f32[1,2,2,128]{3,1,2,0:T(2,128)S(1)}, u32[]{:S(2)}) copy-start(f32[1,2,2,128]{3,1,2,0:T(2,128)S(1)} %copy.287) | copy-start | bytes 6148
  130.4 21.3 %copy-start.48 = (f32[16,1,128]{2,1,0:T(1,128)}, f32[16,1,128]{2,1,0:T(1,128)S(1)}, u32[]{:S(2)}) copy-start(f32[16,1,128]{2,1,0:T(1,128)S(1)} %all-to-all-done) | copy-start | bytes 24580
  155.9 29.4 %copy-start.31 = (f32[16,64,128]{2,1,0:T(8,128)S(1)}, f32[16,64,128]{2,1,0:T(8,128)}, u32[]{:S(2)}) copy-start(f32[16,64,128]{2,1,0:T(8,128)} %get-tuple-element.189) | copy-start | bytes 1572868
  155.9 29.4 %copy-start.32 = (f32[16,64,128]{2,1,0:T(8,128)S(1)}, f32[16,64,128]{2,1,0:T(8,128)}, u32[]{:S(2)}) copy-start(f32[16,64,128]{2,1,0:T(8,128)} %get-tuple-element.190) | copy-start | bytes 1572868
  170.9 55.0 %collective-permute-start.6 = (bf16[512,2048]{1,0:T(8,128)(2,1)}, bf16[512,2048]{1,0:T(8,128)(2,1)S(1)}, u32[]{:S(2)}, u32[]{:S(2)}) collective-permute-start(bf16[512,2048]{1,0:T(8,128)(2,1)} %collective-permute-done.5), channel_id=1, source_target_pairs={{0,1},{1,0},{2,3},{3,2},{4,5},{5,4},{6,7},{7,6},{8,9},{9,8},{10,11... | collective-permute-start | bytes 6291464 | tf_op jit(solution)/shard_map/ppermute | solution.py:429
  191.0 15.7 %copy-start.59 = (f32[1,8,2,128]{3,2,1,0:T(2,128)S(1)}, f32[1,8,2,128]{3,2,1,0:T(2,128)}, u32[]{:S(2)}) copy-start(f32[1,8,2,128]{3,2,1,0:T(2,128)} %get-tuple-element.175) | copy-start | bytes 24580
  200.9 19.7 %all-to-all-start.1 = ((bf16[16,128,128]{1,2,0:T(8,128)(2,1)}), bf16[16,128,128]{1,2,0:T(8,128)(2,1)S(1)}, u32[]{:S(2)}, u32[]{:S(2)}) async-start(bf16[16,128,128]{1,2,0:T(8,128)(2,1)} %copy.231), calls=%async_computation.1 | async-start | bytes 1048576 | tf_op jit(solution)/shard_map/all_to_all | solution.py:455
  206.6 248.0 %all-gather.12.cloned.1.call-start = ((), (), s32[]{:S(2)}) async-start(), calls=%async_computation.9 | async-start | bytes 8912896 | tf_op jit(solution)/shard_map/all_gather | solution.py:449
  206.7 19.8 %copy-start.43 = (f32[1,8,2,128]{3,1,2,0:T(8,128)}, f32[1,8,2,128]{3,1,2,0:T(8,128)S(1)}, u32[]{:S(2)}) copy-start(f32[1,8,2,128]{3,1,2,0:T(8,128)S(1)} %copy.295) | copy-start | bytes 24580
  228.8 412.8 %reduce-scatter.2.cloned.1.call-start = ((), (), s32[]{:S(2)}) async-start(), calls=%async_computation.11 | async-start | bytes 8912896 | tf_op jit(solution)/shard_map/reduce_scatter | solution.py:458
  228.8 245.3 %collective-permute-start.8 = (bf16[1024,2816]{1,0:T(8,128)(2,1)}, bf16[1024,2816]{1,0:T(8,128)(2,1)}, u32[]{:S(2)}, u32[]{:S(2)}) collective-permute-start(bf16[1024,2816]{1,0:T(8,128)(2,1)} %bitcast.274), channel_id=1, source_target_pairs={{16,0},{0,16},{17,1},{1,17},{18,2},{2,18},{19,3},{3,19},{20,4},{4,... | collective-permute-start | bytes 17301512 | tf_op jit(solution)/shard_map/ppermute | solution.py:379
  230.1 213.7 %collective-permute-start.7 = (bf16[704,2048]{1,0:T(8,128)(2,1)}, bf16[704,2048]{1,0:T(8,128)(2,1)}, u32[]{:S(2)}, u32[]{:S(2)}) collective-permute-start(bf16[704,2048]{1,0:T(8,128)(2,1)} %bitcast.233), channel_id=1, source_target_pairs={{16,0},{0,16},{17,1},{1,17},{18,2},{2,18},{19,3},{3,19},{20,4},{4,... | collective-permute-start | bytes 8650760 | tf_op jit(solution)/shard_map/ppermute | solution.py:379
  233.8 207.6 %collective-permute-start.10 = (bf16[352,1024]{1,0:T(8,128)(2,1)}, bf16[352,1024]{1,0:T(8,128)(2,1)}, u32[]{:S(2)}, u32[]{:S(2)}) collective-permute-start(bf16[352,1024]{1,0:T(8,128)(2,1)} %pad_maximum_fusion.11), channel_id=1, source_target_pairs={{16,0},{0,16},{17,1},{1,17},{18,2},{2,18},{19,3},{3,19},{20,4},{4,... | collective-permute-start | bytes 2162696 | tf_op jit(solution)/shard_map/ppermute | solution.py:379
  238.0 201.6 %collective-permute-start.9 = (bf16[88,2048]{1,0:T(8,128)(2,1)}, bf16[88,2048]{1,0:T(8,128)(2,1)}, u32[]{:S(2)}, u32[]{:S(2)}) collective-permute-start(bf16[88,2048]{1,0:T(8,128)(2,1)} %get-tuple-element.148), channel_id=1, source_target_pairs={{16,0},{0,16},{17,1},{1,17},{18,2},{2,18},{19,3},{3,19},{20,4},{4,... | collective-permute-start | bytes 1081352 | tf_op jit(solution)/shard_map/ppermute | solution.py:379
  245.2 196.2 %copy-start.36 = (bf16[1024,88]{0,1:T(8,128)(2,1)S(1)}, bf16[1024,88]{0,1:T(8,128)(2,1)}, u32[]{:S(2)}) copy-start(bf16[1024,88]{0,1:T(8,128)(2,1)} %copy-done.35) | copy-start | bytes 540676
  454.7 18.2 %slice-start = ((s8[8388608]{0:T(1024)(128)(4,1)}), s8[4194304]{0:T(1024)(128)(4,1)S(1)}, s32[]{:S(2)}) async-start(s8[8388608]{0:T(1024)(128)(4,1)} %bitcast.202), calls=%async_computation.16 | async-start | bytes 8388608
  476.1 18.7 %copy-start.7 = (bf16[1024,2048]{1,0:T(8,128)(2,1)S(1)}, bf16[1024,2048]{1,0:T(8,128)(2,1)}, u32[]{:S(2)}) copy-start(bf16[1024,2048]{1,0:T(8,128)(2,1)} %fusion) | copy-start | bytes 12582916
  538.1 391.8 %all-gather.16.cloned.1.call-start = ((), (), s32[]{:S(2)}) async-start(), calls=%async_computation.12 | async-start | bytes 8912896 | tf_op jit(solution)/shard_map/all_gather | solution.py:449
  558.4 83.2 %copy-start.1 = (f32[128,2048]{1,0:T(8,128)S(1)}, f32[128,2048]{1,0:T(8,128)}, u32[]{:S(2)}) copy-start(f32[128,2048]{1,0:T(8,128)} %copy-done) | copy-start | bytes 3145732
  558.4 83.2 %copy-start.44 = (f32[1,8,2,128]{3,1,2,0:T(8,128)S(1)}, f32[1,8,2,128]{3,1,2,0:T(8,128)}, u32[]{:S(2)}) copy-start(f32[1,8,2,128]{3,1,2,0:T(8,128)} %copy-done.43) | copy-start | bytes 24580
  558.4 83.2 %copy-start.61 = (f32[128]{0:T(128)S(1)}, f32[128]{0:T(128)}, u32[]{:S(2)}) copy-start(f32[128]{0:T(128)} %copy-done.60) | copy-start | bytes 1540
  558.4 84.8 %copy-start.21 = (bf16[2,1,64,2048]{3,2,1,0:T(8,128)(2,1)S(1)}, bf16[2,1,64,2048]{3,2,1,0:T(8,128)(2,1)}, u32[]{:S(2)}) copy-start(bf16[2,1,64,2048]{3,2,1,0:T(8,128)(2,1)} %param.17) | copy-start | bytes 1572868
  649.7 14.0 %copy-start.70 = (f32[32]{0:T(128)S(1)}, f32[32]{0:T(128)}, u32[]{:S(2)}) copy-start(f32[32]{0:T(128)} %copy-done.69) | copy-start | bytes 388
  657.9 26.1 %all-to-all-start.2 = ((bf16[16,128,128]{2,1,0:T(8,128)(2,1)}), bf16[16,128,128]{2,1,0:T(8,128)(2,1)S(1)}, u32[]{:S(2)}, u32[]{:S(2)}) async-start(bf16[16,128,128]{2,1,0:T(8,128)(2,1)} %bitcast_bitcast_fusion.1), calls=%async_computation.3 | async-start | bytes 1048576 | tf_op jit(solution)/shard_map/all_to_all | solution.py:455
  698.6 65.1 %all-to-all-start.3 = ((bf16[16,128,512]{1,2,0:T(8,128)(2,1)}), bf16[16,128,512]{1,2,0:T(8,128)(2,1)}, u32[]{:S(2)}, u32[]{:S(2)}) async-start(bf16[16,128,512]{1,2,0:T(8,128)(2,1)} %copy.248), calls=%async_computation.4 | async-start | bytes 4194304 | tf_op jit(solution)/shard_map/all_to_all | solution.py:455
  704.5 279.0 %all-gather.18.cloned.1.call-start = ((), (), s32[]{:S(2)}) async-start(), calls=%async_computation.13 | async-start | bytes 3133440 | tf_op jit(solution)/shard_map/all_gather | solution.py:449
  706.8 24.9 %collective-permute-start.15 = (bf16[128,4096]{1,0:T(8,128)(2,1)}, bf16[128,4096]{1,0:T(8,128)(2,1)}, u32[]{:S(2)}, u32[]{:S(2)}) collective-permute-start(bf16[128,4096]{1,0:T(8,128)(2,1)} %constant_dynamic-slice_fusion.4), channel_id=1, source_target_pairs={{16,0},{0,16},{17,1},{1,17},{18,2},{2,18},{19,3},{3,19},{20,4},{4,... | collective-permute-start | bytes 3145736 | tf_op jit(solution)/shard_map/ppermute | solution.py:379
  731.7 38.8 %collective-permute-start.16 = (bf16[128,4096]{1,0:T(8,128)(2,1)}, bf16[128,4096]{1,0:T(8,128)(2,1)}, u32[]{:S(2)}, u32[]{:S(2)}) collective-permute-start(bf16[128,4096]{1,0:T(8,128)(2,1)} %collective-permute-done.15), channel_id=1, source_target_pairs={{0,1},{1,0},{2,3},{3,2},{4,5},{5,4},{6,7},{7,6},{8,9},{9,8},{10,11... | collective-permute-start | bytes 3145736 | tf_op jit(solution)/shard_map/ppermute | solution.py:429
  779.4 520.1 %all-gather.22.cloned.1.call-start = ((), (), s32[]{:S(2)}) async-start(), calls=%async_computation.15 | async-start | bytes 18382848 | tf_op jit(solution)/shard_map/all_gather | solution.py:452
  792.4 26.4 %slice-start.2 = ((f32[352,2048]{1,0:T(8,128)}), f32[352,1024]{1,0:T(8,128)S(1)}, s32[]{:S(2)}) async-start(f32[352,2048]{1,0:T(8,128)} %copy-done.17), calls=%async_computation.18 | async-start | bytes 2883584 | tf_op jit(solution)/shard_map/slice | solution.py:601
  793.5 25.3 %collective-permute-start.21 = (bf16[528,1024]{1,0:T(8,128)(2,1)}, bf16[528,1024]{1,0:T(8,128)(2,1)}, u32[]{:S(2)}, u32[]{:S(2)}) collective-permute-start(bf16[528,1024]{1,0:T(8,128)(2,1)} %pad_maximum_fusion.8), channel_id=1, source_target_pairs={{0,16},{16,0},{1,17},{17,1},{2,18},{18,2},{3,19},{19,3},{4,20},{20... | collective-permute-start | bytes 3244040 | tf_op jit(solution)/shard_map/ppermute | solution.py:382
  821.5 86.2 %copy-start.58 = (f32[2048]{0:T(1024)S(1)}, f32[2048]{0:T(1024)}, u32[]{:S(2)}) copy-start(f32[2048]{0:T(1024)} %copy-done.57) | copy-start | bytes 24580
  825.2 68.7 %collective-permute-start.13 = (bf16[512,3072]{1,0:T(8,128)(2,1)}, bf16[512,3072]{1,0:T(8,128)(2,1)}, u32[]{:S(2)}, u32[]{:S(2)}) collective-permute-start(bf16[512,3072]{1,0:T(8,128)(2,1)} %constant_dynamic-slice_fusion.5), channel_id=1, source_target_pairs={{16,0},{0,16},{17,1},{1,17},{18,2},{2,18},{19,3},{3,19},{20,4},{4,... | collective-permute-start | bytes 9437192 | tf_op jit(solution)/shard_map/ppermute | solution.py:379
  894.0 78.1 %collective-permute-start.14 = (bf16[512,3072]{1,0:T(8,128)(2,1)}, bf16[512,3072]{1,0:T(8,128)(2,1)}, u32[]{:S(2)}, u32[]{:S(2)}) collective-permute-start(bf16[512,3072]{1,0:T(8,128)(2,1)} %collective-permute-done.13), channel_id=1, source_target_pairs={{0,1},{1,0},{2,3},{3,2},{4,5},{5,4},{6,7},{7,6},{8,9},{9,8},{10,11... | collective-permute-start | bytes 9437192 | tf_op jit(solution)/shard_map/ppermute | solution.py:429
  897.0 32.9 %all-to-all-start.6 = ((bf16[16,128,128]{2,1,0:T(8,128)(2,1)}), bf16[16,128,128]{2,1,0:T(8,128)(2,1)}, u32[]{:S(2)}, u32[]{:S(2)}) async-start(bf16[16,128,128]{2,1,0:T(8,128)(2,1)} %bitcast_bitcast_fusion), calls=%async_computation.7 | async-start | bytes 1048576 | tf_op jit(solution)/shard_map/all_to_all | solution.py:455
  907.5 421.1 %all-gather.20.cloned.1.call-start = ((), (), s32[]{:S(2)}) async-start(), calls=%async_computation.14 | async-start | bytes 15040512 | tf_op jit(solution)/shard_map/all_gather | solution.py:452
  936.9 18.6 %collective-permute-start.17 = (bf16[1024,384]{1,0:T(8,128)(2,1)}, bf16[1024,384]{1,0:T(8,128)(2,1)}, u32[]{:S(2)}, u32[]{:S(2)}) collective-permute-start(bf16[1024,384]{1,0:T(8,128)(2,1)} %pad_maximum_fusion.10), channel_id=1, source_target_pairs={{0,16},{16,0},{1,17},{17,1},{2,18},{18,2},{3,19},{19,3},{4,20},{20... | collective-permute-start | bytes 2359304 | tf_op jit(solution)/shard_map/ppermute | solution.py:382
  982.1 5.2 collective-permute-start.19
  987.1 3.4 collective-permute-start.18
  991.6 256.3 %collective-permute-start.22 = (bf16[1024,2816]{1,0:T(8,128)(2,1)}, bf16[1024,2816]{1,0:T(8,128)(2,1)}, u32[]{:S(2)}, u32[]{:S(2)}) collective-permute-start(bf16[1024,2816]{1,0:T(8,128)(2,1)} %convolution_convert_fusion), channel_id=1, source_target_pairs={{0,16},{16,0},{1,17},{17,1},{2,18},{18,2},{3,19},{19,3},{4,20},{20... | collective-permute-start | bytes 17301512 | tf_op jit(solution)/shard_map/ppermute | solution.py:382
  991.9 269.9 %all-to-all-start.4 = ((bf16[16,64,2048]{2,1,0:T(8,128)(2,1)}), bf16[16,64,2048]{2,1,0:T(8,128)(2,1)}, u32[]{:S(2)}, u32[]{:S(2)}) async-start(bf16[16,64,2048]{2,1,0:T(8,128)(2,1)} %bitcast.227), calls=%async_computation.5 | async-start | bytes 8388608 | tf_op jit(solution)/shard_map/all_to_all | solution.py:455
  1003.6 172.9 %collective-permute-start.11 = (bf16[704,2048]{1,0:T(8,128)(2,1)}, bf16[704,2048]{1,0:T(8,128)(2,1)}, u32[]{:S(2)}, u32[]{:S(2)}) collective-permute-start(bf16[704,2048]{1,0:T(8,128)(2,1)} %constant_dynamic-slice_fusion.6), channel_id=1, source_target_pairs={{16,0},{0,16},{17,1},{1,17},{18,2},{2,18},{19,3},{3,19},{20,4},{4,... | collective-permute-start | bytes 8650760 | tf_op jit(solution)/shard_map/ppermute | solution.py:379
  1004.8 233.5 %collective-permute-start.23 = (bf16[704,2048]{1,0:T(8,128)(2,1)}, bf16[704,2048]{1,0:T(8,128)(2,1)}, u32[]{:S(2)}, u32[]{:S(2)}) collective-permute-start(bf16[704,2048]{1,0:T(8,128)(2,1)} %convolution_convert_fusion.2), channel_id=1, source_target_pairs={{0,16},{16,0},{1,17},{17,1},{2,18},{18,2},{3,19},{19,3},{4,20},{20... | collective-permute-start | bytes 8650760 | tf_op jit(solution)/shard_map/ppermute | solution.py:382
  1005.6 242.3 %copy-start.16 = (bf16[32,32,2048]{2,1,0:T(8,128)(2,1)S(1)}, bf16[32,32,2048]{2,1,0:T(8,128)(2,1)}, u32[]{:S(2)}) copy-start(bf16[32,32,2048]{2,1,0:T(8,128)(2,1)} %copy-done.14) | copy-start | bytes 12582916
  1176.5 119.7 %collective-permute-start.12 = (bf16[704,2048]{1,0:T(8,128)(2,1)}, bf16[704,2048]{1,0:T(8,128)(2,1)}, u32[]{:S(2)}, u32[]{:S(2)}) collective-permute-start(bf16[704,2048]{1,0:T(8,128)(2,1)} %collective-permute-done.11), channel_id=1, source_target_pairs={{0,1},{1,0},{2,3},{3,2},{4,5},{5,4},{6,7},{7,6},{8,9},{9,8},{10,11... | collective-permute-start | bytes 8650760 | tf_op jit(solution)/shard_map/ppermute | solution.py:429
  1263.1 25.9 %all-to-all-start.5 = ((bf16[16,128,176]{1,2,0:T(8,128)(2,1)}), bf16[16,128,176]{1,2,0:T(8,128)(2,1)}, u32[]{:S(2)}, u32[]{:S(2)}) async-start(bf16[16,128,176]{1,2,0:T(8,128)(2,1)} %copy.251), calls=%async_computation.6 | async-start | bytes 1441792 | tf_op jit(solution)/shard_map/all_to_all | solution.py:455
  1271.5 3.1 collective-permute-start.20
  (50 other events, 291.7 us)
Sparse Core Ops, SparseCore 0:
  17.0 76.8 all-gather.9
  96.1 72.8 all-gather.13
  228.9 73.9 all-gather.11
  538.2 103.3 reduce-scatter.1
  643.6 119.0 all-gather.15
  779.5 50.1 all-gather.17
  831.8 98.4 all-gather.21
  991.7 189.3 all-gather.19
where the time goes:
time: 1370 us; the launch traced here: 1360 us
  waiting for transfers between devices  801 us (58%)
  matrix products  211 us (15%)
  local copies, waits for them, and re-layouts  113 us (8%)
  starting transfers between devices  78.1 us (6%)
  Pallas kernels  73.6 us (5%)
  other arithmetic  63.9 us (5%)
  between operations  16.1 us (1%)
    ppermute x12, waiting for transfers between devices, shift(): lax.ppermute(x, 'dp', [((i + step) % parts, i) for i in range(parts)])  482 us
    ppermute x7, waiting for transfers between devices, send(): lax.ppermute(x, 'dp', [(i, (i + step) % parts) for i in range(parts)])  91.1 us
    all_to_all x7, waiting for transfers between devices, swap(): return lax.all_to_all(x, 'expert', split_axis=0, concat_axis=0, tiled=True)  78.2 us
    dot_general x14, matrix products, dot_nt(): lax.dot_general(left, right, (((1,), (1,)), ((), ())), preferred_element_...  77.7 us
    all_gather x5, waiting for transfers between devices, spread(): return lax.all_gather(x, 'expert', axis=0, tiled=True)  77 us
    reduce_scatter x1, waiting for transfers between devices, collect(): return lax.psum_scatter(x, 'expert', scatter_dimension=0, tiled=True)  71.6 us
    dot_general x10, matrix products, dot_tn(): lax.dot_general(left, right, (((0,), (0,)), ((), ())), preferred_element_...  66.8 us
    dot_general x10, matrix products, dot(): return jnp.dot(left, right, preferred_element_type=f32)  59.6 us
  transfers between devices with their start and end apart: 39, of which 17 were waited for; matrix products, arithmetic and copies ran while one was open for 23% of the time, Pallas kernels for 3%

commit v1 on v0

--- a/solution.py
+++ b/solution.py
@@ -214,13 +214,15 @@
     )(q_nope, roped, kvup, segs[:, :, None], segs[:, None, :], lse, dout, cosine, sine)
 
 
-def put_back_kernel(place_ref, rows_ref, units_ref, weight_ref, out_ref):
+def put_back_kernel(place_ref, rows_ref, units_ref, *refs):
+    *weight_refs, out_ref = refs
     left = jnp.concatenate([place_ref[0], units_ref[...]], 1)
-    right = jnp.concatenate([rows_ref[...], weight_ref[...]], 0)
+    weight = jnp.concatenate([w[...] for w in weight_refs], 1)
+    right = jnp.concatenate([rows_ref[...], weight], 0)
     out_ref[...] = dot(left, right).astype(bf16)
 
 
-def put_back(place, rows, units, weight):
+def put_back(place, rows, units, *weights):
     many, size, height = place.shape
     total, count = units.shape
     width = rows.shape[1]
@@ -232,15 +234,15 @@
             pl.BlockSpec((1, size, height), lambda i: (i, 0, 0)),
             pl.BlockSpec((height, width), lambda i: (i, 0)),
             pl.BlockSpec((size, count), lambda i: (i, 0)),
-            pl.BlockSpec(weight.shape, lambda i: (0, 0)),
+            *(pl.BlockSpec(w.shape, lambda i: (0, 0)) for w in weights),
         ],
         out_specs=pl.BlockSpec((size, width), lambda i: (i, 0)),
         cost_estimate=pl.CostEstimate(
             flops=2 * total * width * (height + count),
             transcendentals=0,
-            bytes_accessed=2 * (total * width + rows.size + units.size + weight.size),
-        ),
-    )(place, rows, units, weight)
+            bytes_accessed=2 * (total * width + rows.size + units.size + count * width),
+        ),
+    )(place, rows, units, *weights)
 
 
 def shared_in_kernel(x_ref, out_ref, *, runs, piece):
@@ -306,12 +308,14 @@
             x[c * step : (c + 1) * step, a + b :] for x in (one, two) for c in range(runs)
         ]
         kvup_ref[:, e * runs * rest : (e + 2) * runs * rest] = jnp.concatenate(pieces, 1)
+    half = count // 2
+    rows = []
     for e in range(extra_ref.shape[0]):
         x = extra_ref[e].astype(f32)
         tail = x[height : height + height // 2]
-        half = count // 2
         tail = jnp.concatenate([tail[:, :half], tail[:, half:]], 0)
-        down_ref[e * height : (e + 1) * height] = jnp.concatenate([x[:height], tail], 1)
+        rows.append(jnp.concatenate([x[:height], tail], 1))
+    down_ref[...] = jnp.concatenate(rows, 0).T
 
 
 def attn_rows(stacked, rows, a, b, kvup_height, down_height):
@@ -325,7 +329,7 @@
             jax.ShapeDtypeStruct((rows, groups * a), f32),
             jax.ShapeDtypeStruct((rows, groups * b), f32),
             jax.ShapeDtypeStruct((kvup_height, groups * kvup_width), f32),
-            jax.ShapeDtypeStruct((groups * down_height, count * 3 // 2), f32),
+            jax.ShapeDtypeStruct((count * 3 // 2, groups * down_height), f32),
         ),
         grid=(steps,),
         in_specs=[
@@ -336,7 +340,7 @@
             pl.BlockSpec((size, groups * a), lambda i: (i, 0)),
             pl.BlockSpec((size, groups * b), lambda i: (i, 0)),
             pl.BlockSpec((kvup_height // steps, groups * kvup_width), lambda i: (i, 0)),
-            pl.BlockSpec((groups // steps * down_height, count * 3 // 2), lambda i: (i, 0)),
+            pl.BlockSpec((count * 3 // 2, groups // steps * down_height), lambda i: (0, i)),
         ),
         cost_estimate=pl.CostEstimate(
             flops=0, transcendentals=0, bytes_accessed=6 * stacked.size
@@ -534,7 +538,8 @@
         0,
     )
     wso_own = lax.dynamic_slice_in_dim(w_shared_out, me * run, run, 0)
-    wsi_me = jnp.concatenate([wsi_own] + others(wsi_own), 1)
+    wsi_blocks = [wsi_own] + others(wsi_own)
+    wsi_me = jnp.concatenate(wsi_blocks, 1)
     wso_me = lay_out(wso_own, others(wso_own))
     wei_others = others(w_expert_in[0])
     weo_others = others(w_expert_out[0])
@@ -578,7 +583,9 @@
     weo = lay_out(w_expert_out[0], weo_others)
     epre = dot(arrived, wei)
     eact = swiglu(epre).astype(bf16)
-    deact = dot_nt(dyexp, weo)
+    gated = (gate_slots * dot(eact, weo)).astype(bf16)
+    returned = swap(gated.reshape(groups, micro * capacity, width))
+    deact = dot_nt(after(dyexp, gated), weo)
     depre = swiglu_back(epre, deact).astype(bf16)
     dhid_rows = dot_nt(depre, wei).astype(bf16)
 
@@ -586,7 +593,7 @@
     sact = swiglu(spre).astype(bf16)
     dsact = dot_nt(dy_all, wso_me)
     dspre = swiglu_back(spre, dsact).astype(bf16)
-    dhid_part = put_back(place, dhid_rows, dspre, wsi_me)
+    dhid_part = put_back(place, dhid_rows, dspre, *wsi_blocks)
     dhid_sum = collect(dhid_part)
 
     arrived, depre, eact, dyexp, dspre, sact = lax.optimization_barrier(
@@ -614,8 +621,8 @@
 
     sent_in = [expert_in_grad(r).astype(bf16) for r in range(1, parts)]
     sent_out = [expert_out_grad(r).astype(bf16) for r in range(1, parts)]
-    gated = (gate_slots * dot(eact, weo)).astype(bf16)
-    dhid_sum = after(dhid_sum, gated, *sent_in, *sent_out)
+    hidden = swap(after(sact, returned).reshape(groups, own, -1))
+    dhid_sum = after(dhid_sum, returned, hidden, *sent_in, *sent_out)
     got_in = [send(x, r).astype(f32) for r, x in enumerate(sent_in, 1)]
     got_out = [send(x, r).astype(f32) for r, x in enumerate(sent_out, 1)]
     dhid = natural(dhid_sum, 1).astype(f32)
@@ -659,9 +666,7 @@
 
     g_attn = exchanged(attn_grads(0), lambda r: attn_grads(r).astype(bf16))
 
-    gated, sact = lax.optimization_barrier((gated, sact, moved))[:2]
-    returned = swap(gated.reshape(groups, micro * capacity, width))
-    hidden = swap(after(sact, returned).reshape(groups, own, -1))
+    returned, hidden = lax.optimization_barrier((returned, hidden, moved))[:2]
     hidden = hidden.reshape(groups, own, parts, run).transpose(1, 2, 0, 3).reshape(own, ff)
     hit_own = routes_own.reshape(micro, rows, 1, top) == expert_ids[:, None]
     hit_own = jnp.any(hit_own, -1)
@@ -745,7 +750,7 @@
         input_grad.reshape(micro, 1, rows, width),
         gains[0],
         query_grad,
-        g_down,
+        g_down.T,
         gains[1],
         kvup_grad,
         out_grad,

time: 1370 us -> 1420 us (1.036)
  waiting for transfers between devices: 801 us -> 845 us
    all_to_all x7, waiting for transfers between devices: 78.2 us -> 182 us  [swap(): return lax.all_to_all(x, 'expert', split_axis=0, concat_axis=0, tiled=True)]
    reduce_scatter x1, waiting for transfers between devices: 71.6 us -> 0.01 us  [collect(): return lax.psum_scatter(x, 'expert', scatter_dimension=0, tiled=True)]
  transfers between devices with their start and end apart: 39 -> 39, of which waited for: 17 -> 17; matrix products, arithmetic and copies ran while one was open for 23% -> 24% of each run, Pallas kernels for 3% -> 3%
where the time goes in v1:
time: 1420 us; the launch traced here: 1400 us
  waiting for transfers between devices  845 us (60%)
  matrix products  208 us (15%)
  local copies, waits for them, and re-layouts  112 us (8%)
  starting transfers between devices  86.9 us (6%)
  Pallas kernels  73.6 us (5%)
  other arithmetic  62.8 us (4%)
  between operations  16.2 us (1%)
    ppermute x12, waiting for transfers between devices, shift(): lax.ppermute(x, 'dp', [((i + step) % parts, i) for i in range(parts)])  494 us
    all_to_all x7, waiting for transfers between devices, swap(): return lax.all_to_all(x, 'expert', split_axis=0, concat_axis=0, tiled=True)  182 us
    ppermute x7, waiting for transfers between devices, send(): lax.ppermute(x, 'dp', [(i, (i + step) % parts) for i in range(parts)])  91 us
    all_gather x5, waiting for transfers between devices, spread(): return lax.all_gather(x, 'expert', axis=0, tiled=True)  77 us
    dot_general x14, matrix products, dot_nt(): lax.dot_general(left, right, (((1,), (1,)), ((), ())), preferred_element_...  73.4 us
    dot_general x10, matrix products, dot_tn(): lax.dot_general(left, right, (((0,), (0,)), ((), ())), preferred_element_...  67.8 us
    dot_general x10, matrix products, dot(): return jnp.dot(left, right, preferred_element_type=f32)  56.4 us
    all_to_all x7, starting transfers between devices, swap(): return lax.all_to_all(x, 'expert', split_axis=0, concat_axis=0, tiled=True)  55.7 us
  transfers between devices with their start and end apart: 39, of which 17 were waited for; matrix products, arithmetic and copies ran while one was open for 24% of the time, Pallas kernels for 3%

profile of v1, /device:TPU:1, one launch (start us, length us, event | category | flops | bytes accessed | tf_op | source)
XLA Modules:
  0.0 1403.9 jit_solution(6741433391782702781)
XLA Ops:
  16.4 77.0 %all-gather.10.cloned.1.call-done = bf16[2048,2048]{1,0:T(8,128)(2,1)} async-done(((bf16[128,2048]{1,0:T(8,128)(2,1)}), bf16[2048,2048]{1,0:T(8,128)(2,1)}) %all-gather.10.cloned.1.call-update) | async-done | bytes 8388624 | tf_op jit(solution)/shard_map/all_gather | solution.py:453
  94.2 3.5 all-to-all-start
  103.7 3.2 constant_dynamic-slice_fusion.13
  109.3 13.2 collective-permute-done.2
  130.9 7.2 dynamic_update_slice.63
  138.2 7.6 dynamic_update_slice.64
  151.5 18.8 %collective-permute-done.5 = bf16[512,2048]{1,0:T(8,128)(2,1)} collective-permute-done((bf16[512,2048]{1,0:T(8,128)(2,1)}, bf16[512,2048]{1,0:T(8,128)(2,1)}, u32[]{:S(2)}, u32[]{:S(2)}) %collective-permute-start.5) | collective-permute-done | bytes 2097184 | tf_op jit(solution)/shard_map/ppermute | solution.py:383
  171.4 12.4 fusion.120
  190.4 7.9 shard_map.255
  200.3 5.7 all-to-all-start.1
  206.1 13.9 all-to-all-done.1
  220.0 3.1 fusion.62
  238.1 3.3 broadcast_in_dim.106
  246.3 192.7 %collective-permute-done.9 = bf16[88,2048]{1,0:T(8,128)(2,1)} collective-permute-done((bf16[88,2048]{1,0:T(8,128)(2,1)}, bf16[88,2048]{1,0:T(8,128)(2,1)}, u32[]{:S(2)}, u32[]{:S(2)}) %collective-permute-start.9) | collective-permute-done | bytes 360480 | tf_op jit(solution)/shard_map/ppermute | solution.py:383
  440.8 3.8 constant_dynamic-update-slice_fusion.3
  444.6 4.6 fusion.50
  451.8 4.6 convolution_convert_fusion.1
  456.4 17.5 %fusion.2 = f32[1024,2816]{1,0:T(8,128)S(1)} fusion(bf16[1024,2048]{1,0:T(8,128)(2,1)S(1)} %bitcast.218, bf16[1024,2816]{1,0:T(8,128)(2,1)} %collective-permute-done.7, bf16[1024,2816]{1,0:T(8,128)(2,1)} %bitcast.275), kind=kOutput, calls=%fused_computation.6 | convolution fusion | flops 11834228736 | bytes 27262976 | tf_op jit(solution)/shard_map/dot_general | solution.py:76
  474.0 4.4 copy-done.13
  481.8 10.9 multiply_convert_fusion
  492.7 14.5 %multiply_convert_fusion.2 = (bf16[1024,1408]{1,0:T(8,128)(2,1)}, bf16[1024,1408]{1,0:T(8,128)(2,1)}) fusion(f32[1024,2816]{1,0:T(8,128)} %copy-done.13, bf16[1024,2048]{1,0:T(8,128)(2,1)S(1)} %copy-done.6, bf16[1408,2048]{1,0:T(8,128)(2,1)} %constant_dynamic-update-slice_fusion.3), kind=kOutput, calls=%fused_computation.10 | convolution fusion | flops 5924323328 | bytes 27262976 | tf_op jit(solution)/shard_map/dot_general | solution.py:84
  507.2 7.3 fusion.14
  514.5 4.5 multiply_convert_fusion.7
  520.9 18.2 %fusion.3.rows_ref = bf16[1024,2048]{1,0:T(8,128)(2,1)} fusion(bf16[1024,2816]{1,0:T(8,128)(2,1)} %collective-permute-done.7, bf16[1024,2816]{1,0:T(8,128)(2,1)} %bitcast.276, bf16[1024,1408]{1,0:T(8,128)(2,1)} %get-tuple-element.154, bf16[1024,1408]{1,0:T(8,128)(2,1)} %get-tuple-element.153), kind=kOutput, calls=%fused_computation.16 | convolution fusion | flops 11847860224 | bytes 21495808 | tf_op jit(solution)/shard_map/dot_general | solution.py:84
  539.1 10.9 shard_map.256
  550.0 5.6 all-to-all-start.2
  556.2 6.7 pad_maximum_fusion.3
  564.1 4.9 convolution_convert_fusion.2
  569.1 98.4 %all-to-all-done.2 = bf16[16,64,2048]{2,1,0:T(8,128)(2,1)} async-done(((bf16[16,64,2048]{2,1,0:T(8,128)(2,1)}), bf16[16,64,2048]{2,1,0:T(8,128)(2,1)}, u32[]{:S(2)}, u32[]{:S(2)}) %all-to-all-start.2) | async-done | bytes 4194336 | tf_op jit(solution)/shard_map/all_to_all | solution.py:459
  668.7 19.1 %all-to-all-start.3 = ((bf16[16,128,176]{1,2,0:T(8,128)(2,1)}), bf16[16,128,176]{1,2,0:T(8,128)(2,1)S(1)}, u32[]{:S(2)}, u32[]{:S(2)}) async-start(bf16[16,128,176]{1,2,0:T(8,128)(2,1)} %copy.241), calls=%async_computation.3 | async-start | bytes 1441792 | tf_op jit(solution)/shard_map/all_to_all | solution.py:459
  687.9 11.1 convolution_convert_fusion
  699.0 16.3 %all-to-all-done.3 = bf16[16,128,176]{1,2,0:T(8,128)(2,1)S(1)} async-done(((bf16[16,128,176]{1,2,0:T(8,128)(2,1)}), bf16[16,128,176]{1,2,0:T(8,128)(2,1)S(1)}, u32[]{:S(2)}, u32[]{:S(2)}) %all-to-all-start.3) | async-done | bytes 720928 | tf_op jit(solution)/shard_map/all_to_all | solution.py:459
  732.5 6.4 all-to-all-start.4
  742.2 15.9 %all-to-all-done.4 = bf16[16,128,128]{2,1,0:T(8,128)(2,1)S(1)} async-done(((bf16[16,128,128]{2,1,0:T(8,128)(2,1)}), bf16[16,128,128]{2,1,0:T(8,128)(2,1)S(1)}, u32[]{:S(2)}, u32[]{:S(2)}) %all-to-all-start.4) | async-done | bytes 524320 | tf_op jit(solution)/shard_map/all_to_all | solution.py:459
  758.9 9.9 shard_map.257
  768.7 3.9 copy.244
  772.6 4.9 all-to-all-start.5
  781.2 23.5 %collective-permute-done.15 = bf16[128,4096]{1,0:T(8,128)(2,1)} collective-permute-done((bf16[128,4096]{1,0:T(8,128)(2,1)}, bf16[128,4096]{1,0:T(8,128)(2,1)}, u32[]{:S(2)}, u32[]{:S(2)}) %collective-permute-start.15) | collective-permute-done | bytes 1048608 | tf_op jit(solution)/shard_map/ppermute | solution.py:383
  808.0 28.4 %all-to-all-done.5 = bf16[16,128,512]{1,2,0:T(8,128)(2,1)} async-done(((bf16[16,128,512]{1,2,0:T(8,128)(2,1)}), bf16[16,128,512]{1,2,0:T(8,128)(2,1)}, u32[]{:S(2)}, u32[]{:S(2)}) %all-to-all-start.5) | async-done | bytes 2097184 | tf_op jit(solution)/shard_map/all_to_all | solution.py:459
  852.1 5.6 fusion.127
  857.9 6.0 fusion.128
  868.5 23.0 %collective-permute-done.21 = bf16[528,1024]{1,0:T(8,128)(2,1)} collective-permute-done((bf16[528,1024]{1,0:T(8,128)(2,1)}, bf16[528,1024]{1,0:T(8,128)(2,1)}, u32[]{:S(2)}, u32[]{:S(2)}) %collective-permute-start.21) | collective-permute-done | bytes 1081376 | tf_op jit(solution)/shard_map/ppermute | solution.py:386
  894.1 3.8 constant_dynamic-slice_fusion.5
  899.1 67.5 %collective-permute-done.13 = bf16[512,3072]{1,0:T(8,128)(2,1)} collective-permute-done((bf16[512,3072]{1,0:T(8,128)(2,1)}, bf16[512,3072]{1,0:T(8,128)(2,1)}, u32[]{:S(2)}, u32[]{:S(2)}) %collective-permute-start.13) | collective-permute-done | bytes 3145760 | tf_op jit(solution)/shard_map/ppermute | solution.py:383
  969.7 10.5 all-to-all-start.6
  980.4 4.0 fusion.32
  987.0 5.2 fusion.34
  993.7 8.9 all-to-all-done.6
  1002.6 5.8 fusion.126
  1017.2 11.0 collective-permute-done.17
  1031.7 4.1 fusion.124
  1036.8 5.8 convolution_dynamic-update-slice_fusion.1
  1044.8 4.0 fusion.125
  1064.9 3.8 constant_dynamic-slice_fusion.6
  1070.7 178.7 %collective-permute-done.11 = bf16[704,2048]{1,0:T(8,128)(2,1)} collective-permute-done((bf16[704,2048]{1,0:T(8,128)(2,1)}, bf16[704,2048]{1,0:T(8,128)(2,1)}, u32[]{:S(2)}, u32[]{:S(2)}) %collective-permute-start.11) | collective-permute-done | bytes 2883616 | tf_op jit(solution)/shard_map/ppermute | solution.py:383
  1249.5 7.6 collective-permute-start.12
  1257.1 54.2 %collective-permute-done.23 = bf16[704,2048]{1,0:T(8,128)(2,1)} collective-permute-done((bf16[704,2048]{1,0:T(8,128)(2,1)}, bf16[704,2048]{1,0:T(8,128)(2,1)}, u32[]{:S(2)}, u32[]{:S(2)}) %collective-permute-start.23) | collective-permute-done | bytes 2883616 | tf_op jit(solution)/shard_map/ppermute | solution.py:386
  1311.3 9.7 add_bitcast_fusion.1
  1321.0 12.9 add_bitcast_fusion
  1337.6 3.4 convolution_add_fusion.1
  1345.4 3.6 fusion.7
  1350.2 17.3 %shard_map.259 = f32[1024,5632]{1,0:T(8,128)} custom-call(bf16[16,528,1024]{2,1,0:T(8,128)(2,1)} %bitcast.200), custom_call_target="tpu_custom_call" | custom-call | bytes 34603008 | tf_op jit(solution)/shard_map/pallas_call | solution.py:273
  1367.5 11.7 shard_map.260
  1380.2 15.8 %shard_map.258 = (f32[1024,2048]{1,0:T(8,128)}, f32[1024,3072]{1,0:T(8,128)}, f32[256,4096]{1,0:T(8,128)}, f32[576,1024]{1,0:T(8,128)}) custom-call(bf16[16,1152,384]{2,1,0:T(8,128)(2,1)} %bitcast.203, bf16[16,1152,384]{2,1,0:T(8,128)(2,1)} %bitcast.204), custom_call_target="tpu_custom_call" | custom-call | bytes 42467328 | tf_op jit(solution)/shard_map/pallas_call | solution.py:326
  (409 shorter events, 178.1 us)
Async XLA Ops:
  7.2 86.2 %copy-start.62 = (f32[2,1,64,6]{2,1,3,0:T(1,128)S(1)}, f32[2,1,64,6]{2,1,3,0:T(1,128)}, u32[]{:S(2)}) copy-start(f32[2,1,64,6]{2,1,3,0:T(1,128)} %param.20) | copy-start | bytes 9220
  7.2 86.3 %copy-start.63 = (s32[2,1,64,6]{2,1,3,0:T(1,128)S(1)}, s32[2,1,64,6]{2,1,3,0:T(1,128)}, u32[]{:S(2)}) copy-start(s32[2,1,64,6]{2,1,3,0:T(1,128)} %param.19) | copy-start | bytes 9220
  7.2 93.3 %copy-start.33 = (bf16[1024,576]{0,1:T(8,128)(2,1)S(1)}, bf16[1024,576]{0,1:T(8,128)(2,1)}, u32[]{:S(2)}) copy-start(bf16[1024,576]{0,1:T(8,128)(2,1)} %param.23) | copy-start | bytes 3538948
  7.2 86.1 %all-gather.10.cloned.1.call-start = ((), (), s32[]{:S(2)}) async-start(), calls=%async_computation.8 | async-start | bytes 8912896 | tf_op jit(solution)/shard_map/all_gather | solution.py:453
  9.7 3.5 collective-permute-start
  13.2 84.5 %copy-start.64 = (f32[128]{0:T(128)}, f32[128]{0:T(128)S(1)}, u32[]{:S(2)}) copy-start(f32[128]{0:T(128)S(1)} %rsqrt.38) | copy-start | bytes 1540
  16.3 428.2 %all-gather.14.cloned.1.call-start = ((), (), s32[]{:S(2)}) async-start(), calls=%async_computation.10 | async-start | bytes 8912896 | tf_op jit(solution)/shard_map/all_gather | solution.py:453
  94.2 33.7 %all-to-all-start = ((f32[16,1,128]{2,1,0:T(1,128)}), f32[16,1,128]{2,1,0:T(1,128)S(1)}, u32[]{:S(2)}, u32[]{:S(2)}) async-start(f32[16,1,128]{2,1,0:T(1,128)} %bitcast.2), calls=%async_computation | async-start | bytes 16384 | tf_op jit(solution)/shard_map/all_to_all | solution.py:459
  99.3 30.8 %collective-permute-start.1 = (bf16[1024,192]{0,1:T(8,128)(2,1)S(1)}, bf16[1024,192]{0,1:T(8,128)(2,1)S(1)}, u32[]{:S(2)}, u32[]{:S(2)}) collective-permute-start(bf16[1024,192]{0,1:T(8,128)(2,1)S(1)} %copy.269), channel_id=1, source_target_pairs={{16,0},{0,16},{17,1},{1,17},{18,2},{2,18},{19,3},{3,19},{20,4},{4,... | collective-permute-start | bytes 1179656 | tf_op jit(solution)/shard_map/ppermute | solution.py:383
  100.6 21.9 %collective-permute-start.2 = (bf16[512,576]{0,1:T(8,128)(2,1)S(1)}, bf16[512,576]{0,1:T(8,128)(2,1)}, u32[]{:S(2)}, u32[]{:S(2)}) collective-permute-start(bf16[512,576]{0,1:T(8,128)(2,1)S(1)} %constant_dynamic-slice_fusion.15), channel_id=1, source_target_pairs={{16,0},{0,16},{17,1},{1,17},{18,2},{2,18},{19,3},{3,19},{20,4},{4,... | collective-permute-start | bytes 1769480 | tf_op jit(solution)/shard_map/ppermute | solution.py:383
  102.5 23.6 %copy-start.34 = (bf16[1024,576]{0,1:T(8,128)(2,1)S(1)}, bf16[1024,576]{0,1:T(8,128)(2,1)}, u32[]{:S(2)}) copy-start(bf16[1024,576]{0,1:T(8,128)(2,1)} %param.23) | copy-start | bytes 3538948
  102.5 26.6 %collective-permute-start.4 = (bf16[256,256]{1,0:T(8,128)(2,1)}, bf16[256,256]{1,0:T(8,128)(2,1)}, u32[]{:S(2)}, u32[]{:S(2)}) collective-permute-start(bf16[256,256]{1,0:T(8,128)(2,1)} %get-tuple-element.152), channel_id=1, source_target_pairs={{16,0},{0,16},{17,1},{1,17},{18,2},{2,18},{19,3},{3,19},{20,4},{4,... | collective-permute-start | bytes 393224 | tf_op jit(solution)/shard_map/ppermute | solution.py:383
  106.9 19.6 %copy-start.56 = (s32[2,1,1024]{2,1,0:T(1,128)S(1)}, s32[2,1,1024]{2,1,0:T(1,128)}, u32[]{:S(2)}) copy-start(s32[2,1,1024]{2,1,0:T(1,128)} %seg_row.3) | copy-start | bytes 24580
  106.9 63.4 %collective-permute-start.5 = (bf16[512,2048]{1,0:T(8,128)(2,1)}, bf16[512,2048]{1,0:T(8,128)(2,1)}, u32[]{:S(2)}, u32[]{:S(2)}) collective-permute-start(bf16[512,2048]{1,0:T(8,128)(2,1)} %constant_dynamic-slice_fusion.13), channel_id=1, source_target_pairs={{16,0},{0,16},{17,1},{1,17},{18,2},{2,18},{19,3},{3,19},{20,4},{4,... | collective-permute-start | bytes 6291464 | tf_op jit(solution)/shard_map/ppermute | solution.py:383
  107.4 20.5 %copy-start.68 = (f32[32]{0:T(128)}, f32[32]{0:T(128)S(1)}, u32[]{:S(2)}) copy-start(f32[32]{0:T(128)S(1)} %multiply_power_fusion) | copy-start | bytes 388
  122.5 15.7 %collective-permute-start.3 = (bf16[512,576]{0,1:T(8,128)(2,1)}, bf16[512,576]{0,1:T(8,128)(2,1)}, u32[]{:S(2)}, u32[]{:S(2)}) collective-permute-start(bf16[512,576]{0,1:T(8,128)(2,1)} %collective-permute-done.2), channel_id=1, source_target_pairs={{0,1},{1,0},{2,3},{3,2},{4,5},{5,4},{6,7},{7,6},{8,9},{9,8},{10,11... | collective-permute-start | bytes 1769480 | tf_op jit(solution)/shard_map/ppermute | solution.py:433
  127.9 60.7 %copy-start.54 = (f32[1,2,2,128]{3,1,2,0:T(2,128)}, f32[1,2,2,128]{3,1,2,0:T(2,128)S(1)}, u32[]{:S(2)}) copy-start(f32[1,2,2,128]{3,1,2,0:T(2,128)S(1)} %copy.281) | copy-start | bytes 6148
  151.5 33.2 %copy-start.36 = (f32[16,64,128]{2,1,0:T(8,128)S(1)}, f32[16,64,128]{2,1,0:T(8,128)}, u32[]{:S(2)}) copy-start(f32[16,64,128]{2,1,0:T(8,128)} %get-tuple-element.190) | copy-start | bytes 1572868
  151.5 33.2 %copy-start.37 = (f32[16,64,128]{2,1,0:T(8,128)S(1)}, f32[16,64,128]{2,1,0:T(8,128)}, u32[]{:S(2)}) copy-start(f32[16,64,128]{2,1,0:T(8,128)} %get-tuple-element.191) | copy-start | bytes 1572868
  170.3 55.0 %collective-permute-start.6 = (bf16[512,2048]{1,0:T(8,128)(2,1)}, bf16[512,2048]{1,0:T(8,128)(2,1)S(1)}, u32[]{:S(2)}, u32[]{:S(2)}) collective-permute-start(bf16[512,2048]{1,0:T(8,128)(2,1)} %collective-permute-done.5), channel_id=1, source_target_pairs={{0,1},{1,0},{2,3},{3,2},{4,5},{5,4},{6,7},{7,6},{8,9},{9,8},{10,11... | collective-permute-start | bytes 6291464 | tf_op jit(solution)/shard_map/ppermute | solution.py:433
  200.3 19.7 %all-to-all-start.1 = ((bf16[16,128,128]{1,2,0:T(8,128)(2,1)}), bf16[16,128,128]{1,2,0:T(8,128)(2,1)S(1)}, u32[]{:S(2)}, u32[]{:S(2)}) async-start(bf16[16,128,128]{1,2,0:T(8,128)(2,1)} %copy.226), calls=%async_computation.1 | async-start | bytes 1048576 | tf_op jit(solution)/shard_map/all_to_all | solution.py:459
  206.0 245.7 %all-gather.12.cloned.1.call-start = ((), (), s32[]{:S(2)}) async-start(), calls=%async_computation.9 | async-start | bytes 8912896 | tf_op jit(solution)/shard_map/all_gather | solution.py:453
  206.1 19.8 %copy-start.47 = (f32[1,8,2,128]{3,1,2,0:T(8,128)}, f32[1,8,2,128]{3,1,2,0:T(8,128)S(1)}, u32[]{:S(2)}) copy-start(f32[1,8,2,128]{3,1,2,0:T(8,128)S(1)} %copy.289) | copy-start | bytes 24580
  228.2 488.0 %reduce-scatter.2.cloned.1.call-start = ((), (), s32[]{:S(2)}) async-start(), calls=%async_computation.11 | async-start | bytes 8912896 | tf_op jit(solution)/shard_map/reduce_scatter | solution.py:462
  228.2 228.2 %collective-permute-start.7 = (bf16[1024,2816]{1,0:T(8,128)(2,1)}, bf16[1024,2816]{1,0:T(8,128)(2,1)}, u32[]{:S(2)}, u32[]{:S(2)}) collective-permute-start(bf16[1024,2816]{1,0:T(8,128)(2,1)} %bitcast.274), channel_id=1, source_target_pairs={{16,0},{0,16},{17,1},{1,17},{18,2},{2,18},{19,3},{3,19},{20,4},{4,... | collective-permute-start | bytes 17301512 | tf_op jit(solution)/shard_map/ppermute | solution.py:383
  229.5 211.3 %collective-permute-start.8 = (bf16[704,2048]{1,0:T(8,128)(2,1)}, bf16[704,2048]{1,0:T(8,128)(2,1)}, u32[]{:S(2)}, u32[]{:S(2)}) collective-permute-start(bf16[704,2048]{1,0:T(8,128)(2,1)} %bitcast.236), channel_id=1, source_target_pairs={{16,0},{0,16},{17,1},{1,17},{18,2},{2,18},{19,3},{3,19},{20,4},{4,... | collective-permute-start | bytes 8650760 | tf_op jit(solution)/shard_map/ppermute | solution.py:383
  233.2 274.0 %collective-permute-start.10 = (bf16[352,1024]{1,0:T(8,128)(2,1)}, bf16[352,1024]{1,0:T(8,128)(2,1)}, u32[]{:S(2)}, u32[]{:S(2)}) collective-permute-start(bf16[352,1024]{1,0:T(8,128)(2,1)} %pad_maximum_fusion.10.refs_0_), channel_id=1, source_target_pairs={{16,0},{0,16},{17,1},{1,17},{18,2},{2,18},{19,3},{3,19},{20,4},{4,... | collective-permute-start | bytes 2162696 | tf_op jit(solution)/shard_map/ppermute | solution.py:383
  237.4 201.6 %collective-permute-start.9 = (bf16[88,2048]{1,0:T(8,128)(2,1)}, bf16[88,2048]{1,0:T(8,128)(2,1)}, u32[]{:S(2)}, u32[]{:S(2)}) collective-permute-start(bf16[88,2048]{1,0:T(8,128)(2,1)} %get-tuple-element.150), channel_id=1, source_target_pairs={{16,0},{0,16},{17,1},{1,17},{18,2},{2,18},{19,3},{3,19},{20,4},{4,... | collective-permute-start | bytes 1081352 | tf_op jit(solution)/shard_map/ppermute | solution.py:383
  456.4 17.6 %copy-start.14 = (bf16[32,32,2048]{2,1,0:T(8,128)(2,1)}, bf16[32,32,2048]{2,1,0:T(8,128)(2,1)S(1)}, u32[]{:S(2)}) copy-start(bf16[32,32,2048]{2,1,0:T(8,128)(2,1)S(1)} %convolution_convert_fusion.1) | copy-start | bytes 12582916
  481.8 32.8 %slice-start = ((s8[8388608]{0:T(1024)(128)(4,1)}), s8[4194304]{0:T(1024)(128)(4,1)S(1)}, s32[]{:S(2)}) async-start(s8[8388608]{0:T(1024)(128)(4,1)} %bitcast.198), calls=%async_computation.16 | async-start | bytes 8388608
  492.7 21.8 %slice-start.1 = ((s8[8388608]{0:T(1024)(128)(4,1)}), s8[4194304]{0:T(1024)(128)(4,1)S(1)}, s32[]{:S(2)}) async-start(s8[8388608]{0:T(1024)(128)(4,1)} %bitcast.198), calls=%async_computation.17 | async-start | bytes 8388608
  519.1 148.4 %copy-start.18 = (bf16[2048,176]{1,0:T(8,128)(2,1)}, bf16[2048,176]{1,0:T(8,128)(2,1)S(1)}, u32[]{:S(2)}) copy-start(bf16[2048,176]{1,0:T(8,128)(2,1)S(1)} %get-tuple-element.43) | copy-start | bytes 2162692
  550.0 117.4 %all-to-all-start.2 = ((bf16[16,64,2048]{2,1,0:T(8,128)(2,1)}), bf16[16,64,2048]{2,1,0:T(8,128)(2,1)}, u32[]{:S(2)}, u32[]{:S(2)}) async-start(bf16[16,64,2048]{2,1,0:T(8,128)(2,1)} %bitcast.230), calls=%async_computation.2 | async-start | bytes 8388608 | tf_op jit(solution)/shard_map/all_to_all | solution.py:459
  555.6 447.0 %all-gather.16.cloned.1.call-start = ((), (), s32[]{:S(2)}) async-start(), calls=%async_computation.12 | async-start | bytes 8912896 | tf_op jit(solution)/shard_map/all_gather | solution.py:453
  668.7 46.6 %all-to-all-start.3 = ((bf16[16,128,176]{1,2,0:T(8,128)(2,1)}), bf16[16,128,176]{1,2,0:T(8,128)(2,1)S(1)}, u32[]{:S(2)}, u32[]{:S(2)}) async-start(bf16[16,128,176]{1,2,0:T(8,128)(2,1)} %copy.241), calls=%async_computation.3 | async-start | bytes 1441792 | tf_op jit(solution)/shard_map/all_to_all | solution.py:459
  687.8 28.3 %copy-start.1 = (f32[128,2048]{1,0:T(8,128)S(1)}, f32[128,2048]{1,0:T(8,128)}, u32[]{:S(2)}) copy-start(f32[128,2048]{1,0:T(8,128)} %copy-done) | copy-start | bytes 3145732
  687.8 28.3 %copy-start.48 = (f32[1,8,2,128]{3,1,2,0:T(8,128)S(1)}, f32[1,8,2,128]{3,1,2,0:T(8,128)}, u32[]{:S(2)}) copy-start(f32[1,8,2,128]{3,1,2,0:T(8,128)} %copy-done.47) | copy-start | bytes 24580
  687.9 28.3 %copy-start.60 = (f32[128]{0:T(128)S(1)}, f32[128]{0:T(128)}, u32[]{:S(2)}) copy-start(f32[128]{0:T(128)} %copy-done.59) | copy-start | bytes 1540
  687.9 29.9 %copy-start.22 = (bf16[2,1,64,2048]{3,2,1,0:T(8,128)(2,1)S(1)}, bf16[2,1,64,2048]{3,2,1,0:T(8,128)(2,1)}, u32[]{:S(2)}) copy-start(bf16[2,1,64,2048]{3,2,1,0:T(8,128)(2,1)} %param.17) | copy-start | bytes 1572868
  724.4 14.6 %copy-start.69 = (f32[32]{0:T(128)S(1)}, f32[32]{0:T(128)}, u32[]{:S(2)}) copy-start(f32[32]{0:T(128)} %copy-done.68) | copy-start | bytes 388
  732.5 25.5 %all-to-all-start.4 = ((bf16[16,128,128]{2,1,0:T(8,128)(2,1)}), bf16[16,128,128]{2,1,0:T(8,128)(2,1)S(1)}, u32[]{:S(2)}, u32[]{:S(2)}) async-start(bf16[16,128,128]{2,1,0:T(8,128)(2,1)} %bitcast_bitcast_fusion.1), calls=%async_computation.5 | async-start | bytes 1048576 | tf_op jit(solution)/shard_map/all_to_all | solution.py:459
  772.6 63.8 %all-to-all-start.5 = ((bf16[16,128,512]{1,2,0:T(8,128)(2,1)}), bf16[16,128,512]{1,2,0:T(8,128)(2,1)}, u32[]{:S(2)}, u32[]{:S(2)}) async-start(bf16[16,128,512]{1,2,0:T(8,128)(2,1)} %copy.244), calls=%async_computation.6 | async-start | bytes 4194304 | tf_op jit(solution)/shard_map/all_to_all | solution.py:459
  777.5 277.7 %all-gather.18.cloned.1.call-start = ((), (), s32[]{:S(2)}) async-start(), calls=%async_computation.13 | async-start | bytes 3133440 | tf_op jit(solution)/shard_map/all_gather | solution.py:453
  779.9 24.9 %collective-permute-start.15 = (bf16[128,4096]{1,0:T(8,128)(2,1)}, bf16[128,4096]{1,0:T(8,128)(2,1)}, u32[]{:S(2)}, u32[]{:S(2)}) collective-permute-start(bf16[128,4096]{1,0:T(8,128)(2,1)} %constant_dynamic-slice_fusion.4), channel_id=1, source_target_pairs={{16,0},{0,16},{17,1},{1,17},{18,2},{2,18},{19,3},{3,19},{20,4},{4,... | collective-permute-start | bytes 3145736 | tf_op jit(solution)/shard_map/ppermute | solution.py:383
  804.7 38.5 %collective-permute-start.16 = (bf16[128,4096]{1,0:T(8,128)(2,1)}, bf16[128,4096]{1,0:T(8,128)(2,1)}, u32[]{:S(2)}, u32[]{:S(2)}) collective-permute-start(bf16[128,4096]{1,0:T(8,128)(2,1)} %collective-permute-done.15), channel_id=1, source_target_pairs={{0,1},{1,0},{2,3},{3,2},{4,5},{5,4},{6,7},{7,6},{8,9},{9,8},{10,11... | collective-permute-start | bytes 3145736 | tf_op jit(solution)/shard_map/ppermute | solution.py:433
  852.0 498.1 %all-gather.22.cloned.1.call-start = ((), (), s32[]{:S(2)}) async-start(), calls=%async_computation.15 | async-start | bytes 18382848 | tf_op jit(solution)/shard_map/all_gather | solution.py:456
  865.1 26.4 %slice-start.4 = ((f32[352,2048]{1,0:T(8,128)}), f32[352,1024]{1,0:T(8,128)S(1)}, s32[]{:S(2)}) async-start(f32[352,2048]{1,0:T(8,128)} %copy-done.16), calls=%async_computation.20 | async-start | bytes 2883584 | tf_op jit(solution)/shard_map/slice | solution.py:608
  866.2 25.3 %collective-permute-start.21 = (bf16[528,1024]{1,0:T(8,128)(2,1)}, bf16[528,1024]{1,0:T(8,128)(2,1)}, u32[]{:S(2)}, u32[]{:S(2)}) collective-permute-start(bf16[528,1024]{1,0:T(8,128)(2,1)} %pad_maximum_fusion.7), channel_id=1, source_target_pairs={{0,16},{16,0},{1,17},{17,1},{2,18},{18,2},{3,19},{19,3},{4,20},{20... | collective-permute-start | bytes 3244040 | tf_op jit(solution)/shard_map/ppermute | solution.py:386
  894.1 86.3 %copy-start.58 = (f32[2048]{0:T(1024)S(1)}, f32[2048]{0:T(1024)}, u32[]{:S(2)}) copy-start(f32[2048]{0:T(1024)} %copy-done.57) | copy-start | bytes 24580
  897.9 68.7 %collective-permute-start.13 = (bf16[512,3072]{1,0:T(8,128)(2,1)}, bf16[512,3072]{1,0:T(8,128)(2,1)}, u32[]{:S(2)}, u32[]{:S(2)}) collective-permute-start(bf16[512,3072]{1,0:T(8,128)(2,1)} %constant_dynamic-slice_fusion.5), channel_id=1, source_target_pairs={{16,0},{0,16},{17,1},{1,17},{18,2},{2,18},{19,3},{3,19},{20,4},{4,... | collective-permute-start | bytes 9437192 | tf_op jit(solution)/shard_map/ppermute | solution.py:383
  966.6 78.1 %collective-permute-start.14 = (bf16[512,3072]{1,0:T(8,128)(2,1)}, bf16[512,3072]{1,0:T(8,128)(2,1)}, u32[]{:S(2)}, u32[]{:S(2)}) collective-permute-start(bf16[512,3072]{1,0:T(8,128)(2,1)} %collective-permute-done.13), channel_id=1, source_target_pairs={{0,1},{1,0},{2,3},{3,2},{4,5},{5,4},{6,7},{7,6},{8,9},{9,8},{10,11... | collective-permute-start | bytes 9437192 | tf_op jit(solution)/shard_map/ppermute | solution.py:433
  969.7 32.9 %all-to-all-start.6 = ((bf16[16,128,128]{2,1,0:T(8,128)(2,1)}), bf16[16,128,128]{2,1,0:T(8,128)(2,1)}, u32[]{:S(2)}, u32[]{:S(2)}) async-start(bf16[16,128,128]{2,1,0:T(8,128)(2,1)} %bitcast_bitcast_fusion), calls=%async_computation.7 | async-start | bytes 1048576 | tf_op jit(solution)/shard_map/all_to_all | solution.py:459
  980.1 399.1 %all-gather.20.cloned.1.call-start = ((), (), s32[]{:S(2)}) async-start(), calls=%async_computation.14 | async-start | bytes 15040512 | tf_op jit(solution)/shard_map/all_gather | solution.py:456
  1009.6 18.6 %collective-permute-start.17 = (bf16[1024,384]{1,0:T(8,128)(2,1)}, bf16[1024,384]{1,0:T(8,128)(2,1)}, u32[]{:S(2)}, u32[]{:S(2)}) collective-permute-start(bf16[1024,384]{1,0:T(8,128)(2,1)} %pad_maximum_fusion.9), channel_id=1, source_target_pairs={{0,16},{16,0},{1,17},{17,1},{2,18},{18,2},{3,19},{19,3},{4,20},{20... | collective-permute-start | bytes 2359304 | tf_op jit(solution)/shard_map/ppermute | solution.py:386
  1053.9 6.5 collective-permute-start.19
  1060.1 3.4 collective-permute-start.18
  1064.6 256.3 %collective-permute-start.22 = (bf16[1024,2816]{1,0:T(8,128)(2,1)}, bf16[1024,2816]{1,0:T(8,128)(2,1)}, u32[]{:S(2)}, u32[]{:S(2)}) collective-permute-start(bf16[1024,2816]{1,0:T(8,128)(2,1)} %convolution_convert_fusion), channel_id=1, source_target_pairs={{0,16},{16,0},{1,17},{17,1},{2,18},{18,2},{3,19},{19,3},{4,20},{20... | collective-permute-start | bytes 17301512 | tf_op jit(solution)/shard_map/ppermute | solution.py:386
  1068.7 180.8 %collective-permute-start.11 = (bf16[704,2048]{1,0:T(8,128)(2,1)}, bf16[704,2048]{1,0:T(8,128)(2,1)}, u32[]{:S(2)}, u32[]{:S(2)}) collective-permute-start(bf16[704,2048]{1,0:T(8,128)(2,1)} %constant_dynamic-slice_fusion.6), channel_id=1, source_target_pairs={{16,0},{0,16},{17,1},{1,17},{18,2},{2,18},{19,3},{3,19},{20,4},{4,... | collective-permute-start | bytes 8650760 | tf_op jit(solution)/shard_map/ppermute | solution.py:383
  1069.9 241.4 %collective-permute-start.23 = (bf16[704,2048]{1,0:T(8,128)(2,1)}, bf16[704,2048]{1,0:T(8,128)(2,1)}, u32[]{:S(2)}, u32[]{:S(2)}) collective-permute-start(bf16[704,2048]{1,0:T(8,128)(2,1)} %convolution_convert_fusion.2), channel_id=1, source_target_pairs={{0,16},{16,0},{1,17},{17,1},{2,18},{18,2},{3,19},{19,3},{4,20},{20... | collective-permute-start | bytes 8650760 | tf_op jit(solution)/shard_map/ppermute | solution.py:386
  1070.7 250.2 %copy-start.15 = (bf16[32,32,2048]{2,1,0:T(8,128)(2,1)S(1)}, bf16[32,32,2048]{2,1,0:T(8,128)(2,1)}, u32[]{:S(2)}) copy-start(bf16[32,32,2048]{2,1,0:T(8,128)(2,1)} %copy-done.14) | copy-start | bytes 12582916
  1249.5 96.0 %collective-permute-start.12 = (bf16[704,2048]{1,0:T(8,128)(2,1)}, bf16[704,2048]{1,0:T(8,128)(2,1)}, u32[]{:S(2)}, u32[]{:S(2)}) collective-permute-start(bf16[704,2048]{1,0:T(8,128)(2,1)} %collective-permute-done.11), channel_id=1, source_target_pairs={{0,1},{1,0},{2,3},{3,2},{4,5},{5,4},{6,7},{7,6},{8,9},{9,8},{10,11... | collective-permute-start | bytes 8650760 | tf_op jit(solution)/shard_map/ppermute | solution.py:433
  1311.2 25.3 %slice-start.2 = ((s8[5767168]{0:T(1024)(128)(4,1)}), s8[4194304]{0:T(1024)(128)(4,1)S(1)}, s32[]{:S(2)}) async-start(s8[5767168]{0:T(1024)(128)(4,1)} %bitcast.210), calls=%async_computation.18 | async-start | bytes 8388608
  1320.9 15.6 %slice-start.3 = ((s8[5767168]{0:T(1024)(128)(4,1)}), s8[1572864]{0:T(1024)(128)(4,1)S(1)}, s32[]{:S(2)}) async-start(s8[5767168]{0:T(1024)(128)(4,1)} %bitcast.210), calls=%async_computation.19 | async-start | bytes 3145728
  1345.2 3.8 collective-permute-start.20
  (51 other events, 243.5 us)
Sparse Core Ops, SparseCore 0:
  16.4 76.8 all-gather.9
  95.5 72.8 all-gather.13
  228.3 73.8 all-gather.11
  550.2 164.8 reduce-scatter.1
  717.0 118.1 all-gather.15
  852.2 49.9 all-gather.17
  904.3 98.4 all-gather.21
  1064.7 109.5 all-gather.19

commit v2 on v1

--- a/solution.py
+++ b/solution.py
@@ -583,9 +583,7 @@
     weo = lay_out(w_expert_out[0], weo_others)
     epre = dot(arrived, wei)
     eact = swiglu(epre).astype(bf16)
-    gated = (gate_slots * dot(eact, weo)).astype(bf16)
-    returned = swap(gated.reshape(groups, micro * capacity, width))
-    deact = dot_nt(after(dyexp, gated), weo)
+    deact = dot_nt(dyexp, weo)
     depre = swiglu_back(epre, deact).astype(bf16)
     dhid_rows = dot_nt(depre, wei).astype(bf16)
 
@@ -599,6 +597,10 @@
     arrived, depre, eact, dyexp, dspre, sact = lax.optimization_barrier(
         (arrived, depre, eact, dyexp, dspre, sact, dhid_part)
     )[:6]
+    hidden = swap(sact.reshape(groups, own, -1))
+    gated = (gate_slots * dot(eact, weo)).astype(bf16)
+    returned = swap(after(gated, hidden).reshape(groups, micro * capacity, width))
+    dspre, sact = lax.optimization_barrier((dspre, sact, gated))[:2]
     g_si = dot_tn(dspre, hid_all)
     g_so = dot_tn(sact, dy_all)
 
@@ -621,7 +623,6 @@
 
     sent_in = [expert_in_grad(r).astype(bf16) for r in range(1, parts)]
     sent_out = [expert_out_grad(r).astype(bf16) for r in range(1, parts)]
-    hidden = swap(after(sact, returned).reshape(groups, own, -1))
     dhid_sum = after(dhid_sum, returned, hidden, *sent_in, *sent_out)
     got_in = [send(x, r).astype(f32) for r, x in enumerate(sent_in, 1)]
     got_out = [send(x, r).astype(f32) for r, x in enumerate(sent_out, 1)]

time: 1420 us -> 1420 us (level)
  starting transfers between devices: 86.9 us -> 72.2 us
    reduce_scatter x1, waiting for transfers between devices: 0.01 us -> 32.3 us  [collect(): return lax.psum_scatter(x, 'expert', scatter_dimension=0, tiled=True)]
    all_to_all x7, waiting for transfers between devices: 182 us -> 162 us  [swap(): return lax.all_to_all(x, 'expert', split_axis=0, concat_axis=0, tiled=True)]
    all_to_all x7, starting transfers between devices: 55.7 us -> 41.5 us  [swap(): return lax.all_to_all(x, 'expert', split_axis=0, concat_axis=0, tiled=True)]
  transfers between devices with their start and end apart: 39 -> 39, of which waited for: 17 -> 18; matrix products, arithmetic and copies ran while one was open for 24% -> 23% of each run, Pallas kernels for 3% -> 3%
where the time goes in v2:
time: 1420 us; the launch traced here: 1400 us
  waiting for transfers between devices  854 us (60%)
  matrix products  213 us (15%)
  local copies, waits for them, and re-layouts  109 us (8%)
  Pallas kernels  73.8 us (5%)
  starting transfers between devices  72.2 us (5%)
  other arithmetic  62.3 us (4%)
  between operations  15.9 us (1%)
    ppermute x12, waiting for transfers between devices, shift(): lax.ppermute(x, 'dp', [((i + step) % parts, i) for i in range(parts)])  490 us
    all_to_all x7, waiting for transfers between devices, swap(): return lax.all_to_all(x, 'expert', split_axis=0, concat_axis=0, tiled=True)  162 us
    ppermute x7, waiting for transfers between devices, send(): lax.ppermute(x, 'dp', [(i, (i + step) % parts) for i in range(parts)])  91.2 us
    dot_general x14, matrix products, dot_nt(): lax.dot_general(left, right, (((1,), (1,)), ((), ())), preferred_element_...  77.6 us
    all_gather x5, waiting for transfers between devices, spread(): return lax.all_gather(x, 'expert', axis=0, tiled=True)  77 us
    dot_general x10, matrix products, dot_tn(): lax.dot_general(left, right, (((0,), (0,)), ((), ())), preferred_element_...  70.7 us
    dot_general x10, matrix products, dot(): return jnp.dot(left, right, preferred_element_type=f32)  58.1 us
    all_to_all x7, starting transfers between devices, swap(): return lax.all_to_all(x, 'expert', split_axis=0, concat_axis=0, tiled=True)  41.5 us
  transfers between devices with their start and end apart: 39, of which 18 were waited for; matrix products, arithmetic and copies ran while one was open for 23% of the time, Pallas kernels for 3%

profile of v2, /device:TPU:1, one launch (start us, length us, event | category | flops | bytes accessed | tf_op | source)
XLA Modules:
  0.0 1400.4 jit_solution(16587650007461254893)
XLA Ops:
  17.0 77.0 %all-gather.10.cloned.1.call-done = bf16[2048,2048]{1,0:T(8,128)(2,1)} async-done(((bf16[128,2048]{1,0:T(8,128)(2,1)}), bf16[2048,2048]{1,0:T(8,128)(2,1)}) %all-gather.10.cloned.1.call-update) | async-done | bytes 8388624 | tf_op jit(solution)/shard_map/all_gather | solution.py:453
  94.8 3.5 all-to-all-start
  103.8 3.2 constant_dynamic-slice_fusion.13
  109.3 13.8 collective-permute-done.2
  135.4 7.2 dynamic_update_slice.63
  142.6 7.6 dynamic_update_slice.64
  156.0 14.9 %collective-permute-done.5 = bf16[512,2048]{1,0:T(8,128)(2,1)} collective-permute-done((bf16[512,2048]{1,0:T(8,128)(2,1)}, bf16[512,2048]{1,0:T(8,128)(2,1)}, u32[]{:S(2)}, u32[]{:S(2)}) %collective-permute-start.5) | collective-permute-done | bytes 2097184 | tf_op jit(solution)/shard_map/ppermute | solution.py:383
  172.0 12.4 fusion.120
  191.0 8.1 shard_map.255
  201.1 5.7 all-to-all-start.1
  207.0 13.9 all-to-all-done.1
  220.9 3.1 fusion.62
  238.6 3.3 broadcast_in_dim.106
  248.4 191.5 %collective-permute-done.9 = bf16[88,2048]{1,0:T(8,128)(2,1)} collective-permute-done((bf16[88,2048]{1,0:T(8,128)(2,1)}, bf16[88,2048]{1,0:T(8,128)(2,1)}, u32[]{:S(2)}, u32[]{:S(2)}) %collective-permute-start.9) | collective-permute-done | bytes 360480 | tf_op jit(solution)/shard_map/ppermute | solution.py:383
  441.7 3.8 constant_dynamic-update-slice_fusion.3
  445.5 4.6 fusion.50
  452.7 8.0 fusion.14
  460.7 7.1 multiply_convert_fusion.7
  472.8 18.7 %fusion.2 = f32[1024,2816]{1,0:T(8,128)} fusion(bf16[1024,2048]{1,0:T(8,128)(2,1)S(1)} %bitcast.218, bf16[1024,2816]{1,0:T(8,128)(2,1)} %collective-permute-done.8, bf16[1024,2816]{1,0:T(8,128)(2,1)} %bitcast.275), kind=kOutput, calls=%fused_computation.6 | convolution fusion | flops 11834228736 | bytes 27262976 | tf_op jit(solution)/shard_map/dot_general | solution.py:76
  491.5 15.3 %multiply_convert_fusion.3 = (bf16[1024,1408]{1,0:T(8,128)(2,1)}, bf16[1024,1408]{1,0:T(8,128)(2,1)}, bf16[1024,1408]{1,0:T(8,128)(2,1)}) fusion(f32[1024,2816]{1,0:T(8,128)} %fusion.2, bf16[1024,2048]{1,0:T(8,128)(2,1)S(1)} %copy-done.6, bf16[1408,2048]{1,0:T(8,128)(2,1)} %constant_dynamic-update-slice_fusion.3), kind=kOutput, calls=%fused_computation.11 | convolution fusion | flops 5928648704 | bytes 30146560 | tf_op jit(solution)/shard_map/dot_general | solution.py:84
  506.8 18.2 %fusion.3.rows_ref = bf16[1024,2048]{1,0:T(8,128)(2,1)} fusion(bf16[1024,2816]{1,0:T(8,128)(2,1)} %collective-permute-done.8, bf16[1024,2816]{1,0:T(8,128)(2,1)} %bitcast.276, bf16[1024,1408]{1,0:T(8,128)(2,1)} %get-tuple-element.156, bf16[1024,1408]{1,0:T(8,128)(2,1)} %get-tuple-element.155), kind=kOutput, calls=%fused_computation.16 | convolution fusion | flops 11847860224 | bytes 21495808 | tf_op jit(solution)/shard_map/dot_general | solution.py:84
  525.0 10.9 shard_map.256
  535.9 5.6 pad_maximum_fusion.3
  542.8 5.9 all-to-all-start.2
  548.7 11.5 multiply_convert_fusion
  560.2 5.9 all-to-all-done.2
  566.9 5.2 all-to-all-start.3
  572.7 7.9 convolution_convert_fusion.2
  580.6 11.2 convolution_convert_fusion
  591.8 87.0 %all-to-all-done.3 = bf16[16,64,2048]{2,1,0:T(8,128)(2,1)} async-done(((bf16[16,64,2048]{2,1,0:T(8,128)(2,1)}), bf16[16,64,2048]{2,1,0:T(8,128)(2,1)}, u32[]{:S(2)}, u32[]{:S(2)}) %all-to-all-start.3) | async-done | bytes 4194336 | tf_op jit(solution)/shard_map/all_to_all | solution.py:459
  678.8 32.3 %reduce-scatter.2.cloned.1.call-done = bf16[128,2048]{1,0:T(8,128)(2,1)} async-done(((bf16[2048,2048]{1,0:T(8,128)(2,1)}), bf16[128,2048]{1,0:T(8,128)(2,1)}) %reduce-scatter.2.cloned.1.call-update) | async-done | bytes 524304 | tf_op jit(solution)/shard_map/reduce_scatter | solution.py:462
  727.5 4.8 all-to-all-start.4
  735.5 17.3 %all-to-all-done.4 = bf16[16,128,128]{2,1,0:T(8,128)(2,1)S(1)} async-done(((bf16[16,128,128]{2,1,0:T(8,128)(2,1)}), bf16[16,128,128]{2,1,0:T(8,128)(2,1)S(1)}, u32[]{:S(2)}, u32[]{:S(2)}) %all-to-all-start.4) | async-done | bytes 524320 | tf_op jit(solution)/shard_map/all_to_all | solution.py:459
  753.6 9.8 shard_map.257
  763.5 3.9 copy.244
  767.4 6.0 all-to-all-start.5
  777.0 23.6 %collective-permute-done.15 = bf16[128,4096]{1,0:T(8,128)(2,1)} collective-permute-done((bf16[128,4096]{1,0:T(8,128)(2,1)}, bf16[128,4096]{1,0:T(8,128)(2,1)}, u32[]{:S(2)}, u32[]{:S(2)}) %collective-permute-start.15) | collective-permute-done | bytes 1048608 | tf_op jit(solution)/shard_map/ppermute | solution.py:383
  803.9 28.9 %all-to-all-done.5 = bf16[16,128,512]{1,2,0:T(8,128)(2,1)} async-done(((bf16[16,128,512]{1,2,0:T(8,128)(2,1)}), bf16[16,128,512]{1,2,0:T(8,128)(2,1)}, u32[]{:S(2)}, u32[]{:S(2)}) %all-to-all-start.5) | async-done | bytes 2097184 | tf_op jit(solution)/shard_map/all_to_all | solution.py:459
  848.6 5.6 fusion.127
  854.4 6.0 fusion.128
  865.0 23.0 %collective-permute-done.21 = bf16[528,1024]{1,0:T(8,128)(2,1)} collective-permute-done((bf16[528,1024]{1,0:T(8,128)(2,1)}, bf16[528,1024]{1,0:T(8,128)(2,1)}, u32[]{:S(2)}, u32[]{:S(2)}) %collective-permute-start.21) | collective-permute-done | bytes 1081376 | tf_op jit(solution)/shard_map/ppermute | solution.py:386
  890.6 3.8 constant_dynamic-slice_fusion.5
  895.6 67.5 %collective-permute-done.13 = bf16[512,3072]{1,0:T(8,128)(2,1)} collective-permute-done((bf16[512,3072]{1,0:T(8,128)(2,1)}, bf16[512,3072]{1,0:T(8,128)(2,1)}, u32[]{:S(2)}, u32[]{:S(2)}) %collective-permute-start.13) | collective-permute-done | bytes 3145760 | tf_op jit(solution)/shard_map/ppermute | solution.py:383
  966.1 10.5 all-to-all-start.6
  976.9 3.9 fusion.32
  983.4 5.2 fusion.34
  990.1 9.0 all-to-all-done.6
  999.0 5.8 fusion.126
  1013.7 11.0 collective-permute-done.17
  1028.2 4.1 fusion.124
  1033.4 5.8 convolution_dynamic-update-slice_fusion.1
  1041.5 4.0 fusion.125
  1057.4 2.9 collective-permute-done.18
  1061.7 3.8 constant_dynamic-slice_fusion.6
  1067.5 178.9 %collective-permute-done.11 = bf16[704,2048]{1,0:T(8,128)(2,1)} collective-permute-done((bf16[704,2048]{1,0:T(8,128)(2,1)}, bf16[704,2048]{1,0:T(8,128)(2,1)}, u32[]{:S(2)}, u32[]{:S(2)}) %collective-permute-start.11) | collective-permute-done | bytes 2883616 | tf_op jit(solution)/shard_map/ppermute | solution.py:383
  1246.4 7.5 collective-permute-start.12
  1253.8 54.3 %collective-permute-done.23 = bf16[704,2048]{1,0:T(8,128)(2,1)} collective-permute-done((bf16[704,2048]{1,0:T(8,128)(2,1)}, bf16[704,2048]{1,0:T(8,128)(2,1)}, u32[]{:S(2)}, u32[]{:S(2)}) %collective-permute-start.23) | collective-permute-done | bytes 2883616 | tf_op jit(solution)/shard_map/ppermute | solution.py:386
  1308.2 9.7 add_bitcast_fusion.1
  1317.9 12.8 add_bitcast_fusion
  1334.4 3.4 convolution_add_fusion.1
  1342.2 3.6 fusion.7
  1346.9 17.3 %shard_map.259 = f32[1024,5632]{1,0:T(8,128)} custom-call(bf16[16,528,1024]{2,1,0:T(8,128)(2,1)} %bitcast.198), custom_call_target="tpu_custom_call" | custom-call | bytes 34603008 | tf_op jit(solution)/shard_map/pallas_call | solution.py:273
  1364.3 11.7 shard_map.260
  1376.9 15.8 %shard_map.258 = (f32[1024,2048]{1,0:T(8,128)}, f32[1024,3072]{1,0:T(8,128)}, f32[256,4096]{1,0:T(8,128)}, f32[576,1024]{1,0:T(8,128)}) custom-call(bf16[16,1152,384]{2,1,0:T(8,128)(2,1)} %bitcast.201, bf16[16,1152,384]{2,1,0:T(8,128)(2,1)} %bitcast.202), custom_call_target="tpu_custom_call" | custom-call | bytes 42467328 | tf_op jit(solution)/shard_map/pallas_call | solution.py:326
  (422 shorter events, 179.0 us)
Async XLA Ops:
  7.2 86.8 %copy-start.69 = (f32[2,1,64,6]{2,1,3,0:T(1,128)S(1)}, f32[2,1,64,6]{2,1,3,0:T(1,128)}, u32[]{:S(2)}) copy-start(f32[2,1,64,6]{2,1,3,0:T(1,128)} %param.20) | copy-start | bytes 9220
  7.2 86.9 %copy-start.70 = (s32[2,1,64,6]{2,1,3,0:T(1,128)S(1)}, s32[2,1,64,6]{2,1,3,0:T(1,128)}, u32[]{:S(2)}) copy-start(s32[2,1,64,6]{2,1,3,0:T(1,128)} %param.19) | copy-start | bytes 9220
  7.2 93.9 %copy-start.31 = (bf16[1024,576]{0,1:T(8,128)(2,1)S(1)}, bf16[1024,576]{0,1:T(8,128)(2,1)}, u32[]{:S(2)}) copy-start(bf16[1024,576]{0,1:T(8,128)(2,1)} %param.23) | copy-start | bytes 3538948
  7.2 86.7 %all-gather.10.cloned.1.call-start = ((), (), s32[]{:S(2)}) async-start(), calls=%async_computation.8 | async-start | bytes 8912896 | tf_op jit(solution)/shard_map/all_gather | solution.py:453
  9.7 3.5 collective-permute-start
  13.2 85.1 %copy-start.71 = (f32[128]{0:T(128)}, f32[128]{0:T(128)S(1)}, u32[]{:S(2)}) copy-start(f32[128]{0:T(128)S(1)} %rsqrt.38) | copy-start | bytes 1540
  13.3 80.6 %copy-start.58 = (bf16[2,2304]{1,0:T(2,128)(2,1)}, bf16[2,2304]{1,0:T(2,128)(2,1)S(1)}, u32[]{:S(2)}) copy-start(bf16[2,2304]{1,0:T(2,128)(2,1)S(1)} %dynamic_update_slice.61) | copy-start | bytes 27652
  16.9 428.5 %all-gather.14.cloned.1.call-start = ((), (), s32[]{:S(2)}) async-start(), calls=%async_computation.10 | async-start | bytes 8912896 | tf_op jit(solution)/shard_map/all_gather | solution.py:453
  94.8 35.7 %all-to-all-start = ((f32[16,1,128]{2,1,0:T(1,128)}), f32[16,1,128]{2,1,0:T(1,128)S(1)}, u32[]{:S(2)}, u32[]{:S(2)}) async-start(f32[16,1,128]{2,1,0:T(1,128)} %bitcast.2), calls=%async_computation | async-start | bytes 16384 | tf_op jit(solution)/shard_map/all_to_all | solution.py:459
  99.9 34.7 %collective-permute-start.1 = (bf16[1024,192]{0,1:T(8,128)(2,1)S(1)}, bf16[1024,192]{0,1:T(8,128)(2,1)S(1)}, u32[]{:S(2)}, u32[]{:S(2)}) collective-permute-start(bf16[1024,192]{0,1:T(8,128)(2,1)S(1)} %copy.269), channel_id=1, source_target_pairs={{16,0},{0,16},{17,1},{1,17},{18,2},{2,18},{19,3},{3,19},{20,4},{4,... | collective-permute-start | bytes 1179656 | tf_op jit(solution)/shard_map/ppermute | solution.py:383
  101.2 21.9 %collective-permute-start.2 = (bf16[512,576]{0,1:T(8,128)(2,1)S(1)}, bf16[512,576]{0,1:T(8,128)(2,1)}, u32[]{:S(2)}, u32[]{:S(2)}) collective-permute-start(bf16[512,576]{0,1:T(8,128)(2,1)S(1)} %constant_dynamic-slice_fusion.15), channel_id=1, source_target_pairs={{16,0},{0,16},{17,1},{1,17},{18,2},{2,18},{19,3},{3,19},{20,4},{4,... | collective-permute-start | bytes 1769480 | tf_op jit(solution)/shard_map/ppermute | solution.py:383
  102.5 24.3 %copy-start.32 = (bf16[1024,576]{0,1:T(8,128)(2,1)S(1)}, bf16[1024,576]{0,1:T(8,128)(2,1)}, u32[]{:S(2)}) copy-start(bf16[1024,576]{0,1:T(8,128)(2,1)} %param.23) | copy-start | bytes 3538948
  102.5 31.1 %collective-permute-start.4 = (bf16[256,256]{1,0:T(8,128)(2,1)S(1)}, bf16[256,256]{1,0:T(8,128)(2,1)}, u32[]{:S(2)}, u32[]{:S(2)}) collective-permute-start(bf16[256,256]{1,0:T(8,128)(2,1)S(1)} %get-tuple-element.154), channel_id=1, source_target_pairs={{16,0},{0,16},{17,1},{1,17},{18,2},{2,18},{19,3},{3,19},{20,4},{4,... | collective-permute-start | bytes 393224 | tf_op jit(solution)/shard_map/ppermute | solution.py:383
  106.9 20.2 %copy-start.61 = (s32[2,1,1024]{2,1,0:T(1,128)S(1)}, s32[2,1,1024]{2,1,0:T(1,128)}, u32[]{:S(2)}) copy-start(s32[2,1,1024]{2,1,0:T(1,128)} %seg_row.3) | copy-start | bytes 24580
  106.9 64.0 %collective-permute-start.5 = (bf16[512,2048]{1,0:T(8,128)(2,1)}, bf16[512,2048]{1,0:T(8,128)(2,1)}, u32[]{:S(2)}, u32[]{:S(2)}) collective-permute-start(bf16[512,2048]{1,0:T(8,128)(2,1)} %constant_dynamic-slice_fusion.13), channel_id=1, source_target_pairs={{16,0},{0,16},{17,1},{1,17},{18,2},{2,18},{19,3},{3,19},{20,4},{4,... | collective-permute-start | bytes 6291464 | tf_op jit(solution)/shard_map/ppermute | solution.py:383
  107.4 17.5 %copy-start.75 = (f32[32]{0:T(128)}, f32[32]{0:T(128)S(1)}, u32[]{:S(2)}) copy-start(f32[32]{0:T(128)S(1)} %multiply_power_fusion) | copy-start | bytes 388
  123.1 19.5 %collective-permute-start.3 = (bf16[512,576]{0,1:T(8,128)(2,1)}, bf16[512,576]{0,1:T(8,128)(2,1)}, u32[]{:S(2)}, u32[]{:S(2)}) collective-permute-start(bf16[512,576]{0,1:T(8,128)(2,1)} %collective-permute-done.2), channel_id=1, source_target_pairs={{0,1},{1,0},{2,3},{3,2},{4,5},{5,4},{6,7},{7,6},{8,9},{9,8},{10,11... | collective-permute-start | bytes 1769480 | tf_op jit(solution)/shard_map/ppermute | solution.py:433
  130.5 58.7 %copy-start.59 = (f32[1,2,2,128]{3,1,2,0:T(2,128)}, f32[1,2,2,128]{3,1,2,0:T(2,128)S(1)}, u32[]{:S(2)}) copy-start(f32[1,2,2,128]{3,1,2,0:T(2,128)S(1)} %copy.281) | copy-start | bytes 6148
  130.5 21.3 %copy-start.51 = (f32[16,1,128]{2,1,0:T(1,128)}, f32[16,1,128]{2,1,0:T(1,128)S(1)}, u32[]{:S(2)}) copy-start(f32[16,1,128]{2,1,0:T(1,128)S(1)} %all-to-all-done) | copy-start | bytes 24580
  156.0 29.4 %copy-start.34 = (f32[16,64,128]{2,1,0:T(8,128)S(1)}, f32[16,64,128]{2,1,0:T(8,128)}, u32[]{:S(2)}) copy-start(f32[16,64,128]{2,1,0:T(8,128)} %get-tuple-element.193) | copy-start | bytes 1572868
  156.0 29.4 %copy-start.35 = (f32[16,64,128]{2,1,0:T(8,128)S(1)}, f32[16,64,128]{2,1,0:T(8,128)}, u32[]{:S(2)}) copy-start(f32[16,64,128]{2,1,0:T(8,128)} %get-tuple-element.194) | copy-start | bytes 1572868
  170.9 55.2 %collective-permute-start.6 = (bf16[512,2048]{1,0:T(8,128)(2,1)}, bf16[512,2048]{1,0:T(8,128)(2,1)S(1)}, u32[]{:S(2)}, u32[]{:S(2)}) collective-permute-start(bf16[512,2048]{1,0:T(8,128)(2,1)} %collective-permute-done.5), channel_id=1, source_target_pairs={{0,1},{1,0},{2,3},{3,2},{4,5},{5,4},{6,7},{7,6},{8,9},{9,8},{10,11... | collective-permute-start | bytes 6291464 | tf_op jit(solution)/shard_map/ppermute | solution.py:433
  201.1 19.7 %all-to-all-start.1 = ((bf16[16,128,128]{1,2,0:T(8,128)(2,1)}), bf16[16,128,128]{1,2,0:T(8,128)(2,1)S(1)}, u32[]{:S(2)}, u32[]{:S(2)}) async-start(bf16[16,128,128]{1,2,0:T(8,128)(2,1)} %copy.226), calls=%async_computation.1 | async-start | bytes 1048576 | tf_op jit(solution)/shard_map/all_to_all | solution.py:459
  206.9 245.8 %all-gather.12.cloned.1.call-start = ((), (), s32[]{:S(2)}) async-start(), calls=%async_computation.9 | async-start | bytes 8912896 | tf_op jit(solution)/shard_map/all_gather | solution.py:453
  207.0 19.8 %copy-start.46 = (f32[1,8,2,128]{3,1,2,0:T(8,128)}, f32[1,8,2,128]{3,1,2,0:T(8,128)S(1)}, u32[]{:S(2)}) copy-start(f32[1,8,2,128]{3,1,2,0:T(8,128)S(1)} %copy.289) | copy-start | bytes 24580
  229.1 482.1 %reduce-scatter.2.cloned.1.call-start = ((), (), s32[]{:S(2)}) async-start(), calls=%async_computation.11 | async-start | bytes 8912896 | tf_op jit(solution)/shard_map/reduce_scatter | solution.py:462
  229.1 212.6 %collective-permute-start.7 = (bf16[704,2048]{1,0:T(8,128)(2,1)}, bf16[704,2048]{1,0:T(8,128)(2,1)}, u32[]{:S(2)}, u32[]{:S(2)}) collective-permute-start(bf16[704,2048]{1,0:T(8,128)(2,1)} %bitcast.236), channel_id=1, source_target_pairs={{16,0},{0,16},{17,1},{1,17},{18,2},{2,18},{19,3},{3,19},{20,4},{4,... | collective-permute-start | bytes 8650760 | tf_op jit(solution)/shard_map/ppermute | solution.py:383
  230.4 240.4 %collective-permute-start.8 = (bf16[1024,2816]{1,0:T(8,128)(2,1)}, bf16[1024,2816]{1,0:T(8,128)(2,1)}, u32[]{:S(2)}, u32[]{:S(2)}) collective-permute-start(bf16[1024,2816]{1,0:T(8,128)(2,1)} %bitcast.274), channel_id=1, source_target_pairs={{16,0},{0,16},{17,1},{1,17},{18,2},{2,18},{19,3},{3,19},{20,4},{4,... | collective-permute-start | bytes 17301512 | tf_op jit(solution)/shard_map/ppermute | solution.py:383
  233.2 219.4 %collective-permute-start.10 = (bf16[352,1024]{1,0:T(8,128)(2,1)S(1)}, bf16[352,1024]{1,0:T(8,128)(2,1)S(1)}, u32[]{:S(2)}, u32[]{:S(2)}) collective-permute-start(bf16[352,1024]{1,0:T(8,128)(2,1)S(1)} %pad_maximum_fusion.10.refs_0_), channel_id=1, source_target_pairs={{16,0},{0,16},{17,1},{1,17},{18,2},{2,18},{19,3},{3,19},{20,4},{4,... | collective-permute-start | bytes 2162696 | tf_op jit(solution)/shard_map/ppermute | solution.py:383
  237.4 202.6 %collective-permute-start.9 = (bf16[88,2048]{1,0:T(8,128)(2,1)}, bf16[88,2048]{1,0:T(8,128)(2,1)}, u32[]{:S(2)}, u32[]{:S(2)}) collective-permute-start(bf16[88,2048]{1,0:T(8,128)(2,1)} %get-tuple-element.152), channel_id=1, source_target_pairs={{16,0},{0,16},{17,1},{1,17},{18,2},{2,18},{19,3},{3,19},{20,4},{4,... | collective-permute-start | bytes 1081352 | tf_op jit(solution)/shard_map/ppermute | solution.py:383
  246.7 198.8 %copy-start.43 = (s32[32,64]{1,0:T(8,128)S(1)}, s32[32,64]{1,0:T(8,128)}, u32[]{:S(2)}) copy-start(s32[32,64]{1,0:T(8,128)} %copy-done.42) | copy-start | bytes 24580
  246.7 198.8 %copy-start.55 = (pred[32,64]{1,0:T(8,128)(4,1)S(1)}, pred[32,64]{1,0:T(8,128)(4,1)}, u32[]{:S(2)}) copy-start(pred[32,64]{1,0:T(8,128)(4,1)} %copy-done.54) | copy-start | bytes 6148
  467.8 73.8 %copy-start.17 = (bf16[2048,176]{1,0:T(8,128)(2,1)}, bf16[2048,176]{1,0:T(8,128)(2,1)S(1)}, u32[]{:S(2)}) copy-start(bf16[2048,176]{1,0:T(8,128)(2,1)S(1)} %get-tuple-element.63) | copy-start | bytes 2162692
  472.8 18.7 %copy-start.6 = (bf16[1024,2048]{1,0:T(8,128)(2,1)S(1)}, bf16[1024,2048]{1,0:T(8,128)(2,1)}, u32[]{:S(2)}) copy-start(bf16[1024,2048]{1,0:T(8,128)(2,1)} %fusion) | copy-start | bytes 12582916
  542.8 23.3 %all-to-all-start.2 = ((bf16[16,128,176]{1,2,0:T(8,128)(2,1)}), bf16[16,128,176]{1,2,0:T(8,128)(2,1)S(1)}, u32[]{:S(2)}, u32[]{:S(2)}) async-start(bf16[16,128,176]{1,2,0:T(8,128)(2,1)} %copy.241), calls=%async_computation.2 | async-start | bytes 1441792 | tf_op jit(solution)/shard_map/all_to_all | solution.py:459
  566.9 111.9 %all-to-all-start.3 = ((bf16[16,64,2048]{2,1,0:T(8,128)(2,1)}), bf16[16,64,2048]{2,1,0:T(8,128)(2,1)}, u32[]{:S(2)}, u32[]{:S(2)}) async-start(bf16[16,64,2048]{2,1,0:T(8,128)(2,1)} %bitcast.230), calls=%async_computation.3 | async-start | bytes 8388608 | tf_op jit(solution)/shard_map/all_to_all | solution.py:459
  572.1 426.9 %all-gather.16.cloned.1.call-start = ((), (), s32[]{:S(2)}) async-start(), calls=%async_computation.12 | async-start | bytes 8912896 | tf_op jit(solution)/shard_map/all_gather | solution.py:453
  580.6 130.6 %copy-start.1 = (f32[128,2048]{1,0:T(8,128)S(1)}, f32[128,2048]{1,0:T(8,128)}, u32[]{:S(2)}) copy-start(f32[128,2048]{1,0:T(8,128)} %copy-done) | copy-start | bytes 3145732
  580.6 130.6 %copy-start.47 = (f32[1,8,2,128]{3,1,2,0:T(8,128)S(1)}, f32[1,8,2,128]{3,1,2,0:T(8,128)}, u32[]{:S(2)}) copy-start(f32[1,8,2,128]{3,1,2,0:T(8,128)} %copy-done.46) | copy-start | bytes 24580
  580.6 130.6 %copy-start.67 = (f32[128]{0:T(128)S(1)}, f32[128]{0:T(128)}, u32[]{:S(2)}) copy-start(f32[128]{0:T(128)} %copy-done.66) | copy-start | bytes 1540
  580.6 132.2 %copy-start.19 = (bf16[2,1,64,2048]{3,2,1,0:T(8,128)(2,1)S(1)}, bf16[2,1,64,2048]{3,2,1,0:T(8,128)(2,1)}, u32[]{:S(2)}) copy-start(bf16[2,1,64,2048]{3,2,1,0:T(8,128)(2,1)} %param.17) | copy-start | bytes 1572868
  727.5 25.3 %all-to-all-start.4 = ((bf16[16,128,128]{2,1,0:T(8,128)(2,1)}), bf16[16,128,128]{2,1,0:T(8,128)(2,1)S(1)}, u32[]{:S(2)}, u32[]{:S(2)}) async-start(bf16[16,128,128]{2,1,0:T(8,128)(2,1)} %bitcast_bitcast_fusion.1), calls=%async_computation.5 | async-start | bytes 1048576 | tf_op jit(solution)/shard_map/all_to_all | solution.py:459
  767.4 65.4 %all-to-all-start.5 = ((bf16[16,128,512]{1,2,0:T(8,128)(2,1)}), bf16[16,128,512]{1,2,0:T(8,128)(2,1)}, u32[]{:S(2)}, u32[]{:S(2)}) async-start(bf16[16,128,512]{1,2,0:T(8,128)(2,1)} %copy.244), calls=%async_computation.6 | async-start | bytes 4194304 | tf_op jit(solution)/shard_map/all_to_all | solution.py:459
  773.4 278.6 %all-gather.18.cloned.1.call-start = ((), (), s32[]{:S(2)}) async-start(), calls=%async_computation.13 | async-start | bytes 3133440 | tf_op jit(solution)/shard_map/all_gather | solution.py:453
  775.7 24.9 %collective-permute-start.15 = (bf16[128,4096]{1,0:T(8,128)(2,1)}, bf16[128,4096]{1,0:T(8,128)(2,1)}, u32[]{:S(2)}, u32[]{:S(2)}) collective-permute-start(bf16[128,4096]{1,0:T(8,128)(2,1)} %constant_dynamic-slice_fusion.4), channel_id=1, source_target_pairs={{16,0},{0,16},{17,1},{1,17},{18,2},{2,18},{19,3},{3,19},{20,4},{4,... | collective-permute-start | bytes 3145736 | tf_op jit(solution)/shard_map/ppermute | solution.py:383
  800.6 39.0 %collective-permute-start.16 = (bf16[128,4096]{1,0:T(8,128)(2,1)}, bf16[128,4096]{1,0:T(8,128)(2,1)}, u32[]{:S(2)}, u32[]{:S(2)}) collective-permute-start(bf16[128,4096]{1,0:T(8,128)(2,1)} %collective-permute-done.15), channel_id=1, source_target_pairs={{0,1},{1,0},{2,3},{3,2},{4,5},{5,4},{6,7},{7,6},{8,9},{9,8},{10,11... | collective-permute-start | bytes 3145736 | tf_op jit(solution)/shard_map/ppermute | solution.py:433
  848.5 498.5 %all-gather.22.cloned.1.call-start = ((), (), s32[]{:S(2)}) async-start(), calls=%async_computation.15 | async-start | bytes 18382848 | tf_op jit(solution)/shard_map/all_gather | solution.py:456
  861.5 26.5 %slice-start.4 = ((f32[352,2048]{1,0:T(8,128)}), f32[352,1024]{1,0:T(8,128)S(1)}, s32[]{:S(2)}) async-start(f32[352,2048]{1,0:T(8,128)} %copy-done.15), calls=%async_computation.20 | async-start | bytes 2883584 | tf_op jit(solution)/shard_map/slice | solution.py:610
  862.6 25.3 %collective-permute-start.21 = (bf16[528,1024]{1,0:T(8,128)(2,1)}, bf16[528,1024]{1,0:T(8,128)(2,1)}, u32[]{:S(2)}, u32[]{:S(2)}) collective-permute-start(bf16[528,1024]{1,0:T(8,128)(2,1)} %pad_maximum_fusion.7), channel_id=1, source_target_pairs={{0,16},{16,0},{1,17},{17,1},{2,18},{18,2},{3,19},{19,3},{4,20},{20... | collective-permute-start | bytes 3244040 | tf_op jit(solution)/shard_map/ppermute | solution.py:386
  890.6 86.3 %copy-start.63 = (f32[2048]{0:T(1024)S(1)}, f32[2048]{0:T(1024)}, u32[]{:S(2)}) copy-start(f32[2048]{0:T(1024)} %copy-done.62) | copy-start | bytes 24580
  894.4 68.7 %collective-permute-start.13 = (bf16[512,3072]{1,0:T(8,128)(2,1)}, bf16[512,3072]{1,0:T(8,128)(2,1)}, u32[]{:S(2)}, u32[]{:S(2)}) collective-permute-start(bf16[512,3072]{1,0:T(8,128)(2,1)} %constant_dynamic-slice_fusion.5), channel_id=1, source_target_pairs={{16,0},{0,16},{17,1},{1,17},{18,2},{2,18},{19,3},{3,19},{20,4},{4,... | collective-permute-start | bytes 9437192 | tf_op jit(solution)/shard_map/ppermute | solution.py:383
  963.1 78.4 %collective-permute-start.14 = (bf16[512,3072]{1,0:T(8,128)(2,1)}, bf16[512,3072]{1,0:T(8,128)(2,1)}, u32[]{:S(2)}, u32[]{:S(2)}) collective-permute-start(bf16[512,3072]{1,0:T(8,128)(2,1)} %collective-permute-done.13), channel_id=1, source_target_pairs={{0,1},{1,0},{2,3},{3,2},{4,5},{5,4},{6,7},{7,6},{8,9},{9,8},{10,11... | collective-permute-start | bytes 9437192 | tf_op jit(solution)/shard_map/ppermute | solution.py:433
  966.1 32.9 %all-to-all-start.6 = ((bf16[16,128,128]{2,1,0:T(8,128)(2,1)}), bf16[16,128,128]{2,1,0:T(8,128)(2,1)}, u32[]{:S(2)}, u32[]{:S(2)}) async-start(bf16[16,128,128]{2,1,0:T(8,128)(2,1)} %bitcast_bitcast_fusion), calls=%async_computation.7 | async-start | bytes 1048576 | tf_op jit(solution)/shard_map/all_to_all | solution.py:459
  976.6 399.4 %all-gather.20.cloned.1.call-start = ((), (), s32[]{:S(2)}) async-start(), calls=%async_computation.14 | async-start | bytes 15040512 | tf_op jit(solution)/shard_map/all_gather | solution.py:456
  1006.0 18.6 %collective-permute-start.17 = (bf16[1024,384]{1,0:T(8,128)(2,1)}, bf16[1024,384]{1,0:T(8,128)(2,1)}, u32[]{:S(2)}, u32[]{:S(2)}) collective-permute-start(bf16[1024,384]{1,0:T(8,128)(2,1)} %pad_maximum_fusion.9), channel_id=1, source_target_pairs={{0,16},{16,0},{1,17},{17,1},{2,18},{18,2},{3,19},{19,3},{4,20},{20... | collective-permute-start | bytes 2359304 | tf_op jit(solution)/shard_map/ppermute | solution.py:386
  1050.7 6.5 collective-permute-start.19
  1056.9 3.4 collective-permute-start.18
  1061.4 256.4 %collective-permute-start.22 = (bf16[1024,2816]{1,0:T(8,128)(2,1)}, bf16[1024,2816]{1,0:T(8,128)(2,1)}, u32[]{:S(2)}, u32[]{:S(2)}) collective-permute-start(bf16[1024,2816]{1,0:T(8,128)(2,1)} %convolution_convert_fusion), channel_id=1, source_target_pairs={{0,16},{16,0},{1,17},{17,1},{2,18},{18,2},{3,19},{19,3},{4,20},{20... | collective-permute-start | bytes 17301512 | tf_op jit(solution)/shard_map/ppermute | solution.py:386
  1065.5 180.9 %collective-permute-start.11 = (bf16[704,2048]{1,0:T(8,128)(2,1)}, bf16[704,2048]{1,0:T(8,128)(2,1)}, u32[]{:S(2)}, u32[]{:S(2)}) collective-permute-start(bf16[704,2048]{1,0:T(8,128)(2,1)} %constant_dynamic-slice_fusion.6), channel_id=1, source_target_pairs={{16,0},{0,16},{17,1},{1,17},{18,2},{2,18},{19,3},{3,19},{20,4},{4,... | collective-permute-start | bytes 8650760 | tf_op jit(solution)/shard_map/ppermute | solution.py:383
  1066.7 241.4 %collective-permute-start.23 = (bf16[704,2048]{1,0:T(8,128)(2,1)}, bf16[704,2048]{1,0:T(8,128)(2,1)}, u32[]{:S(2)}, u32[]{:S(2)}) collective-permute-start(bf16[704,2048]{1,0:T(8,128)(2,1)} %convolution_convert_fusion.2), channel_id=1, source_target_pairs={{0,16},{16,0},{1,17},{17,1},{2,18},{18,2},{3,19},{19,3},{4,20},{20... | collective-permute-start | bytes 8650760 | tf_op jit(solution)/shard_map/ppermute | solution.py:386
  1067.5 250.4 %copy-start.14 = (bf16[32,32,2048]{2,1,0:T(8,128)(2,1)S(1)}, bf16[32,32,2048]{2,1,0:T(8,128)(2,1)}, u32[]{:S(2)}) copy-start(bf16[32,32,2048]{2,1,0:T(8,128)(2,1)} %copy-done.12) | copy-start | bytes 12582916
  1246.4 95.8 %collective-permute-start.12 = (bf16[704,2048]{1,0:T(8,128)(2,1)}, bf16[704,2048]{1,0:T(8,128)(2,1)}, u32[]{:S(2)}, u32[]{:S(2)}) collective-permute-start(bf16[704,2048]{1,0:T(8,128)(2,1)} %collective-permute-done.11), channel_id=1, source_target_pairs={{0,1},{1,0},{2,3},{3,2},{4,5},{5,4},{6,7},{7,6},{8,9},{9,8},{10,11... | collective-permute-start | bytes 8650760 | tf_op jit(solution)/shard_map/ppermute | solution.py:433
  1308.2 25.2 %slice-start.2 = ((s8[5767168]{0:T(1024)(128)(4,1)}), s8[4194304]{0:T(1024)(128)(4,1)S(1)}, s32[]{:S(2)}) async-start(s8[5767168]{0:T(1024)(128)(4,1)} %bitcast.210), calls=%async_computation.18 | async-start | bytes 8388608
  1342.0 3.8 collective-permute-start.20
  (58 other events, 294.3 us)
Sparse Core Ops, SparseCore 0:
  17.0 76.8 all-gather.9
  96.1 72.8 all-gather.13
  229.2 73.8 all-gather.11
  536.1 175.0 reduce-scatter.1
  713.2 118.6 all-gather.15
  848.6 50.0 all-gather.17
  900.3 98.4 all-gather.21
  1061.6 109.4 all-gather.19

commit v3 on v2

--- a/solution.py
+++ b/solution.py
@@ -599,7 +599,6 @@
     )[:6]
     hidden = swap(sact.reshape(groups, own, -1))
     gated = (gate_slots * dot(eact, weo)).astype(bf16)
-    returned = swap(after(gated, hidden).reshape(groups, micro * capacity, width))
     dspre, sact = lax.optimization_barrier((dspre, sact, gated))[:2]
     g_si = dot_tn(dspre, hid_all)
     g_so = dot_tn(sact, dy_all)
@@ -623,7 +622,7 @@
 
     sent_in = [expert_in_grad(r).astype(bf16) for r in range(1, parts)]
     sent_out = [expert_out_grad(r).astype(bf16) for r in range(1, parts)]
-    dhid_sum = after(dhid_sum, returned, hidden, *sent_in, *sent_out)
+    dhid_sum = after(dhid_sum, gated, hidden, *sent_in, *sent_out)
     got_in = [send(x, r).astype(f32) for r, x in enumerate(sent_in, 1)]
     got_out = [send(x, r).astype(f32) for r, x in enumerate(sent_out, 1)]
     dhid = natural(dhid_sum, 1).astype(f32)
@@ -667,7 +666,8 @@
 
     g_attn = exchanged(attn_grads(0), lambda r: attn_grads(r).astype(bf16))
 
-    returned, hidden = lax.optimization_barrier((returned, hidden, moved))[:2]
+    returned = after(gated, moved).reshape(groups, micro * capacity, width)
+    returned = swap(returned)
     hidden = hidden.reshape(groups, own, parts, run).transpose(1, 2, 0, 3).reshape(own, ff)
     hit_own = routes_own.reshape(micro, rows, 1, top) == expert_ids[:, None]
     hit_own = jnp.any(hit_own, -1)

time: 1420 us -> 1340 us (0.944)
  waiting for transfers between devices: 854 us -> 774 us
    all_to_all x7, waiting for transfers between devices: 162 us -> 69 us  [swap(): return lax.all_to_all(x, 'expert', split_axis=0, concat_axis=0, tiled=True)]
    reduce_scatter x1, waiting for transfers between devices: 32.3 us -> 61.3 us  [collect(): return lax.psum_scatter(x, 'expert', scatter_dimension=0, tiled=True)]
  transfers between devices with their start and end apart: 39 -> 39, of which waited for: 18 -> 16; matrix products, arithmetic and copies ran while one was open for 23% -> 24% of each run, Pallas kernels for 3% -> 4%
where the time goes in v3:
time: 1340 us; the launch traced here: 1320 us
  waiting for transfers between devices  774 us (58%)
  matrix products  208 us (16%)
  local copies, waits for them, and re-layouts  111 us (8%)
  starting transfers between devices  75.5 us (6%)
  Pallas kernels  73.5 us (5%)
  other arithmetic  65 us (5%)
  between operations  16.2 us (1%)
    ppermute x12, waiting for transfers between devices, shift(): lax.ppermute(x, 'dp', [((i + step) % parts, i) for i in range(parts)])  482 us
    ppermute x7, waiting for transfers between devices, send(): lax.ppermute(x, 'dp', [(i, (i + step) % parts) for i in range(parts)])  83.5 us
    dot_general x14, matrix products, dot_nt(): lax.dot_general(left, right, (((1,), (1,)), ((), ())), preferred_element_...  77.9 us
    all_gather x5, waiting for transfers between devices, spread(): return lax.all_gather(x, 'expert', axis=0, tiled=True)  77 us
    all_to_all x7, waiting for transfers between devices, swap(): return lax.all_to_all(x, 'expert', split_axis=0, concat_axis=0, tiled=True)  69 us
    dot_general x10, matrix products, dot_tn(): lax.dot_general(left, right, (((0,), (0,)), ((), ())), preferred_element_...  62.9 us
    reduce_scatter x1, waiting for transfers between devices, collect(): return lax.psum_scatter(x, 'expert', scatter_dimension=0, tiled=True)  61.3 us
    dot_general x10, matrix products, dot(): return jnp.dot(left, right, preferred_element_type=f32)  60.5 us
  transfers between devices with their start and end apart: 39, of which 16 were waited for; matrix products, arithmetic and copies ran while one was open for 24% of the time, Pallas kernels for 4%

profile of v3, /device:TPU:1, one launch (start us, length us, event | category | flops | bytes accessed | tf_op | source)
XLA Modules:
  0.0 1323.1 jit_solution(5493163457595400172)
XLA Ops:
  17.0 77.0 %all-gather.10.cloned.1.call-done = bf16[2048,2048]{1,0:T(8,128)(2,1)} async-done(((bf16[128,2048]{1,0:T(8,128)(2,1)}), bf16[2048,2048]{1,0:T(8,128)(2,1)}) %all-gather.10.cloned.1.call-update) | async-done | bytes 8388624 | tf_op jit(solution)/shard_map/all_gather | solution.py:453
  94.8 3.5 all-to-all-start
  103.8 3.2 constant_dynamic-slice_fusion.13
  109.3 13.8 %collective-permute-done.2 = bf16[512,576]{0,1:T(8,128)(2,1)} collective-permute-done((bf16[512,576]{0,1:T(8,128)(2,1)S(1)}, bf16[512,576]{0,1:T(8,128)(2,1)}, u32[]{:S(2)}, u32[]{:S(2)}) %collective-permute-start.2) | collective-permute-done | bytes 589856 | tf_op jit(solution)/shard_map/ppermute | solution.py:383
  135.4 7.2 dynamic_update_slice.63
  142.6 7.6 dynamic_update_slice.64
  155.9 14.9 %collective-permute-done.5 = bf16[512,2048]{1,0:T(8,128)(2,1)} collective-permute-done((bf16[512,2048]{1,0:T(8,128)(2,1)}, bf16[512,2048]{1,0:T(8,128)(2,1)}, u32[]{:S(2)}, u32[]{:S(2)}) %collective-permute-start.5) | collective-permute-done | bytes 2097184 | tf_op jit(solution)/shard_map/ppermute | solution.py:383
  172.0 12.4 fusion.120
  191.0 7.9 shard_map.255
  200.9 5.7 all-to-all-start.1
  206.7 13.9 %all-to-all-done.1 = bf16[16,128,128]{1,2,0:T(8,128)(2,1)S(1)} async-done(((bf16[16,128,128]{1,2,0:T(8,128)(2,1)}), bf16[16,128,128]{1,2,0:T(8,128)(2,1)S(1)}, u32[]{:S(2)}, u32[]{:S(2)}) %all-to-all-start.1) | async-done | bytes 524320 | tf_op jit(solution)/shard_map/all_to_all | solution.py:459
  220.6 3.1 fusion.62
  238.3 3.3 broadcast_in_dim.106
  248.1 191.5 %collective-permute-done.9 = bf16[88,2048]{1,0:T(8,128)(2,1)} collective-permute-done((bf16[88,2048]{1,0:T(8,128)(2,1)}, bf16[88,2048]{1,0:T(8,128)(2,1)}, u32[]{:S(2)}, u32[]{:S(2)}) %collective-permute-start.9) | collective-permute-done | bytes 360480 | tf_op jit(solution)/shard_map/ppermute | solution.py:383
  441.4 3.8 constant_dynamic-update-slice_fusion.3
  445.2 4.6 fusion.50
  452.4 8.4 fusion.14
  460.8 7.1 multiply_convert_fusion.7
  472.9 18.7 %fusion.2 = f32[1024,2816]{1,0:T(8,128)} fusion(bf16[1024,2048]{1,0:T(8,128)(2,1)S(1)} %bitcast.220, bf16[1024,2816]{1,0:T(8,128)(2,1)} %collective-permute-done.8, bf16[1024,2816]{1,0:T(8,128)(2,1)} %bitcast.277), kind=kOutput, calls=%fused_computation.6 | convolution fusion | flops 11834228736 | bytes 27262976 | tf_op jit(solution)/shard_map/dot_general | solution.py:76
  491.6 15.4 %multiply_convert_fusion.3 = (bf16[1024,1408]{1,0:T(8,128)(2,1)}, bf16[1024,1408]{1,0:T(8,128)(2,1)}, bf16[1024,1408]{1,0:T(8,128)(2,1)}) fusion(f32[1024,2816]{1,0:T(8,128)} %fusion.2, bf16[1024,2048]{1,0:T(8,128)(2,1)S(1)} %copy-done.6, bf16[1408,2048]{1,0:T(8,128)(2,1)} %constant_dynamic-update-slice_fusion.3), kind=kOutput, calls=%fused_computation.11 | convolution fusion | flops 5928648704 | bytes 30146560 | tf_op jit(solution)/shard_map/dot_general | solution.py:84
  506.9 18.2 %fusion.3.rows_ref = bf16[1024,2048]{1,0:T(8,128)(2,1)} fusion(bf16[1024,2816]{1,0:T(8,128)(2,1)} %collective-permute-done.8, bf16[1024,2816]{1,0:T(8,128)(2,1)} %bitcast.278, bf16[1024,1408]{1,0:T(8,128)(2,1)} %get-tuple-element.152, bf16[1024,1408]{1,0:T(8,128)(2,1)} %get-tuple-element.151), kind=kOutput, calls=%fused_computation.16 | convolution fusion | flops 11847860224 | bytes 21495808 | tf_op jit(solution)/shard_map/dot_general | solution.py:84
  525.1 10.9 shard_map.256
  536.7 5.6 pad_maximum_fusion.3
  543.5 5.9 all-to-all-start.2
  549.4 8.4 convolution_convert_fusion.2
  557.8 11.2 multiply_convert_fusion
  569.1 8.4 convolution_convert_fusion
  578.3 61.3 %reduce-scatter.2.cloned.1.call-done = bf16[128,2048]{1,0:T(8,128)(2,1)} async-done(((bf16[2048,2048]{1,0:T(8,128)(2,1)}), bf16[128,2048]{1,0:T(8,128)(2,1)}) %reduce-scatter.2.cloned.1.call-update) | async-done | bytes 524304 | tf_op jit(solution)/shard_map/reduce_scatter | solution.py:462
  641.5 2.8 fusion.121
  656.3 5.4 all-to-all-start.3
  664.9 17.3 %all-to-all-done.3 = bf16[16,128,128]{2,1,0:T(8,128)(2,1)S(1)} async-done(((bf16[16,128,128]{2,1,0:T(8,128)(2,1)}), bf16[16,128,128]{2,1,0:T(8,128)(2,1)S(1)}, u32[]{:S(2)}, u32[]{:S(2)}) %all-to-all-start.3) | async-done | bytes 524320 | tf_op jit(solution)/shard_map/all_to_all | solution.py:459
  683.0 9.9 shard_map.257
  692.8 3.9 copy.244
  696.7 5.7 all-to-all-start.4
  706.1 23.6 %collective-permute-done.15 = bf16[128,4096]{1,0:T(8,128)(2,1)} collective-permute-done((bf16[128,4096]{1,0:T(8,128)(2,1)}, bf16[128,4096]{1,0:T(8,128)(2,1)}, u32[]{:S(2)}, u32[]{:S(2)}) %collective-permute-start.15) | collective-permute-done | bytes 1048608 | tf_op jit(solution)/shard_map/ppermute | solution.py:383
  733.0 28.7 %all-to-all-done.4 = bf16[16,128,512]{1,2,0:T(8,128)(2,1)} async-done(((bf16[16,128,512]{1,2,0:T(8,128)(2,1)}), bf16[16,128,512]{1,2,0:T(8,128)(2,1)}, u32[]{:S(2)}, u32[]{:S(2)}) %all-to-all-start.4) | async-done | bytes 2097184 | tf_op jit(solution)/shard_map/all_to_all | solution.py:459
  777.5 5.8 fusion.127
  783.4 6.0 fusion.128
  794.0 23.0 %collective-permute-done.21 = bf16[528,1024]{1,0:T(8,128)(2,1)} collective-permute-done((bf16[528,1024]{1,0:T(8,128)(2,1)}, bf16[528,1024]{1,0:T(8,128)(2,1)}, u32[]{:S(2)}, u32[]{:S(2)}) %collective-permute-start.21) | collective-permute-done | bytes 1081376 | tf_op jit(solution)/shard_map/ppermute | solution.py:386
  819.7 3.8 constant_dynamic-slice_fusion.5
  824.6 67.5 %collective-permute-done.13 = bf16[512,3072]{1,0:T(8,128)(2,1)} collective-permute-done((bf16[512,3072]{1,0:T(8,128)(2,1)}, bf16[512,3072]{1,0:T(8,128)(2,1)}, u32[]{:S(2)}, u32[]{:S(2)}) %collective-permute-start.13) | collective-permute-done | bytes 3145760 | tf_op jit(solution)/shard_map/ppermute | solution.py:383
  895.2 10.4 all-to-all-start.6
  905.7 4.0 fusion.32
  912.4 5.3 fusion.34
  919.0 9.1 all-to-all-done.6
  928.1 5.8 fusion.126
  942.8 10.9 collective-permute-done.17
  957.2 4.1 fusion.124
  962.4 5.8 convolution_dynamic-update-slice_fusion.1
  970.3 4.0 fusion.125
  985.7 2.9 collective-permute-done.18
  990.0 3.8 constant_dynamic-slice_fusion.6
  995.1 8.1 all-to-all-start.5
  1004.0 170.7 %collective-permute-done.11 = bf16[704,2048]{1,0:T(8,128)(2,1)} collective-permute-done((bf16[704,2048]{1,0:T(8,128)(2,1)}, bf16[704,2048]{1,0:T(8,128)(2,1)}, u32[]{:S(2)}, u32[]{:S(2)}) %collective-permute-start.11) | collective-permute-done | bytes 2883616 | tf_op jit(solution)/shard_map/ppermute | solution.py:383
  1174.7 7.6 collective-permute-start.12
  1182.4 3.8 fusion.56
  1186.2 3.6 convolution_add_fusion.1
  1189.8 46.7 %collective-permute-done.23 = bf16[704,2048]{1,0:T(8,128)(2,1)} collective-permute-done((bf16[704,2048]{1,0:T(8,128)(2,1)}, bf16[704,2048]{1,0:T(8,128)(2,1)}, u32[]{:S(2)}, u32[]{:S(2)}) %collective-permute-start.23) | collective-permute-done | bytes 2883616 | tf_op jit(solution)/shard_map/ppermute | solution.py:386
  1236.5 6.7 add_bitcast_fusion.1
  1243.3 11.2 add_bitcast_fusion
  1266.1 3.3 fusion.7
  1269.4 17.3 %shard_map.259 = f32[1024,5632]{1,0:T(8,128)} custom-call(bf16[16,528,1024]{2,1,0:T(8,128)(2,1)} %bitcast.198), custom_call_target="tpu_custom_call" | custom-call | bytes 34603008 | tf_op jit(solution)/shard_map/pallas_call | solution.py:273
  1286.8 11.7 shard_map.260
  1299.4 15.8 %shard_map.258 = (f32[1024,2048]{1,0:T(8,128)}, f32[1024,3072]{1,0:T(8,128)}, f32[256,4096]{1,0:T(8,128)}, f32[576,1024]{1,0:T(8,128)}) custom-call(bf16[16,1152,384]{2,1,0:T(8,128)(2,1)} %bitcast.201, bf16[16,1152,384]{2,1,0:T(8,128)(2,1)} %bitcast.202), custom_call_target="tpu_custom_call" | custom-call | bytes 42467328 | tf_op jit(solution)/shard_map/pallas_call | solution.py:326
  (437 shorter events, 178.1 us)
Async XLA Ops:
  7.2 86.8 %copy-start.75 = (f32[2,1,64,6]{2,1,3,0:T(1,128)S(1)}, f32[2,1,64,6]{2,1,3,0:T(1,128)}, u32[]{:S(2)}) copy-start(f32[2,1,64,6]{2,1,3,0:T(1,128)} %param.20) | copy-start | bytes 9220
  7.2 86.9 %copy-start.76 = (s32[2,1,64,6]{2,1,3,0:T(1,128)S(1)}, s32[2,1,64,6]{2,1,3,0:T(1,128)}, u32[]{:S(2)}) copy-start(s32[2,1,64,6]{2,1,3,0:T(1,128)} %param.19) | copy-start | bytes 9220
  7.2 93.9 %copy-start.32 = (bf16[1024,576]{0,1:T(8,128)(2,1)S(1)}, bf16[1024,576]{0,1:T(8,128)(2,1)}, u32[]{:S(2)}) copy-start(bf16[1024,576]{0,1:T(8,128)(2,1)} %param.23) | copy-start | bytes 3538948
  7.2 86.7 %all-gather.10.cloned.1.call-start = ((), (), s32[]{:S(2)}) async-start(), calls=%async_computation.8 | async-start | bytes 8912896 | tf_op jit(solution)/shard_map/all_gather | solution.py:453
  9.7 3.5 collective-permute-start
  13.2 85.1 %copy-start.77 = (f32[128]{0:T(128)}, f32[128]{0:T(128)S(1)}, u32[]{:S(2)}) copy-start(f32[128]{0:T(128)S(1)} %rsqrt.38) | copy-start | bytes 1540
  13.4 80.6 %copy-start.63 = (bf16[2,2304]{1,0:T(2,128)(2,1)}, bf16[2,2304]{1,0:T(2,128)(2,1)S(1)}, u32[]{:S(2)}) copy-start(bf16[2,2304]{1,0:T(2,128)(2,1)S(1)} %dynamic_update_slice.61) | copy-start | bytes 27652
  16.9 428.2 %all-gather.14.cloned.1.call-start = ((), (), s32[]{:S(2)}) async-start(), calls=%async_computation.10 | async-start | bytes 8912896 | tf_op jit(solution)/shard_map/all_gather | solution.py:453
  94.8 35.7 %all-to-all-start = ((f32[16,1,128]{2,1,0:T(1,128)}), f32[16,1,128]{2,1,0:T(1,128)S(1)}, u32[]{:S(2)}, u32[]{:S(2)}) async-start(f32[16,1,128]{2,1,0:T(1,128)} %bitcast.2), calls=%async_computation | async-start | bytes 16384 | tf_op jit(solution)/shard_map/all_to_all | solution.py:459
  99.9 34.6 %collective-permute-start.1 = (bf16[1024,192]{0,1:T(8,128)(2,1)S(1)}, bf16[1024,192]{0,1:T(8,128)(2,1)S(1)}, u32[]{:S(2)}, u32[]{:S(2)}) collective-permute-start(bf16[1024,192]{0,1:T(8,128)(2,1)S(1)} %copy.269), channel_id=1, source_target_pairs={{16,0},{0,16},{17,1},{1,17},{18,2},{2,18},{19,3},{3,19},{20,4},{4,... | collective-permute-start | bytes 1179656 | tf_op jit(solution)/shard_map/ppermute | solution.py:383
  101.2 21.9 %collective-permute-start.2 = (bf16[512,576]{0,1:T(8,128)(2,1)S(1)}, bf16[512,576]{0,1:T(8,128)(2,1)}, u32[]{:S(2)}, u32[]{:S(2)}) collective-permute-start(bf16[512,576]{0,1:T(8,128)(2,1)S(1)} %constant_dynamic-slice_fusion.15), channel_id=1, source_target_pairs={{16,0},{0,16},{17,1},{1,17},{18,2},{2,18},{19,3},{3,19},{20,4},{4,... | collective-permute-start | bytes 1769480 | tf_op jit(solution)/shard_map/ppermute | solution.py:383
  102.5 24.3 %copy-start.33 = (bf16[1024,576]{0,1:T(8,128)(2,1)S(1)}, bf16[1024,576]{0,1:T(8,128)(2,1)}, u32[]{:S(2)}) copy-start(bf16[1024,576]{0,1:T(8,128)(2,1)} %param.23) | copy-start | bytes 3538948
  102.5 31.1 %collective-permute-start.4 = (bf16[256,256]{1,0:T(8,128)(2,1)S(1)}, bf16[256,256]{1,0:T(8,128)(2,1)}, u32[]{:S(2)}, u32[]{:S(2)}) collective-permute-start(bf16[256,256]{1,0:T(8,128)(2,1)S(1)} %get-tuple-element.150), channel_id=1, source_target_pairs={{16,0},{0,16},{17,1},{1,17},{18,2},{2,18},{19,3},{3,19},{20,4},{4,... | collective-permute-start | bytes 393224 | tf_op jit(solution)/shard_map/ppermute | solution.py:383
  106.9 64.0 %collective-permute-start.5 = (bf16[512,2048]{1,0:T(8,128)(2,1)}, bf16[512,2048]{1,0:T(8,128)(2,1)}, u32[]{:S(2)}, u32[]{:S(2)}) collective-permute-start(bf16[512,2048]{1,0:T(8,128)(2,1)} %constant_dynamic-slice_fusion.13), channel_id=1, source_target_pairs={{16,0},{0,16},{17,1},{1,17},{18,2},{2,18},{19,3},{3,19},{20,4},{4,... | collective-permute-start | bytes 6291464 | tf_op jit(solution)/shard_map/ppermute | solution.py:383
  123.1 19.5 %collective-permute-start.3 = (bf16[512,576]{0,1:T(8,128)(2,1)}, bf16[512,576]{0,1:T(8,128)(2,1)}, u32[]{:S(2)}, u32[]{:S(2)}) collective-permute-start(bf16[512,576]{0,1:T(8,128)(2,1)} %collective-permute-done.2), channel_id=1, source_target_pairs={{0,1},{1,0},{2,3},{3,2},{4,5},{5,4},{6,7},{7,6},{8,9},{9,8},{10,11... | collective-permute-start | bytes 1769480 | tf_op jit(solution)/shard_map/ppermute | solution.py:433
  130.4 58.8 %copy-start.64 = (f32[1,2,2,128]{3,1,2,0:T(2,128)}, f32[1,2,2,128]{3,1,2,0:T(2,128)S(1)}, u32[]{:S(2)}) copy-start(f32[1,2,2,128]{3,1,2,0:T(2,128)S(1)} %copy.281) | copy-start | bytes 6148
  130.4 21.4 %copy-start.56 = (f32[16,1,128]{2,1,0:T(1,128)}, f32[16,1,128]{2,1,0:T(1,128)S(1)}, u32[]{:S(2)}) copy-start(f32[16,1,128]{2,1,0:T(1,128)S(1)} %all-to-all-done) | copy-start | bytes 24580
  155.9 29.3 %copy-start.35 = (f32[16,64,128]{2,1,0:T(8,128)S(1)}, f32[16,64,128]{2,1,0:T(8,128)}, u32[]{:S(2)}) copy-start(f32[16,64,128]{2,1,0:T(8,128)} %get-tuple-element.189) | copy-start | bytes 1572868
  155.9 29.3 %copy-start.36 = (f32[16,64,128]{2,1,0:T(8,128)S(1)}, f32[16,64,128]{2,1,0:T(8,128)}, u32[]{:S(2)}) copy-start(f32[16,64,128]{2,1,0:T(8,128)} %get-tuple-element.190) | copy-start | bytes 1572868
  170.9 55.0 %collective-permute-start.6 = (bf16[512,2048]{1,0:T(8,128)(2,1)}, bf16[512,2048]{1,0:T(8,128)(2,1)S(1)}, u32[]{:S(2)}, u32[]{:S(2)}) collective-permute-start(bf16[512,2048]{1,0:T(8,128)(2,1)} %collective-permute-done.5), channel_id=1, source_target_pairs={{0,1},{1,0},{2,3},{3,2},{4,5},{5,4},{6,7},{7,6},{8,9},{9,8},{10,11... | collective-permute-start | bytes 6291464 | tf_op jit(solution)/shard_map/ppermute | solution.py:433
  200.9 19.7 %all-to-all-start.1 = ((bf16[16,128,128]{1,2,0:T(8,128)(2,1)}), bf16[16,128,128]{1,2,0:T(8,128)(2,1)S(1)}, u32[]{:S(2)}, u32[]{:S(2)}) async-start(bf16[16,128,128]{1,2,0:T(8,128)(2,1)} %copy.226), calls=%async_computation.1 | async-start | bytes 1048576 | tf_op jit(solution)/shard_map/all_to_all | solution.py:459
  206.6 245.7 %all-gather.12.cloned.1.call-start = ((), (), s32[]{:S(2)}) async-start(), calls=%async_computation.9 | async-start | bytes 8912896 | tf_op jit(solution)/shard_map/all_gather | solution.py:453
  228.8 410.8 %reduce-scatter.2.cloned.1.call-start = ((), (), s32[]{:S(2)}) async-start(), calls=%async_computation.11 | async-start | bytes 8912896 | tf_op jit(solution)/shard_map/reduce_scatter | solution.py:462
  228.8 212.6 %collective-permute-start.7 = (bf16[704,2048]{1,0:T(8,128)(2,1)}, bf16[704,2048]{1,0:T(8,128)(2,1)}, u32[]{:S(2)}, u32[]{:S(2)}) collective-permute-start(bf16[704,2048]{1,0:T(8,128)(2,1)} %bitcast.238), channel_id=1, source_target_pairs={{16,0},{0,16},{17,1},{1,17},{18,2},{2,18},{19,3},{3,19},{20,4},{4,... | collective-permute-start | bytes 8650760 | tf_op jit(solution)/shard_map/ppermute | solution.py:383
  230.1 240.8 %collective-permute-start.8 = (bf16[1024,2816]{1,0:T(8,128)(2,1)}, bf16[1024,2816]{1,0:T(8,128)(2,1)}, u32[]{:S(2)}, u32[]{:S(2)}) collective-permute-start(bf16[1024,2816]{1,0:T(8,128)(2,1)} %bitcast.276), channel_id=1, source_target_pairs={{16,0},{0,16},{17,1},{1,17},{18,2},{2,18},{19,3},{3,19},{20,4},{4,... | collective-permute-start | bytes 17301512 | tf_op jit(solution)/shard_map/ppermute | solution.py:383
  232.9 219.4 %collective-permute-start.10 = (bf16[352,1024]{1,0:T(8,128)(2,1)S(1)}, bf16[352,1024]{1,0:T(8,128)(2,1)S(1)}, u32[]{:S(2)}, u32[]{:S(2)}) collective-permute-start(bf16[352,1024]{1,0:T(8,128)(2,1)S(1)} %pad_maximum_fusion.10.refs_0_), channel_id=1, source_target_pairs={{16,0},{0,16},{17,1},{1,17},{18,2},{2,18},{19,3},{3,19},{20,4},{4,... | collective-permute-start | bytes 2162696 | tf_op jit(solution)/shard_map/ppermute | solution.py:383
  237.1 202.6 %collective-permute-start.9 = (bf16[88,2048]{1,0:T(8,128)(2,1)}, bf16[88,2048]{1,0:T(8,128)(2,1)}, u32[]{:S(2)}, u32[]{:S(2)}) collective-permute-start(bf16[88,2048]{1,0:T(8,128)(2,1)} %get-tuple-element.148), channel_id=1, source_target_pairs={{16,0},{0,16},{17,1},{1,17},{18,2},{2,18},{19,3},{3,19},{20,4},{4,... | collective-permute-start | bytes 1081352 | tf_op jit(solution)/shard_map/ppermute | solution.py:383
  246.4 198.8 %copy-start.48 = (s32[32,64]{1,0:T(8,128)S(1)}, s32[32,64]{1,0:T(8,128)}, u32[]{:S(2)}) copy-start(s32[32,64]{1,0:T(8,128)} %copy-done.47) | copy-start | bytes 24580
  246.4 198.8 %copy-start.60 = (pred[32,64]{1,0:T(8,128)(4,1)S(1)}, pred[32,64]{1,0:T(8,128)(4,1)}, u32[]{:S(2)}) copy-start(pred[32,64]{1,0:T(8,128)(4,1)} %copy-done.59) | copy-start | bytes 6148
  467.8 74.5 %copy-start.18 = (bf16[2048,176]{1,0:T(8,128)(2,1)}, bf16[2048,176]{1,0:T(8,128)(2,1)S(1)}, u32[]{:S(2)}) copy-start(bf16[2048,176]{1,0:T(8,128)(2,1)S(1)} %get-tuple-element.59) | copy-start | bytes 2162692
  536.1 392.0 %all-gather.16.cloned.1.call-start = ((), (), s32[]{:S(2)}) async-start(), calls=%async_computation.12 | async-start | bytes 8912896 | tf_op jit(solution)/shard_map/all_gather | solution.py:453
  543.5 33.9 %all-to-all-start.2 = ((bf16[16,128,176]{1,2,0:T(8,128)(2,1)}), bf16[16,128,176]{1,2,0:T(8,128)(2,1)S(1)}, u32[]{:S(2)}, u32[]{:S(2)}) async-start(bf16[16,128,176]{1,2,0:T(8,128)(2,1)} %copy.241), calls=%async_computation.3 | async-start | bytes 1441792 | tf_op jit(solution)/shard_map/all_to_all | solution.py:459
  569.1 70.5 %copy-start.1 = (f32[128,2048]{1,0:T(8,128)S(1)}, f32[128,2048]{1,0:T(8,128)}, u32[]{:S(2)}) copy-start(f32[128,2048]{1,0:T(8,128)} %copy-done) | copy-start | bytes 3145732
  569.1 70.5 %copy-start.52 = (f32[1,8,2,128]{3,1,2,0:T(8,128)S(1)}, f32[1,8,2,128]{3,1,2,0:T(8,128)}, u32[]{:S(2)}) copy-start(f32[1,8,2,128]{3,1,2,0:T(8,128)} %copy-done.51) | copy-start | bytes 24580
  569.1 70.5 %copy-start.73 = (f32[128]{0:T(128)S(1)}, f32[128]{0:T(128)}, u32[]{:S(2)}) copy-start(f32[128]{0:T(128)} %copy-done.72) | copy-start | bytes 1540
  569.1 72.1 %copy-start.20 = (bf16[2,1,64,2048]{3,2,1,0:T(8,128)(2,1)S(1)}, bf16[2,1,64,2048]{3,2,1,0:T(8,128)(2,1)}, u32[]{:S(2)}) copy-start(bf16[2,1,64,2048]{3,2,1,0:T(8,128)(2,1)} %param.17) | copy-start | bytes 1572868
  656.3 25.9 %all-to-all-start.3 = ((bf16[16,128,128]{2,1,0:T(8,128)(2,1)}), bf16[16,128,128]{2,1,0:T(8,128)(2,1)S(1)}, u32[]{:S(2)}, u32[]{:S(2)}) async-start(bf16[16,128,128]{2,1,0:T(8,128)(2,1)} %bitcast_bitcast_fusion.1), calls=%async_computation.4 | async-start | bytes 1048576 | tf_op jit(solution)/shard_map/all_to_all | solution.py:459
  696.7 65.0 %all-to-all-start.4 = ((bf16[16,128,512]{1,2,0:T(8,128)(2,1)}), bf16[16,128,512]{1,2,0:T(8,128)(2,1)}, u32[]{:S(2)}, u32[]{:S(2)}) async-start(bf16[16,128,512]{1,2,0:T(8,128)(2,1)} %copy.244), calls=%async_computation.5 | async-start | bytes 4194304 | tf_op jit(solution)/shard_map/all_to_all | solution.py:459
  702.5 279.1 %all-gather.18.cloned.1.call-start = ((), (), s32[]{:S(2)}) async-start(), calls=%async_computation.13 | async-start | bytes 3133440 | tf_op jit(solution)/shard_map/all_gather | solution.py:453
  704.9 24.9 %collective-permute-start.15 = (bf16[128,4096]{1,0:T(8,128)(2,1)}, bf16[128,4096]{1,0:T(8,128)(2,1)}, u32[]{:S(2)}, u32[]{:S(2)}) collective-permute-start(bf16[128,4096]{1,0:T(8,128)(2,1)} %constant_dynamic-slice_fusion.4), channel_id=1, source_target_pairs={{16,0},{0,16},{17,1},{1,17},{18,2},{2,18},{19,3},{3,19},{20,4},{4,... | collective-permute-start | bytes 3145736 | tf_op jit(solution)/shard_map/ppermute | solution.py:383
  729.7 38.8 %collective-permute-start.16 = (bf16[128,4096]{1,0:T(8,128)(2,1)}, bf16[128,4096]{1,0:T(8,128)(2,1)}, u32[]{:S(2)}, u32[]{:S(2)}) collective-permute-start(bf16[128,4096]{1,0:T(8,128)(2,1)} %collective-permute-done.15), channel_id=1, source_target_pairs={{0,1},{1,0},{2,3},{3,2},{4,5},{5,4},{6,7},{7,6},{8,9},{9,8},{10,11... | collective-permute-start | bytes 3145736 | tf_op jit(solution)/shard_map/ppermute | solution.py:433
  777.4 492.0 %all-gather.22.cloned.1.call-start = ((), (), s32[]{:S(2)}) async-start(), calls=%async_computation.15 | async-start | bytes 18382848 | tf_op jit(solution)/shard_map/all_gather | solution.py:456
  790.6 26.4 %slice-start.6 = ((f32[352,2048]{1,0:T(8,128)}), f32[352,1024]{1,0:T(8,128)S(1)}, s32[]{:S(2)}) async-start(f32[352,2048]{1,0:T(8,128)} %copy-done.16), calls=%async_computation.22 | async-start | bytes 2883584 | tf_op jit(solution)/shard_map/slice | solution.py:609
  791.7 25.3 %collective-permute-start.21 = (bf16[528,1024]{1,0:T(8,128)(2,1)}, bf16[528,1024]{1,0:T(8,128)(2,1)}, u32[]{:S(2)}, u32[]{:S(2)}) collective-permute-start(bf16[528,1024]{1,0:T(8,128)(2,1)} %pad_maximum_fusion.7), channel_id=1, source_target_pairs={{0,16},{16,0},{1,17},{17,1},{2,18},{18,2},{3,19},{19,3},{4,20},{20... | collective-permute-start | bytes 3244040 | tf_op jit(solution)/shard_map/ppermute | solution.py:386
  819.6 86.1 %copy-start.68 = (f32[2048]{0:T(1024)S(1)}, f32[2048]{0:T(1024)}, u32[]{:S(2)}) copy-start(f32[2048]{0:T(1024)} %copy-done.67) | copy-start | bytes 24580
  823.4 68.7 %collective-permute-start.13 = (bf16[512,3072]{1,0:T(8,128)(2,1)}, bf16[512,3072]{1,0:T(8,128)(2,1)}, u32[]{:S(2)}, u32[]{:S(2)}) collective-permute-start(bf16[512,3072]{1,0:T(8,128)(2,1)} %constant_dynamic-slice_fusion.5), channel_id=1, source_target_pairs={{16,0},{0,16},{17,1},{1,17},{18,2},{2,18},{19,3},{3,19},{20,4},{4,... | collective-permute-start | bytes 9437192 | tf_op jit(solution)/shard_map/ppermute | solution.py:383
  892.2 78.1 %collective-permute-start.14 = (bf16[512,3072]{1,0:T(8,128)(2,1)}, bf16[512,3072]{1,0:T(8,128)(2,1)}, u32[]{:S(2)}, u32[]{:S(2)}) collective-permute-start(bf16[512,3072]{1,0:T(8,128)(2,1)} %collective-permute-done.13), channel_id=1, source_target_pairs={{0,1},{1,0},{2,3},{3,2},{4,5},{5,4},{6,7},{7,6},{8,9},{9,8},{10,11... | collective-permute-start | bytes 9437192 | tf_op jit(solution)/shard_map/ppermute | solution.py:433
  895.2 32.9 %all-to-all-start.6 = ((bf16[16,128,128]{2,1,0:T(8,128)(2,1)}), bf16[16,128,128]{2,1,0:T(8,128)(2,1)}, u32[]{:S(2)}, u32[]{:S(2)}) async-start(bf16[16,128,128]{2,1,0:T(8,128)(2,1)} %bitcast_bitcast_fusion), calls=%async_computation.7 | async-start | bytes 1048576 | tf_op jit(solution)/shard_map/all_to_all | solution.py:459
  905.7 392.8 %all-gather.20.cloned.1.call-start = ((), (), s32[]{:S(2)}) async-start(), calls=%async_computation.14 | async-start | bytes 15040512 | tf_op jit(solution)/shard_map/all_gather | solution.py:456
  935.1 18.5 %collective-permute-start.17 = (bf16[1024,384]{1,0:T(8,128)(2,1)}, bf16[1024,384]{1,0:T(8,128)(2,1)}, u32[]{:S(2)}, u32[]{:S(2)}) collective-permute-start(bf16[1024,384]{1,0:T(8,128)(2,1)} %pad_maximum_fusion.9), channel_id=1, source_target_pairs={{0,16},{16,0},{1,17},{17,1},{2,18},{18,2},{3,19},{19,3},{4,20},{20... | collective-permute-start | bytes 2359304 | tf_op jit(solution)/shard_map/ppermute | solution.py:386
  980.3 5.2 collective-permute-start.19
  985.3 3.4 collective-permute-start.18
  989.8 253.4 %collective-permute-start.22 = (bf16[1024,2816]{1,0:T(8,128)(2,1)}, bf16[1024,2816]{1,0:T(8,128)(2,1)}, u32[]{:S(2)}, u32[]{:S(2)}) collective-permute-start(bf16[1024,2816]{1,0:T(8,128)(2,1)} %convolution_convert_fusion), channel_id=1, source_target_pairs={{0,16},{16,0},{1,17},{17,1},{2,18},{18,2},{3,19},{19,3},{4,20},{20... | collective-permute-start | bytes 17301512 | tf_op jit(solution)/shard_map/ppermute | solution.py:386
  993.8 180.9 %collective-permute-start.11 = (bf16[704,2048]{1,0:T(8,128)(2,1)}, bf16[704,2048]{1,0:T(8,128)(2,1)}, u32[]{:S(2)}, u32[]{:S(2)}) collective-permute-start(bf16[704,2048]{1,0:T(8,128)(2,1)} %constant_dynamic-slice_fusion.6), channel_id=1, source_target_pairs={{16,0},{0,16},{17,1},{1,17},{18,2},{2,18},{19,3},{3,19},{20,4},{4,... | collective-permute-start | bytes 8650760 | tf_op jit(solution)/shard_map/ppermute | solution.py:383
  995.1 187.2 %copy-start.31 = (bf16[16,128,176]{1,2,0:T(8,128)(2,1)S(1)}, bf16[16,128,176]{1,2,0:T(8,128)(2,1)}, u32[]{:S(2)}) copy-start(bf16[16,128,176]{1,2,0:T(8,128)(2,1)} %copy-done.30) | copy-start | bytes 2162692
  995.1 267.3 %all-to-all-start.5 = ((bf16[16,64,2048]{2,1,0:T(8,128)(2,1)}), bf16[16,64,2048]{2,1,0:T(8,128)(2,1)}, u32[]{:S(2)}, u32[]{:S(2)}) async-start(bf16[16,64,2048]{2,1,0:T(8,128)(2,1)} %bitcast.232), calls=%async_computation.6 | async-start | bytes 8388608 | tf_op jit(solution)/shard_map/all_to_all | solution.py:459
  1003.2 233.2 %collective-permute-start.23 = (bf16[704,2048]{1,0:T(8,128)(2,1)}, bf16[704,2048]{1,0:T(8,128)(2,1)}, u32[]{:S(2)}, u32[]{:S(2)}) collective-permute-start(bf16[704,2048]{1,0:T(8,128)(2,1)} %convolution_convert_fusion.2), channel_id=1, source_target_pairs={{0,16},{16,0},{1,17},{17,1},{2,18},{18,2},{3,19},{19,3},{4,20},{20... | collective-permute-start | bytes 8650760 | tf_op jit(solution)/shard_map/ppermute | solution.py:386
  1174.7 91.1 %collective-permute-start.12 = (bf16[704,2048]{1,0:T(8,128)(2,1)}, bf16[704,2048]{1,0:T(8,128)(2,1)}, u32[]{:S(2)}, u32[]{:S(2)}) collective-permute-start(bf16[704,2048]{1,0:T(8,128)(2,1)} %collective-permute-done.11), channel_id=1, source_target_pairs={{0,1},{1,0},{2,3},{3,2},{4,5},{5,4},{6,7},{7,6},{8,9},{9,8},{10,11... | collective-permute-start | bytes 8650760 | tf_op jit(solution)/shard_map/ppermute | solution.py:433
  1182.4 54.1 %copy-start.7 = (bf16[1024,2048]{1,0:T(8,128)(2,1)S(1)}, bf16[1024,2048]{1,0:T(8,128)(2,1)}, u32[]{:S(2)}) copy-start(bf16[1024,2048]{1,0:T(8,128)(2,1)} %fusion) | copy-start | bytes 12582916
  1182.4 54.1 %copy-start.41 = (bf16[1024,1408]{1,0:T(8,128)(2,1)S(1)}, bf16[1024,1408]{1,0:T(8,128)(2,1)}, u32[]{:S(2)}) copy-start(bf16[1024,1408]{1,0:T(8,128)(2,1)} %get-tuple-element.40) | copy-start | bytes 8650756
  1186.2 57.0 %slice-start.4 = ((s8[5767168]{0:T(1024)(128)(4,1)}), s8[4194304]{0:T(1024)(128)(4,1)S(1)}, s32[]{:S(2)}) async-start(s8[5767168]{0:T(1024)(128)(4,1)} %bitcast.208), calls=%async_computation.20 | async-start | bytes 8388608
  1189.8 53.5 %slice-start.5 = ((s8[5767168]{0:T(1024)(128)(4,1)}), s8[1572864]{0:T(1024)(128)(4,1)S(1)}, s32[]{:S(2)}) async-start(s8[5767168]{0:T(1024)(128)(4,1)} %bitcast.208), calls=%async_computation.21 | async-start | bytes 3145728
  1189.8 53.5 %copy-start.15 = (bf16[32,32,2048]{2,1,0:T(8,128)(2,1)S(1)}, bf16[32,32,2048]{2,1,0:T(8,128)(2,1)}, u32[]{:S(2)}) copy-start(bf16[32,32,2048]{2,1,0:T(8,128)(2,1)} %copy-done.13) | copy-start | bytes 12582916
  1258.2 3.1 collective-permute-start.20
  (65 other events, 483.5 us)
Sparse Core Ops, SparseCore 0:
  17.0 76.8 all-gather.9
  96.1 72.8 all-gather.13
  228.9 73.8 all-gather.11
  536.2 103.3 reduce-scatter.1
  641.6 119.0 all-gather.15
  777.5 50.1 all-gather.17
  829.8 98.4 all-gather.21
  989.9 189.6 all-gather.19

commit v4 on v3

--- a/solution.py
+++ b/solution.py
@@ -293,7 +293,7 @@
     return in_grad, out_grad.reshape(groups * piece, -1)
 
 
-def attn_rows_kernel(x_ref, extra_ref, out_ref, query_ref, kvup_ref, down_ref, *, a, b, height):
+def attn_rows_kernel(x_ref, out_ref, query_ref, kvup_ref, *, a, b):
     groups, _, count = x_ref.shape
     rest = count - a - b
     runs = x_ref.shape[1] // kvup_ref.shape[0]
@@ -308,44 +308,33 @@
             x[c * step : (c + 1) * step, a + b :] for x in (one, two) for c in range(runs)
         ]
         kvup_ref[:, e * runs * rest : (e + 2) * runs * rest] = jnp.concatenate(pieces, 1)
-    half = count // 2
-    rows = []
-    for e in range(extra_ref.shape[0]):
-        x = extra_ref[e].astype(f32)
-        tail = x[height : height + height // 2]
-        tail = jnp.concatenate([tail[:, :half], tail[:, half:]], 0)
-        rows.append(jnp.concatenate([x[:height], tail], 1))
-    down_ref[...] = jnp.concatenate(rows, 0).T
-
-
-def attn_rows(stacked, rows, a, b, kvup_height, down_height):
-    groups, _, count = stacked.shape
+
+
+def attn_rows(stacked, a, b, kvup_height):
+    groups, rows, count = stacked.shape
     size = 128
     steps = rows // size
     kvup_width = (count - a - b) * rows // kvup_height
     return pl.pallas_call(
-        functools.partial(attn_rows_kernel, a=a, b=b, height=down_height),
+        functools.partial(attn_rows_kernel, a=a, b=b),
         out_shape=(
             jax.ShapeDtypeStruct((rows, groups * a), f32),
             jax.ShapeDtypeStruct((rows, groups * b), f32),
             jax.ShapeDtypeStruct((kvup_height, groups * kvup_width), f32),
-            jax.ShapeDtypeStruct((count * 3 // 2, groups * down_height), f32),
         ),
         grid=(steps,),
         in_specs=[
             pl.BlockSpec((groups, size, count), lambda i: (0, i, 0)),
-            pl.BlockSpec((groups // steps, size, count), lambda i: (i, steps, 0)),
         ],
         out_specs=(
             pl.BlockSpec((size, groups * a), lambda i: (i, 0)),
             pl.BlockSpec((size, groups * b), lambda i: (i, 0)),
             pl.BlockSpec((kvup_height // steps, groups * kvup_width), lambda i: (i, 0)),
-            pl.BlockSpec((count * 3 // 2, groups // steps * down_height), lambda i: (0, i)),
         ),
         cost_estimate=pl.CostEstimate(
             flops=0, transcendentals=0, bytes_accessed=6 * stacked.size
         ),
-    )(stacked, stacked)
+    )(stacked)
 
 
 def per_device(
@@ -458,6 +447,18 @@
     def swap(x):
         return lax.all_to_all(x, "expert", split_axis=0, concat_axis=0, tiled=True)
 
+    def spread_pairs(x):
+        assert groups & (groups - 1) == 0
+        whole, mask = x[None], groups // 2
+        while mask:
+            partners = [(i, i ^ mask) for i in range(groups)]
+            other = lax.ppermute(whole, "expert", partners)
+            upper = (me // mask) % 2 == 1
+            pair = [jnp.where(upper, other, whole), jnp.where(upper, whole, other)]
+            whole = jnp.stack(pair, 1).reshape((2 * whole.shape[0],) + x.shape)
+            mask //= 2
+        return whole
+
     def collect(x):
         return lax.psum_scatter(x, "expert", scatter_dimension=0, tiled=True)
 
@@ -665,9 +666,57 @@
         )
 
     g_attn = exchanged(attn_grads(0), lambda r: attn_grads(r).astype(bf16))
-
-    returned = after(gated, moved).reshape(groups, micro * capacity, width)
+    g_attn = stack(row_major(g_attn.astype(bf16)))
+
+    dq_own = back_of(moved, 0, qk)
+    dkvup_own = back_of(moved, 256, 512)
+    dkrope_own = jnp.sum(moved[..., qk:256].astype(f32), 0)
+    dlatent = dot_pieces_t(dkvup_own, wkvup)
+    latent_own = lax.dynamic_slice_in_dim(latent_raw, me * own, own, 0)
+    cos_own = jnp.tile(lax.dynamic_slice_in_dim(cosine, me * rows, rows, 0), (micro, 1))
+    sin_own = jnp.tile(lax.dynamic_slice_in_dim(sine, me * rows, rows, 0), (micro, 1))
+    dlatent_raw, g_kv_gain = normed_back(latent_own, gain_kv, dlatent)
+    dkvfull = jnp.concatenate([dlatent_raw, rotate_back(dkrope_own, cos_own, sin_own)], -1)
+    dkvfull = dkvfull.astype(bf16)
+    down = LATENT + ROPE
+    early = jnp.concatenate([g_kv_gain, g_ffn_gain])
+    short = early.shape[0]
+    early = jnp.pad(early, (0, 16 * down - short)).reshape(16, down)
+    dkv_all = spread_pairs(jnp.concatenate([dkvfull, early.astype(bf16)], 0))
+    early = jnp.sum(dkv_all[:, own:].astype(f32), 0).reshape(-1)[:short]
+    dkv_all = dkv_all[:, :own].reshape(total, down)
+    dact = dot_pieces_t(dq_own, wq) + natural(dot_nt(dkvfull, w_down), 1)
+    dx_norm, g_attn_gain = normed_back(x_own.astype(f32), gain_attn, dact)
+    input_grad = dx1 + dx_norm
+
+    height = size // groups
+    act_rows = jnp.concatenate(
+        [
+            lax.dynamic_slice_in_dim(act, c * size + me * height, height, 1)
+            for c in range(parts)
+        ],
+        1,
+    )
+    g_down = dot_tn(act_rows, dkv_all)
+    g_down = exchanged(
+        g_down[:height], lambda r: g_down[r * height : (r + 1) * height].astype(bf16)
+    ).astype(bf16)
+    early_kv, early_ffn = early[:LATENT], early[LATENT:]
+
+    def early_gains(r):
+        return jnp.concatenate([block_of(early_kv, part + r), block_of(early_ffn, part + r)])
+
+    early = exchanged(early_gains(0), early_gains)
+    late = exchanged(block_of(g_attn_gain, part), lambda r: block_of(g_attn_gain, part + r))
+    late_rows = -(-size // down)
+    late = jnp.pad(late, (0, 16 * down - size)).reshape(16, down)
+    last = spread_pairs(jnp.concatenate([g_down, late.astype(bf16)], 0))
+    returned = after(gated, last).reshape(groups, micro * capacity, width)
     returned = swap(returned)
+    g_down = last[:, :height].astype(f32).reshape(size, down)
+    late = jnp.sum(last[:, height : height + late_rows].astype(f32), 0).reshape(-1)[:size]
+    gains = (late, early[: LATENT // parts], early[LATENT // parts :])
+
     hidden = hidden.reshape(groups, own, parts, run).transpose(1, 2, 0, 3).reshape(own, ff)
     hit_own = routes_own.reshape(micro, rows, 1, top) == expert_ids[:, None]
     hit_own = jnp.any(hit_own, -1)
@@ -684,74 +733,17 @@
     ).reshape(own, width)
     out_sum = routed + dot_pieces(hidden, wso)
 
-    dq_own = back_of(moved, 0, qk)
-    dkvup_own = back_of(moved, 256, 512)
-    dkrope_own = jnp.sum(moved[..., qk:256].astype(f32), 0)
-    dlatent = dot_pieces_t(dkvup_own, wkvup)
-    latent_own = lax.dynamic_slice_in_dim(latent_raw, me * own, own, 0)
-    cos_own = jnp.tile(lax.dynamic_slice_in_dim(cosine, me * rows, rows, 0), (micro, 1))
-    sin_own = jnp.tile(lax.dynamic_slice_in_dim(sine, me * rows, rows, 0), (micro, 1))
-    dlatent_raw, g_kv_gain = normed_back(latent_own, gain_kv, dlatent)
-    dkvfull = jnp.concatenate([dlatent_raw, rotate_back(dkrope_own, cos_own, sin_own)], -1)
-    dkvfull = dkvfull.astype(bf16)
-    down = LATENT + ROPE
-    early = jnp.concatenate([g_kv_gain, g_ffn_gain])
-    short = early.shape[0]
-    early = jnp.pad(early, (0, 16 * down - short)).reshape(16, down)
-    dkv_all = spread(jnp.concatenate([dkvfull, early.astype(bf16)], 0))
-    dkv_all = dkv_all.reshape(groups, own + 16, down)
-    early = jnp.sum(dkv_all[:, own:].astype(f32), 0).reshape(-1)[:short]
-    dkv_all = dkv_all[:, :own].reshape(total, down)
-    dact = dot_pieces_t(dq_own, wq) + natural(dot_nt(dkvfull, w_down), 1)
-    dx_norm, g_attn_gain = normed_back(x_own.astype(f32), gain_attn, dact)
-    input_grad = dx1 + dx_norm
-
-    height = size // groups
-    act_rows = jnp.concatenate(
-        [
-            lax.dynamic_slice_in_dim(act, c * size + me * height, height, 1)
-            for c in range(parts)
-        ],
-        1,
-    )
-    g_down = dot_tn(act_rows, dkv_all)
-    g_down = exchanged(
-        g_down[:height], lambda r: g_down[r * height : (r + 1) * height].astype(bf16)
-    ).astype(bf16)
-    early_kv, early_ffn = early[:LATENT], early[LATENT:]
-
-    def early_gains(r):
-        return jnp.concatenate([block_of(early_kv, part + r), block_of(early_ffn, part + r)])
-
-    early = exchanged(early_gains(0), early_gains)
-    late = exchanged(block_of(g_attn_gain, part), lambda r: block_of(g_attn_gain, part + r))
-    count = g_attn.shape[1]
-    tail = g_down[:, count:]
-    tail = jnp.concatenate([tail[: height // 2], tail[height // 2 :]], 1)
-    extra = jnp.concatenate([g_down[:, :count], tail], 0)
-    at_late = size + extra.shape[0]
-    late_rows = -(-size // count)
-    late = jnp.pad(late, (0, late_rows * count - size)).reshape(late_rows, count)
-    extra = jnp.concatenate([extra, late.astype(bf16)], 0)
-    extra = jnp.pad(extra, ((0, 128 - extra.shape[0]), (0, 0)))
-    g_attn = jnp.concatenate([g_attn.astype(bf16), extra], 0)
-    g_attn = stack(row_major(g_attn))
-    late = jnp.sum(g_attn[:, at_late : at_late + late_rows].astype(f32), 0).reshape(-1)[:size]
-    gains = (late, early[: LATENT // parts], early[LATENT // parts :])
-
     mixed = (x1 + out_sum).astype(bf16)
     g_ein = sum(got_in, expert_in_grad(0))
     g_eout = sum(got_out, expert_out_grad(0))
-    out_grad, query_grad, kvup_grad, g_down = attn_rows(
-        g_attn, size, width // groups, qk, LATENT // parts, height
-    )
+    out_grad, query_grad, kvup_grad = attn_rows(g_attn, width // groups, qk, LATENT // parts)
     shared_in_grad, shared_out_grad = shared_rows(g_shared, 2 * parts, run)
     return (
         mixed.reshape(micro, 1, rows, width),
         input_grad.reshape(micro, 1, rows, width),
         gains[0],
         query_grad,
-        g_down.T,
+        g_down,
         gains[1],
         kvup_grad,
         out_grad,

time: 1340 us -> 1420 us (1.060)
  waiting for transfers between devices: 774 us -> 845 us
    ppermute x0 -> x8, waiting for transfers between devices: none -> 84 us  [spread_pairs(): other = lax.ppermute(whole, 'expert', partners)]
    all_to_all x7, waiting for transfers between devices: 69 us -> 32.4 us  [swap(): return lax.all_to_all(x, 'expert', split_axis=0, concat_axis=0, tiled=True)]
    all_gather x5 -> x4, waiting for transfers between devices: 77 us -> 108 us  [spread(): return lax.all_gather(x, 'expert', axis=0, tiled=True)]
  transfers between devices with their start and end apart: 39 -> 46, of which waited for: 16 -> 20; matrix products, arithmetic and copies ran while one was open for 24% -> 22% of each run, Pallas kernels for 4% -> 2%
where the time goes in v4:
time: 1420 us; the launch traced here: 1400 us
  waiting for transfers between devices  845 us (60%)
  matrix products  207 us (15%)
  local copies, waits for them, and re-layouts  114 us (8%)
  starting transfers between devices  76.4 us (5%)
  Pallas kernels  73.2 us (5%)
  other arithmetic  73 us (5%)
  between operations  16.2 us (1%)
    ppermute x12, waiting for transfers between devices, shift(): lax.ppermute(x, 'dp', [((i + step) % parts, i) for i in range(parts)])  472 us
    all_gather x4, waiting for transfers between devices, spread(): return lax.all_gather(x, 'expert', axis=0, tiled=True)  108 us
    ppermute x7, waiting for transfers between devices, send(): lax.ppermute(x, 'dp', [(i, (i + step) % parts) for i in range(parts)])  86.5 us
    ppermute x8, waiting for transfers between devices, spread_pairs(): other = lax.ppermute(whole, 'expert', partners)  84 us
    dot_general x14, matrix products, dot_nt(): lax.dot_general(left, right, (((1,), (1,)), ((), ())), preferred_element_...  76 us
    dot_general x10, matrix products, dot_tn(): lax.dot_general(left, right, (((0,), (0,)), ((), ())), preferred_element_...  63.4 us
    reduce_scatter x1, waiting for transfers between devices, collect(): return lax.psum_scatter(x, 'expert', scatter_dimension=0, tiled=True)  61.9 us
    dot_general x10, matrix products, dot(): return jnp.dot(left, right, preferred_element_type=f32)  60.7 us
  transfers between devices with their start and end apart: 46, of which 20 were waited for; matrix products, arithmetic and copies ran while one was open for 22% of the time, Pallas kernels for 2%

profile of v4, /device:TPU:1, one launch (start us, length us, event | category | flops | bytes accessed | tf_op | source)
XLA Modules:
  0.0 1404.4 jit_solution(18000218135685034717)
XLA Ops:
  16.9 77.0 %all-gather.9.cloned.1.call-done = bf16[2048,2048]{1,0:T(8,128)(2,1)} async-done(((bf16[128,2048]{1,0:T(8,128)(2,1)}), bf16[2048,2048]{1,0:T(8,128)(2,1)}) %all-gather.9.cloned.1.call-update) | async-done | bytes 8388624 | tf_op jit(solution)/shard_map/all_gather | solution.py:442
  94.8 3.5 all-to-all-start
  109.3 13.8 collective-permute-done.2
  135.3 7.2 dynamic_update_slice.63
  142.6 7.6 dynamic_update_slice.64
  155.9 14.9 %collective-permute-done.5 = bf16[512,2048]{1,0:T(8,128)(2,1)} collective-permute-done((bf16[512,2048]{1,0:T(8,128)(2,1)}, bf16[512,2048]{1,0:T(8,128)(2,1)}, u32[]{:S(2)}, u32[]{:S(2)}) %collective-permute-start.5) | collective-permute-done | bytes 2097184 | tf_op jit(solution)/shard_map/ppermute | solution.py:372
  172.0 12.4 fusion.113
  191.0 8.1 shard_map.255
  201.1 5.7 all-to-all-start.1
  207.0 13.9 all-to-all-done.1
  248.4 191.5 %collective-permute-done.9 = bf16[88,2048]{1,0:T(8,128)(2,1)} collective-permute-done((bf16[88,2048]{1,0:T(8,128)(2,1)}, bf16[88,2048]{1,0:T(8,128)(2,1)}, u32[]{:S(2)}, u32[]{:S(2)}) %collective-permute-start.9) | collective-permute-done | bytes 360480 | tf_op jit(solution)/shard_map/ppermute | solution.py:372
  441.6 3.8 constant_dynamic-update-slice_fusion.3
  445.4 4.6 fusion.50
  452.6 8.1 fusion.14
  460.7 7.1 multiply_convert_fusion.7
  472.8 18.7 %fusion.2 = f32[1024,2816]{1,0:T(8,128)} fusion(bf16[1024,2048]{1,0:T(8,128)(2,1)S(1)} %bitcast.288, bf16[1024,2816]{1,0:T(8,128)(2,1)} %collective-permute-done.8, bf16[1024,2816]{1,0:T(8,128)(2,1)} %bitcast.346), kind=kOutput, calls=%fused_computation.6 | convolution fusion | flops 11834228736 | bytes 27262976 | tf_op jit(solution)/shard_map/dot_general | solution.py:76
  491.5 15.4 %multiply_convert_fusion.3 = (bf16[1024,1408]{1,0:T(8,128)(2,1)}, bf16[1024,1408]{1,0:T(8,128)(2,1)}, bf16[1024,1408]{1,0:T(8,128)(2,1)}) fusion(f32[1024,2816]{1,0:T(8,128)} %fusion.2, bf16[1024,2048]{1,0:T(8,128)(2,1)S(1)} %copy-done.6, bf16[1408,2048]{1,0:T(8,128)(2,1)} %constant_dynamic-update-slice_fusion.3), kind=kOutput, calls=%fused_computation.11 | convolution fusion | flops 5928648704 | bytes 30146560 | tf_op jit(solution)/shard_map/dot_general | solution.py:84
  506.9 18.2 %fusion.3.rows_ref = bf16[1024,2048]{1,0:T(8,128)(2,1)} fusion(bf16[1024,2816]{1,0:T(8,128)(2,1)} %collective-permute-done.8, bf16[1024,2816]{1,0:T(8,128)(2,1)} %bitcast.347, bf16[1024,1408]{1,0:T(8,128)(2,1)} %get-tuple-element.163, bf16[1024,1408]{1,0:T(8,128)(2,1)} %get-tuple-element.162), kind=kOutput, calls=%fused_computation.16 | convolution fusion | flops 11847860224 | bytes 21495808 | tf_op jit(solution)/shard_map/dot_general | solution.py:84
  525.2 10.9 shard_map.256
  536.7 5.6 pad_maximum_fusion.3
  543.6 6.1 all-to-all-start.2
  549.7 8.4 convolution_convert_fusion.2
  558.1 11.2 multiply_convert_fusion
  569.4 8.4 convolution_convert_fusion
  577.7 61.9 %reduce-scatter.2.cloned.1.call-done = bf16[128,2048]{1,0:T(8,128)(2,1)} async-done(((bf16[2048,2048]{1,0:T(8,128)(2,1)}), bf16[128,2048]{1,0:T(8,128)(2,1)}) %reduce-scatter.2.cloned.1.call-update) | async-done | bytes 524304 | tf_op jit(solution)/shard_map/reduce_scatter | solution.py:463
  650.9 5.3 all-to-all-start.3
  660.5 18.5 %all-to-all-done.3 = bf16[16,128,128]{2,1,0:T(8,128)(2,1)S(1)} async-done(((bf16[16,128,128]{2,1,0:T(8,128)(2,1)}), bf16[16,128,128]{2,1,0:T(8,128)(2,1)S(1)}, u32[]{:S(2)}, u32[]{:S(2)}) %all-to-all-start.3) | async-done | bytes 524320 | tf_op jit(solution)/shard_map/all_to_all | solution.py:448
  680.0 6.4 all-to-all-start.6
  686.4 10.6 shard_map.257
  697.0 3.8 fusion.32
  703.5 5.3 fusion.34
  710.2 30.6 %all-gather.15.cloned.1.call-done = bf16[2048,2048]{0,1:T(8,128)(2,1)} async-done(((bf16[128,2048]{0,1:T(8,128)(2,1)}), bf16[2048,2048]{0,1:T(8,128)(2,1)}) %all-gather.15.cloned.1.call-update) | async-done | bytes 8388624 | tf_op jit(solution)/shard_map/all_gather | solution.py:442
  740.8 5.8 fusion.119
  754.9 12.2 collective-permute-done.27
  770.0 5.9 fusion.120
  776.0 6.7 fusion.121
  787.3 22.4 %collective-permute-done.29 = bf16[528,1024]{1,0:T(8,128)(2,1)} collective-permute-done((bf16[528,1024]{1,0:T(8,128)(2,1)}, bf16[528,1024]{1,0:T(8,128)(2,1)}, u32[]{:S(2)}, u32[]{:S(2)}) %collective-permute-start.29) | collective-permute-done | bytes 1081376 | tf_op jit(solution)/shard_map/ppermute | solution.py:375
  812.3 4.1 copy.313
  816.4 6.1 all-to-all-start.4
  822.5 3.8 constant_dynamic-slice_fusion.3
  831.0 87.7 %collective-permute-done.11 = bf16[128,4096]{1,0:T(8,128)(2,1)} collective-permute-done((bf16[128,4096]{1,0:T(8,128)(2,1)}, bf16[128,4096]{1,0:T(8,128)(2,1)}, u32[]{:S(2)}, u32[]{:S(2)}) %collective-permute-start.11) | collective-permute-done | bytes 1048608 | tf_op jit(solution)/shard_map/ppermute | solution.py:372
  937.9 13.0 collective-permute-done.13
  953.8 17.9 %collective-permute-done.14 = bf16[2,144,576]{2,1,0:T(8,128)(2,1)} collective-permute-done((bf16[2,144,576]{2,1,0:T(8,128)(2,1)}, bf16[2,144,576]{2,1,0:T(8,128)(2,1)}, u32[]{:S(2)}, u32[]{:S(2)}) %collective-permute-start.14) | collective-permute-done | bytes 331808 | tf_op jit(solution)/shard_map/ppermute | solution.py:455
  978.0 28.5 %collective-permute-done.15 = bf16[4,144,576]{2,1,0:T(8,128)(2,1)} collective-permute-done((bf16[4,144,576]{2,1,0:T(8,128)(2,1)}, bf16[4,144,576]{2,1,0:T(8,128)(2,1)}, u32[]{:S(2)}, u32[]{:S(2)}) %collective-permute-start.15) | collective-permute-done | bytes 663584 | tf_op jit(solution)/shard_map/ppermute | solution.py:455
  1009.4 3.8 collective-permute-start.16
  1013.3 5.1 convolution_dynamic-update-slice_fusion.1
  1019.4 3.9 fusion.116
  1025.2 4.0 fusion.117
  1043.1 4.2 collective-permute-done.17
  1047.6 9.1 collective-permute-done.21
  1057.0 7.3 collective-permute-done.22
  1067.2 8.2 collective-permute-done.23
  1078.0 3.8 constant_dynamic-slice_fusion.2
  1083.2 4.9 all-to-all-start.5
  1089.4 163.7 %collective-permute-done.25 = bf16[704,2048]{1,0:T(8,128)(2,1)} collective-permute-done((bf16[704,2048]{1,0:T(8,128)(2,1)}, bf16[704,2048]{1,0:T(8,128)(2,1)}, u32[]{:S(2)}, u32[]{:S(2)}) %collective-permute-start.25) | collective-permute-done | bytes 2883616 | tf_op jit(solution)/shard_map/ppermute | solution.py:372
  1253.1 5.3 collective-permute-start.26
  1259.7 3.9 fusion.56
  1263.6 3.6 convolution_add_fusion.1
  1267.2 47.7 %collective-permute-done.31 = bf16[704,2048]{1,0:T(8,128)(2,1)} collective-permute-done((bf16[704,2048]{1,0:T(8,128)(2,1)}, bf16[704,2048]{1,0:T(8,128)(2,1)}, u32[]{:S(2)}, u32[]{:S(2)}) %collective-permute-start.31) | collective-permute-done | bytes 2883616 | tf_op jit(solution)/shard_map/ppermute | solution.py:375
  1314.9 6.7 add_bitcast_fusion.1
  1321.7 11.1 add_bitcast_fusion
  1353.8 14.5 %shard_map.258 = (f32[1024,2048]{1,0:T(8,128)}, f32[1024,3072]{1,0:T(8,128)}, f32[256,4096]{1,0:T(8,128)}) custom-call(bf16[16,1024,384]{2,1,0:T(8,128)(2,1)} %bitcast.283), custom_call_target="tpu_custom_call" | custom-call | bytes 37748736 | tf_op jit(solution)/shard_map/pallas_call | solution.py:318
  1368.3 17.4 %shard_map.259 = f32[1024,5632]{1,0:T(8,128)} custom-call(bf16[16,528,1024]{2,1,0:T(8,128)(2,1)} %bitcast.266), custom_call_target="tpu_custom_call" | custom-call | bytes 34603008 | tf_op jit(solution)/shard_map/pallas_call | solution.py:273
  1385.7 11.7 shard_map.260
  (477 shorter events, 209.7 us)
Async XLA Ops:
  7.2 86.8 %copy-start.77 = (f32[2,1,64,6]{2,1,3,0:T(1,128)S(1)}, f32[2,1,64,6]{2,1,3,0:T(1,128)}, u32[]{:S(2)}) copy-start(f32[2,1,64,6]{2,1,3,0:T(1,128)} %param.20) | copy-start | bytes 9220
  7.2 86.9 %copy-start.78 = (s32[2,1,64,6]{2,1,3,0:T(1,128)S(1)}, s32[2,1,64,6]{2,1,3,0:T(1,128)}, u32[]{:S(2)}) copy-start(s32[2,1,64,6]{2,1,3,0:T(1,128)} %param.19) | copy-start | bytes 9220
  7.2 93.9 %copy-start.34 = (bf16[1024,576]{0,1:T(8,128)(2,1)S(1)}, bf16[1024,576]{0,1:T(8,128)(2,1)}, u32[]{:S(2)}) copy-start(bf16[1024,576]{0,1:T(8,128)(2,1)} %param.23) | copy-start | bytes 3538948
  7.2 86.7 %all-gather.9.cloned.1.call-start = ((), (), s32[]{:S(2)}) async-start(), calls=%async_computation.8 | async-start | bytes 8912896 | tf_op jit(solution)/shard_map/all_gather | solution.py:442
  9.7 3.5 collective-permute-start
  13.2 85.1 %copy-start.79 = (f32[128]{0:T(128)}, f32[128]{0:T(128)S(1)}, u32[]{:S(2)}) copy-start(f32[128]{0:T(128)S(1)} %rsqrt.38) | copy-start | bytes 1540
  13.4 80.6 %copy-start.66 = (bf16[2,2304]{1,0:T(2,128)(2,1)}, bf16[2,2304]{1,0:T(2,128)(2,1)S(1)}, u32[]{:S(2)}) copy-start(bf16[2,2304]{1,0:T(2,128)(2,1)S(1)} %dynamic_update_slice.61) | copy-start | bytes 27652
  16.9 428.5 %all-gather.13.cloned.1.call-start = ((), (), s32[]{:S(2)}) async-start(), calls=%async_computation.10 | async-start | bytes 8912896 | tf_op jit(solution)/shard_map/all_gather | solution.py:442
  94.8 35.7 %all-to-all-start = ((f32[16,1,128]{2,1,0:T(1,128)}), f32[16,1,128]{2,1,0:T(1,128)S(1)}, u32[]{:S(2)}, u32[]{:S(2)}) async-start(f32[16,1,128]{2,1,0:T(1,128)} %bitcast.2), calls=%async_computation | async-start | bytes 16384 | tf_op jit(solution)/shard_map/all_to_all | solution.py:448
  99.9 34.6 %collective-permute-start.1 = (bf16[1024,192]{0,1:T(8,128)(2,1)S(1)}, bf16[1024,192]{0,1:T(8,128)(2,1)S(1)}, u32[]{:S(2)}, u32[]{:S(2)}) collective-permute-start(bf16[1024,192]{0,1:T(8,128)(2,1)S(1)} %copy.344), channel_id=1, source_target_pairs={{16,0},{0,16},{17,1},{1,17},{18,2},{2,18},{19,3},{3,19},{20,4},{4,... | collective-permute-start | bytes 1179656 | tf_op jit(solution)/shard_map/ppermute | solution.py:372
  101.2 21.9 %collective-permute-start.2 = (bf16[512,576]{0,1:T(8,128)(2,1)S(1)}, bf16[512,576]{0,1:T(8,128)(2,1)}, u32[]{:S(2)}, u32[]{:S(2)}) collective-permute-start(bf16[512,576]{0,1:T(8,128)(2,1)S(1)} %constant_dynamic-slice_fusion.15), channel_id=1, source_target_pairs={{16,0},{0,16},{17,1},{1,17},{18,2},{2,18},{19,3},{3,19},{20,4},{4,... | collective-permute-start | bytes 1769480 | tf_op jit(solution)/shard_map/ppermute | solution.py:372
  102.5 31.1 %collective-permute-start.4 = (bf16[256,256]{1,0:T(8,128)(2,1)S(1)}, bf16[256,256]{1,0:T(8,128)(2,1)}, u32[]{:S(2)}, u32[]{:S(2)}) collective-permute-start(bf16[256,256]{1,0:T(8,128)(2,1)S(1)} %get-tuple-element.161), channel_id=1, source_target_pairs={{16,0},{0,16},{17,1},{1,17},{18,2},{2,18},{19,3},{3,19},{20,4},{4,... | collective-permute-start | bytes 393224 | tf_op jit(solution)/shard_map/ppermute | solution.py:372
  106.9 64.0 %collective-permute-start.5 = (bf16[512,2048]{1,0:T(8,128)(2,1)}, bf16[512,2048]{1,0:T(8,128)(2,1)}, u32[]{:S(2)}, u32[]{:S(2)}) collective-permute-start(bf16[512,2048]{1,0:T(8,128)(2,1)} %constant_dynamic-slice_fusion.13), channel_id=1, source_target_pairs={{16,0},{0,16},{17,1},{1,17},{18,2},{2,18},{19,3},{3,19},{20,4},{4,... | collective-permute-start | bytes 6291464 | tf_op jit(solution)/shard_map/ppermute | solution.py:372
  123.1 19.5 %collective-permute-start.3 = (bf16[512,576]{0,1:T(8,128)(2,1)}, bf16[512,576]{0,1:T(8,128)(2,1)}, u32[]{:S(2)}, u32[]{:S(2)}) collective-permute-start(bf16[512,576]{0,1:T(8,128)(2,1)} %collective-permute-done.2), channel_id=1, source_target_pairs={{0,1},{1,0},{2,3},{3,2},{4,5},{5,4},{6,7},{7,6},{8,9},{9,8},{10,11... | collective-permute-start | bytes 1769480 | tf_op jit(solution)/shard_map/ppermute | solution.py:422
  130.4 58.8 %copy-start.67 = (f32[1,2,2,128]{3,1,2,0:T(2,128)}, f32[1,2,2,128]{3,1,2,0:T(2,128)S(1)}, u32[]{:S(2)}) copy-start(f32[1,2,2,128]{3,1,2,0:T(2,128)S(1)} %copy.354) | copy-start | bytes 6148
  170.9 55.2 %collective-permute-start.6 = (bf16[512,2048]{1,0:T(8,128)(2,1)}, bf16[512,2048]{1,0:T(8,128)(2,1)S(1)}, u32[]{:S(2)}, u32[]{:S(2)}) collective-permute-start(bf16[512,2048]{1,0:T(8,128)(2,1)} %collective-permute-done.5), channel_id=1, source_target_pairs={{0,1},{1,0},{2,3},{3,2},{4,5},{5,4},{6,7},{7,6},{8,9},{9,8},{10,11... | collective-permute-start | bytes 6291464 | tf_op jit(solution)/shard_map/ppermute | solution.py:422
  201.1 19.7 %all-to-all-start.1 = ((bf16[16,128,128]{1,2,0:T(8,128)(2,1)}), bf16[16,128,128]{1,2,0:T(8,128)(2,1)S(1)}, u32[]{:S(2)}, u32[]{:S(2)}) async-start(bf16[16,128,128]{1,2,0:T(8,128)(2,1)} %copy.295), calls=%async_computation.1 | async-start | bytes 1048576 | tf_op jit(solution)/shard_map/all_to_all | solution.py:448
  206.9 245.7 %all-gather.11.cloned.1.call-start = ((), (), s32[]{:S(2)}) async-start(), calls=%async_computation.9 | async-start | bytes 8912896 | tf_op jit(solution)/shard_map/all_gather | solution.py:442
  229.0 410.6 %reduce-scatter.2.cloned.1.call-start = ((), (), s32[]{:S(2)}) async-start(), calls=%async_computation.11 | async-start | bytes 8912896 | tf_op jit(solution)/shard_map/reduce_scatter | solution.py:463
  229.1 212.6 %collective-permute-start.7 = (bf16[704,2048]{1,0:T(8,128)(2,1)}, bf16[704,2048]{1,0:T(8,128)(2,1)}, u32[]{:S(2)}, u32[]{:S(2)}) collective-permute-start(bf16[704,2048]{1,0:T(8,128)(2,1)} %bitcast.307), channel_id=1, source_target_pairs={{16,0},{0,16},{17,1},{1,17},{18,2},{2,18},{19,3},{3,19},{20,4},{4,... | collective-permute-start | bytes 8650760 | tf_op jit(solution)/shard_map/ppermute | solution.py:372
  230.4 240.5 %collective-permute-start.8 = (bf16[1024,2816]{1,0:T(8,128)(2,1)}, bf16[1024,2816]{1,0:T(8,128)(2,1)}, u32[]{:S(2)}, u32[]{:S(2)}) collective-permute-start(bf16[1024,2816]{1,0:T(8,128)(2,1)} %bitcast.345), channel_id=1, source_target_pairs={{16,0},{0,16},{17,1},{1,17},{18,2},{2,18},{19,3},{3,19},{20,4},{4,... | collective-permute-start | bytes 17301512 | tf_op jit(solution)/shard_map/ppermute | solution.py:372
  233.2 219.4 %collective-permute-start.10 = (bf16[352,1024]{1,0:T(8,128)(2,1)S(1)}, bf16[352,1024]{1,0:T(8,128)(2,1)S(1)}, u32[]{:S(2)}, u32[]{:S(2)}) collective-permute-start(bf16[352,1024]{1,0:T(8,128)(2,1)S(1)} %pad_maximum_fusion.14.refs_0_), channel_id=1, source_target_pairs={{16,0},{0,16},{17,1},{1,17},{18,2},{2,18},{19,3},{3,19},{20,4},{4,... | collective-permute-start | bytes 2162696 | tf_op jit(solution)/shard_map/ppermute | solution.py:372
  237.4 202.5 %collective-permute-start.9 = (bf16[88,2048]{1,0:T(8,128)(2,1)}, bf16[88,2048]{1,0:T(8,128)(2,1)}, u32[]{:S(2)}, u32[]{:S(2)}) collective-permute-start(bf16[88,2048]{1,0:T(8,128)(2,1)} %get-tuple-element.159), channel_id=1, source_target_pairs={{16,0},{0,16},{17,1},{1,17},{18,2},{2,18},{19,3},{3,19},{20,4},{4,... | collective-permute-start | bytes 1081352 | tf_op jit(solution)/shard_map/ppermute | solution.py:372
  246.6 198.8 %copy-start.52 = (s32[32,64]{1,0:T(8,128)S(1)}, s32[32,64]{1,0:T(8,128)}, u32[]{:S(2)}) copy-start(s32[32,64]{1,0:T(8,128)} %copy-done.51) | copy-start | bytes 24580
  246.7 198.8 %copy-start.63 = (pred[32,64]{1,0:T(8,128)(4,1)S(1)}, pred[32,64]{1,0:T(8,128)(4,1)}, u32[]{:S(2)}) copy-start(pred[32,64]{1,0:T(8,128)(4,1)} %copy-done.62) | copy-start | bytes 6148
  467.8 74.5 %copy-start.19 = (bf16[2048,176]{1,0:T(8,128)(2,1)}, bf16[2048,176]{1,0:T(8,128)(2,1)S(1)}, u32[]{:S(2)}) copy-start(bf16[2048,176]{1,0:T(8,128)(2,1)S(1)} %get-tuple-element.57) | copy-start | bytes 2162692
  536.1 204.7 %all-gather.15.cloned.1.call-start = ((), (), s32[]{:S(2)}) async-start(), calls=%async_computation.12 | async-start | bytes 8912896 | tf_op jit(solution)/shard_map/all_gather | solution.py:442
  543.6 34.1 %all-to-all-start.2 = ((bf16[16,128,176]{1,2,0:T(8,128)(2,1)}), bf16[16,128,176]{1,2,0:T(8,128)(2,1)S(1)}, u32[]{:S(2)}, u32[]{:S(2)}) async-start(bf16[16,128,176]{1,2,0:T(8,128)(2,1)} %copy.310), calls=%async_computation.3 | async-start | bytes 1441792 | tf_op jit(solution)/shard_map/all_to_all | solution.py:448
  569.3 70.3 %copy-start.1 = (f32[128,2048]{1,0:T(8,128)S(1)}, f32[128,2048]{1,0:T(8,128)}, u32[]{:S(2)}) copy-start(f32[128,2048]{1,0:T(8,128)} %copy-done) | copy-start | bytes 3145732
  569.3 70.3 %copy-start.55 = (f32[1,8,2,128]{3,1,2,0:T(8,128)S(1)}, f32[1,8,2,128]{3,1,2,0:T(8,128)}, u32[]{:S(2)}) copy-start(f32[1,8,2,128]{3,1,2,0:T(8,128)} %copy-done.54) | copy-start | bytes 24580
  569.3 70.3 %copy-start.75 = (f32[128]{0:T(128)S(1)}, f32[128]{0:T(128)}, u32[]{:S(2)}) copy-start(f32[128]{0:T(128)} %copy-done.74) | copy-start | bytes 1540
  569.3 72.4 %copy-start.21 = (bf16[2,1,64,2048]{3,2,1,0:T(8,128)(2,1)S(1)}, bf16[2,1,64,2048]{3,2,1,0:T(8,128)(2,1)}, u32[]{:S(2)}) copy-start(bf16[2,1,64,2048]{3,2,1,0:T(8,128)(2,1)} %param.17) | copy-start | bytes 1572868
  577.7 64.4 %copy-start.33 = (bf16[16,128,176]{1,2,0:T(8,128)(2,1)}, bf16[16,128,176]{1,2,0:T(8,128)(2,1)S(1)}, u32[]{:S(2)}) copy-start(bf16[16,128,176]{1,2,0:T(8,128)(2,1)S(1)} %all-to-all-done.2) | copy-start | bytes 2162692
  650.9 28.1 %all-to-all-start.3 = ((bf16[16,128,128]{2,1,0:T(8,128)(2,1)}), bf16[16,128,128]{2,1,0:T(8,128)(2,1)S(1)}, u32[]{:S(2)}, u32[]{:S(2)}) async-start(bf16[16,128,128]{2,1,0:T(8,128)(2,1)} %bitcast_bitcast_fusion.1), calls=%async_computation.4 | async-start | bytes 1048576 | tf_op jit(solution)/shard_map/all_to_all | solution.py:448
  680.0 30.3 %all-to-all-start.6 = ((bf16[16,128,128]{2,1,0:T(8,128)(2,1)}), bf16[16,128,128]{2,1,0:T(8,128)(2,1)}, u32[]{:S(2)}, u32[]{:S(2)}) async-start(bf16[16,128,128]{2,1,0:T(8,128)(2,1)} %bitcast_bitcast_fusion), calls=%async_computation.7 | async-start | bytes 1048576 | tf_op jit(solution)/shard_map/all_to_all | solution.py:448
  686.4 667.5 %all-gather.17.cloned.1.call-start = ((), (), s32[]{:S(2)}) async-start(), calls=%async_computation.13 | async-start | bytes 13369344 | tf_op jit(solution)/shard_map/all_gather | solution.py:445
  747.9 19.2 %collective-permute-start.27 = (bf16[1024,384]{1,0:T(8,128)(2,1)}, bf16[1024,384]{1,0:T(8,128)(2,1)}, u32[]{:S(2)}, u32[]{:S(2)}) collective-permute-start(bf16[1024,384]{1,0:T(8,128)(2,1)} %pad_maximum_fusion.12), channel_id=1, source_target_pairs={{0,16},{16,0},{1,17},{17,1},{2,18},{18,2},{3,19},{19,3},{4,20},{20... | collective-permute-start | bytes 2359304 | tf_op jit(solution)/shard_map/ppermute | solution.py:375
  769.9 598.4 %all-gather.19.cloned.1.call-start = ((), (), s32[]{:S(2)}) async-start(), calls=%async_computation.14 | async-start | bytes 18382848 | tf_op jit(solution)/shard_map/all_gather | solution.py:445
  784.9 24.8 %collective-permute-start.29 = (bf16[528,1024]{1,0:T(8,128)(2,1)}, bf16[528,1024]{1,0:T(8,128)(2,1)}, u32[]{:S(2)}, u32[]{:S(2)}) collective-permute-start(bf16[528,1024]{1,0:T(8,128)(2,1)} %pad_maximum_fusion.10), channel_id=1, source_target_pairs={{0,16},{16,0},{1,17},{17,1},{2,18},{18,2},{3,19},{19,3},{4,20},{20... | collective-permute-start | bytes 3244040 | tf_op jit(solution)/shard_map/ppermute | solution.py:375
  816.4 106.4 %all-to-all-start.4 = ((bf16[16,128,512]{1,2,0:T(8,128)(2,1)}), bf16[16,128,512]{1,2,0:T(8,128)(2,1)S(1)}, u32[]{:S(2)}, u32[]{:S(2)}) async-start(bf16[16,128,512]{1,2,0:T(8,128)(2,1)} %copy.313), calls=%async_computation.5 | async-start | bytes 4194304 | tf_op jit(solution)/shard_map/all_to_all | solution.py:448
  826.3 94.8 %collective-permute-start.18 = (bf16[512,3072]{1,0:T(8,128)(2,1)}, bf16[512,3072]{1,0:T(8,128)(2,1)}, u32[]{:S(2)}, u32[]{:S(2)}) collective-permute-start(bf16[512,3072]{1,0:T(8,128)(2,1)} %constant_dynamic-slice_fusion.3), channel_id=1, source_target_pairs={{16,0},{0,16},{17,1},{1,17},{18,2},{2,18},{19,3},{3,19},{20,4},{4,... | collective-permute-start | bytes 9437192 | tf_op jit(solution)/shard_map/ppermute | solution.py:372
  829.4 89.4 %collective-permute-start.11 = (bf16[128,4096]{1,0:T(8,128)(2,1)}, bf16[128,4096]{1,0:T(8,128)(2,1)}, u32[]{:S(2)}, u32[]{:S(2)}) collective-permute-start(bf16[128,4096]{1,0:T(8,128)(2,1)} %constant_dynamic-slice_fusion.4), channel_id=1, source_target_pairs={{16,0},{0,16},{17,1},{1,17},{18,2},{2,18},{19,3},{3,19},{20,4},{4,... | collective-permute-start | bytes 3145736 | tf_op jit(solution)/shard_map/ppermute | solution.py:372
  918.7 8.5 collective-permute-start.12
  921.2 104.1 %collective-permute-start.19 = (bf16[512,3072]{1,0:T(8,128)(2,1)}, bf16[512,3072]{1,0:T(8,128)(2,1)}, u32[]{:S(2)}, u32[]{:S(2)}) collective-permute-start(bf16[512,3072]{1,0:T(8,128)(2,1)} %collective-permute-done.18), channel_id=1, source_target_pairs={{0,1},{1,0},{2,3},{3,2},{4,5},{5,4},{6,7},{7,6},{8,9},{9,8},{10,11... | collective-permute-start | bytes 9437192 | tf_op jit(solution)/shard_map/ppermute | solution.py:422
  935.4 15.5 %collective-permute-start.13 = (bf16[1,144,576]{2,1,0:T(8,128)(2,1)S(1)}, bf16[1,144,576]{2,1,0:T(8,128)(2,1)}, u32[]{:S(2)}, u32[]{:S(2)}) collective-permute-start(bf16[1,144,576]{2,1,0:T(8,128)(2,1)S(1)} %maximum_bitcast_fusion.4), channel_id=1, source_target_pairs={{0,8},{1,9},{2,10},{3,11},{4,12},{5,13},{6,14},{7,15},{8,0},{9,1},... | collective-permute-start | bytes 497672 | tf_op jit(solution)/shard_map/ppermute | solution.py:455
  953.4 18.4 %collective-permute-start.14 = (bf16[2,144,576]{2,1,0:T(8,128)(2,1)}, bf16[2,144,576]{2,1,0:T(8,128)(2,1)}, u32[]{:S(2)}, u32[]{:S(2)}) collective-permute-start(bf16[2,144,576]{2,1,0:T(8,128)(2,1)} %maximum_bitcast_fusion.2), channel_id=1, source_target_pairs={{0,4},{1,5},{2,6},{3,7},{4,0},{5,1},{6,2},{7,3},{8,12},{9,13},{10,... | collective-permute-start | bytes 995336 | tf_op jit(solution)/shard_map/ppermute | solution.py:455
  973.9 32.5 %collective-permute-start.15 = (bf16[4,144,576]{2,1,0:T(8,128)(2,1)}, bf16[4,144,576]{2,1,0:T(8,128)(2,1)}, u32[]{:S(2)}, u32[]{:S(2)}) collective-permute-start(bf16[4,144,576]{2,1,0:T(8,128)(2,1)} %bitcast.45), channel_id=1, source_target_pairs={{0,2},{1,3},{2,0},{3,1},{4,6},{5,7},{6,4},{7,5},{8,10},{9,11},{10,... | collective-permute-start | bytes 1990664 | tf_op jit(solution)/shard_map/ppermute | solution.py:455
  1009.4 26.5 %collective-permute-start.16 = (bf16[8,144,576]{2,1,0:T(8,128)(2,1)}, bf16[8,144,576]{2,1,0:T(8,128)(2,1)}, u32[]{:S(2)}, u32[]{:S(2)}) collective-permute-start(bf16[8,144,576]{2,1,0:T(8,128)(2,1)} %bitcast.48), channel_id=1, source_target_pairs={{0,1},{1,0},{2,3},{3,2},{4,5},{5,4},{6,7},{7,6},{8,9},{9,8},{10,11... | collective-permute-start | bytes 3981320 | tf_op jit(solution)/shard_map/ppermute | solution.py:455
  1035.0 7.9 collective-permute-start.20
  1042.2 5.1 collective-permute-start.17
  1047.5 9.2 collective-permute-start.21
  1056.9 7.4 collective-permute-start.22
  1064.8 10.6 collective-permute-start.23
  1067.2 254.5 %collective-permute-start.30 = (bf16[1024,2816]{1,0:T(8,128)(2,1)}, bf16[1024,2816]{1,0:T(8,128)(2,1)}, u32[]{:S(2)}, u32[]{:S(2)}) collective-permute-start(bf16[1024,2816]{1,0:T(8,128)(2,1)} %convolution_convert_fusion), channel_id=1, source_target_pairs={{0,16},{16,0},{1,17},{17,1},{2,18},{18,2},{3,19},{19,3},{4,20},{20... | collective-permute-start | bytes 17301512 | tf_op jit(solution)/shard_map/ppermute | solution.py:375
  1075.7 6.8 collective-permute-start.24
  1081.8 171.4 %collective-permute-start.25 = (bf16[704,2048]{1,0:T(8,128)(2,1)}, bf16[704,2048]{1,0:T(8,128)(2,1)}, u32[]{:S(2)}, u32[]{:S(2)}) collective-permute-start(bf16[704,2048]{1,0:T(8,128)(2,1)} %constant_dynamic-slice_fusion.2), channel_id=1, source_target_pairs={{16,0},{0,16},{17,1},{1,17},{18,2},{2,18},{19,3},{3,19},{20,4},{4,... | collective-permute-start | bytes 8650760 | tf_op jit(solution)/shard_map/ppermute | solution.py:372
  1083.2 263.5 %all-to-all-start.5 = ((bf16[16,64,2048]{2,1,0:T(8,128)(2,1)}), bf16[16,64,2048]{2,1,0:T(8,128)(2,1)}, u32[]{:S(2)}, u32[]{:S(2)}) async-start(bf16[16,64,2048]{2,1,0:T(8,128)(2,1)} %bitcast.302), calls=%async_computation.6 | async-start | bytes 8388608 | tf_op jit(solution)/shard_map/all_to_all | solution.py:448
  1088.1 226.8 %collective-permute-start.31 = (bf16[704,2048]{1,0:T(8,128)(2,1)}, bf16[704,2048]{1,0:T(8,128)(2,1)}, u32[]{:S(2)}, u32[]{:S(2)}) collective-permute-start(bf16[704,2048]{1,0:T(8,128)(2,1)} %convolution_convert_fusion.2), channel_id=1, source_target_pairs={{0,16},{16,0},{1,17},{17,1},{2,18},{18,2},{3,19},{19,3},{4,20},{20... | collective-permute-start | bytes 8650760 | tf_op jit(solution)/shard_map/ppermute | solution.py:375
  1253.1 97.0 %collective-permute-start.26 = (bf16[704,2048]{1,0:T(8,128)(2,1)}, bf16[704,2048]{1,0:T(8,128)(2,1)}, u32[]{:S(2)}, u32[]{:S(2)}) collective-permute-start(bf16[704,2048]{1,0:T(8,128)(2,1)} %collective-permute-done.25), channel_id=1, source_target_pairs={{0,1},{1,0},{2,3},{3,2},{4,5},{5,4},{6,7},{7,6},{8,9},{9,8},{10,11... | collective-permute-start | bytes 8650760 | tf_op jit(solution)/shard_map/ppermute | solution.py:422
  1259.6 55.3 %copy-start.7 = (bf16[1024,2048]{1,0:T(8,128)(2,1)S(1)}, bf16[1024,2048]{1,0:T(8,128)(2,1)}, u32[]{:S(2)}) copy-start(bf16[1024,2048]{1,0:T(8,128)(2,1)} %fusion) | copy-start | bytes 12582916
  1259.7 55.3 %copy-start.44 = (bf16[1024,1408]{1,0:T(8,128)(2,1)S(1)}, bf16[1024,1408]{1,0:T(8,128)(2,1)}, u32[]{:S(2)}) copy-start(bf16[1024,1408]{1,0:T(8,128)(2,1)} %get-tuple-element.39) | copy-start | bytes 8650756
  1263.6 58.1 %slice-start.4 = ((s8[5767168]{0:T(1024)(128)(4,1)}), s8[4194304]{0:T(1024)(128)(4,1)S(1)}, s32[]{:S(2)}) async-start(s8[5767168]{0:T(1024)(128)(4,1)} %bitcast.273), calls=%async_computation.19 | async-start | bytes 8388608
  1267.2 54.5 %copy-start.16 = (bf16[32,32,2048]{2,1,0:T(8,128)(2,1)S(1)}, bf16[32,32,2048]{2,1,0:T(8,128)(2,1)}, u32[]{:S(2)}) copy-start(bf16[32,32,2048]{2,1,0:T(8,128)(2,1)} %copy-done.14) | copy-start | bytes 12582916
  1334.0 3.4 collective-permute-start.28
  (75 other events, 681.7 us)
Sparse Core Ops, SparseCore 0:
  17.0 76.8 all-gather.8
  96.1 72.8 all-gather.12
  229.2 73.8 all-gather.10
  536.2 103.3 reduce-scatter.1
  641.6 99.1 all-gather.14
  770.0 141.2 all-gather.16
  912.9 111.9 all-gather.18
